TPU v7x, 1024 devices: a whole 4x4x32 slice. The times are simulated.
1024 devices in a mesh: sec: 2 (over core), grp: 16 (over x, y), blk: 32 (over z).
Axes of the slice: x: 4, y: 4, z: 32, core: 2. Of those that a mesh axis runs over, the one named last changes fastest.
Arguments:
- atm_flux: bfloat16 [2, 60, 2097152], P(None, None, ('sec', 'grp', 'blk')), may hold values from -25 to 25
- tile_bank: bfloat16 [128, 128, 128], replicated, may hold values from -1 to 1
- pair_count: int32 [1024], P(('sec', 'grp', 'blk')), may hold values from 32 to 128, as said below
- pair_source: int32 [131072], P(('sec', 'grp', 'blk')), may hold values from 0 to 15
- pair_tile: int32 [131072], P(('sec', 'grp', 'blk')), may hold values from 0 to 127
- pair_target: int32 [131072], P(('sec', 'grp', 'blk')), may hold values from 0 to 63
- tracers: bfloat16 [32, 60, 262144], P(None, None, ('sec', 'grp', 'blk')), may hold values from -6 to 6
- diffusivity: float32 [31, 262144], P(None, ('sec', 'grp', 'blk')), may hold values from 0.2 to 5
- column_depth: int32 [262144], P(('sec', 'grp', 'blk')), may hold values from 0 to 32
Outputs:
- mixed_tracers: float32 [32, 60, 262144], P(None, None, ('sec', 'grp', 'blk'))
Inputs may be any that keep to these rules, and one draw needn't show every extreme that they name: `pair_count`: pairs at positions 127 and below that are at or past a device's count are unused; some device has exactly 128 live pairs. `pair_target`: a target t names ocean block t % 2 of the device at blk index t // 2 with the same sec and grp. Levels at index column_depth and below are dry; 0 marks a land column.
All inputs are finite; a program needn't handle non-finite values.
Results may differ from a plain program's by a relative error of at most 0.013.
Values may be sent and summed in bfloat16 or wider, within the bound.
No kernel may reach another device: no remote copies, remote signals or barrier semaphores. Data moves between devices by JAX's collectives and lax.ppermute only.
A program may use at most 64 MiB of HBM per device.

v0:
```python
import jax
import jax.numpy as jnp
from jax import lax
from jax.sharding import PartitionSpec as P

pair_group = 16


def column_factors(diffusivity, column_depth):
    layer_count = diffusivity.shape[0] + 1
    layer_ids = jnp.arange(layer_count, dtype=jnp.int32)
    active = layer_ids[:, None] < column_depth[None, :]
    interior = diffusivity * active[1:].astype(diffusivity.dtype)
    boundary = jnp.zeros_like(diffusivity[:1])
    coupling = jnp.concatenate([boundary, interior, boundary], axis=0)
    diagonal = 1.0 + coupling[:-1] + coupling[1:]
    inverse_pivot = []
    upper_ratio = []
    for k in range(layer_count):
        if k == 0:
            pivot_entry = diagonal[0]
        else:
            pivot_entry = diagonal[k] + coupling[k] * upper_ratio[k - 1]
        inverse = 1.0 / pivot_entry
        inverse_pivot.append(inverse)
        upper_ratio.append(-coupling[k + 1] * inverse)
    live_mask = active.astype(diffusivity.dtype)[:, None, :]
    surface = (column_depth > 0).astype(diffusivity.dtype)
    return (coupling, inverse_pivot, upper_ratio, live_mask, surface)


def mix_once(column_state, surface_term, factors):
    coupling, inverse_pivot, upper_ratio, live_mask, surface = factors
    right_side = column_state.at[0].add(surface_term * surface[None, :]) * live_mask
    forward = []
    for k in range(right_side.shape[0]):
        if k == 0:
            carried = right_side[0]
        else:
            carried = right_side[k] + coupling[k][None, :] * forward[k - 1]
        forward.append(carried * inverse_pivot[k][None, :])
    solved = [forward[-1]]
    for k in range(right_side.shape[0] - 2, -1, -1):
        solved.append(forward[k] - upper_ratio[k][None, :] * solved[-1])
    return jnp.stack(solved[::-1])


def merge_sources(arrived):
    return jnp.sum(arrived.astype(jnp.float32), axis=0)


def body(
    atm_flux,
    tile_bank,
    pair_count,
    pair_source,
    pair_tile,
    pair_target,
    tracers,
    diffusivity,
    column_depth,
):
    sub_count, field_count, atm_rows = atm_flux.shape
    tile_width = tile_bank.shape[1]
    source_blocks = atm_rows // tile_width
    columns = tracers.shape[2]
    ocean_blocks = columns // tile_width
    peer_count = lax.axis_size("blk")
    devices_all = lax.axis_size("sec") * lax.axis_size("grp") * peer_count
    stacked = sub_count * field_count
    flux_blocks = atm_flux.reshape(stacked, source_blocks, tile_width)
    live_count = pair_count[0]

    def add_group(group_index, slot_sums):
        first_pair = group_index * pair_group
        sources = lax.dynamic_slice_in_dim(pair_source, first_pair, pair_group)
        tile_ids = lax.dynamic_slice_in_dim(pair_tile, first_pair, pair_group)
        targets = lax.dynamic_slice_in_dim(pair_target, first_pair, pair_group)
        picked = jnp.take(flux_blocks, sources, axis=1)
        chosen = jnp.take(tile_bank, tile_ids, axis=0)
        products = jnp.einsum("sgr,grc->gsc", picked, chosen, preferred_element_type=jnp.float32)
        live_pairs = (first_pair + jnp.arange(pair_group, dtype=jnp.int32) < live_count).astype(
            jnp.float32
        )
        products = products * live_pairs[:, None, None]
        return slot_sums.at[targets // ocean_blocks, :, targets % ocean_blocks].add(products)

    zero_sums = jnp.zeros((peer_count, stacked, ocean_blocks, tile_width), jnp.float32)
    rounds = pair_source.shape[0] // pair_group
    outgoing = lax.fori_loop(0, rounds, add_group, zero_sums).astype(jnp.bfloat16)
    outgoing = outgoing.reshape(peer_count, sub_count, field_count, columns)
    atm_part = jnp.sum(atm_flux.astype(jnp.float32), axis=2)
    forcing = merge_sources(
        lax.all_to_all(outgoing, "blk", split_axis=0, concat_axis=0, tiled=True)
    )
    ocean_late = jnp.sum(forcing, axis=2)
    atm_total, ocean_total = lax.psum((atm_part, ocean_late), ("sec", "grp", "blk"))
    correction = (atm_total * (ocean_blocks / source_blocks) - ocean_total) / (
        columns * devices_all
    )
    factors = column_factors(diffusivity, column_depth)
    column_state = tracers.astype(jnp.float32)
    for substep in range(sub_count):
        column_state = mix_once(
            column_state, forcing[substep] + correction[substep][:, None], factors
        )
    return column_state


def solution(mesh):
    placed = (
        P(None, None, ("sec", "grp", "blk")),
        P(),
        P(("sec", "grp", "blk")),
        P(("sec", "grp", "blk")),
        P(("sec", "grp", "blk")),
        P(("sec", "grp", "blk")),
        P(None, None, ("sec", "grp", "blk")),
        P(None, ("sec", "grp", "blk")),
        P(("sec", "grp", "blk")),
    )
    return jax.shard_map(
        body,
        mesh=mesh,
        in_specs=placed,
        out_specs=P(None, None, ("sec", "grp", "blk")),
        check_vma=False,
    )
```

profile of v0, /device:TPU:1, one launch (start us, length us, event | category | flops | bytes accessed | tf_op | source)
XLA Modules:
  0.0 461.3 jit_solution(13323544844673783989)
XLA Ops:
  0.0 1.2 copy.39
  1.6 2.1 broadcast_in_dim.91
  3.8 66.7 %while.17 = (s32[]{:T(128)}, f32[32,120,2,128]{3,1,2,0:T(8,128)}, s32[128]{0:T(128)S(1)}, s32[128]{0:T(128)S(1)}, bf16[120,16,128]{2,0,1:T(8,128)(2,1)S(1)}, /*i...) while((s32[]{:T(128)}, f32[32,120,2,128]{3,1,2,0:T(8,128)}, ...), condition=%wide.region_2.3_spmd, body=%wide.region_0.2_spmd.sunk | while | flops 63916820 | bytes 6988919 | solution.py:90
  3.8 0.7 compare_and_fusion.4
  4.5 2.8 gather_fusion
  7.4 0.6 gather_fusion.1
  8.1 0.5 convolution_multiply_fusion.2
  8.7 3.4 scatter_fusion
  12.1 0.7 compare_and_fusion.4
  12.8 2.8 gather_fusion
  15.8 0.6 gather_fusion.1
  17.0 3.5 scatter_fusion
  20.5 0.7 compare_and_fusion.4
  21.2 2.8 gather_fusion
  24.1 0.6 gather_fusion.1
  24.8 0.5 convolution_multiply_fusion.2
  25.4 3.4 scatter_fusion
  28.8 0.7 compare_and_fusion.4
  29.5 2.8 gather_fusion
  32.5 0.6 gather_fusion.1
  33.1 0.5 convolution_multiply_fusion.2
  33.7 3.4 scatter_fusion
  37.1 0.7 compare_and_fusion.4
  37.8 2.8 gather_fusion
  40.7 0.6 gather_fusion.1
  42.0 3.4 scatter_fusion
  45.4 0.7 compare_and_fusion.4
  46.1 2.8 gather_fusion
  49.0 0.6 gather_fusion.1
  50.3 3.4 scatter_fusion
  53.7 0.7 compare_and_fusion.4
  54.4 2.8 gather_fusion
  57.4 0.6 gather_fusion.1
  58.6 3.5 scatter_fusion
  62.1 0.7 compare_and_fusion.4
  62.8 2.8 gather_fusion
  65.7 0.6 gather_fusion.1
  67.0 3.5 scatter_fusion
  70.4 2.4 convert_element_type.38
  72.8 2.2 copy.41
  75.0 2.5 reshape.30268
  77.6 4.8 %copy.42 = bf16[32,2,60,256]{3,1,2,0:T(2,128)(2,1)} copy(bf16[32,2,60,256]{3,0,2,1:T(8,128)(2,1)} %reshape.30268) | data formatting | bytes 3932160 | tf_op jit(solution)/shard_map/reshape | solution.py:91
  82.4 29.3 %all-to-all-start = ((bf16[32,2,60,256]{3,1,2,0:T(2,128)(2,1)}), bf16[32,2,60,256]{3,1,2,0:T(2,128)(2,1)}, u32[]{:S(2)}, u32[]{:S(2)}) async-start(bf16[32,2,60,256]{3,1,2,0:T(2,128)(2,1)} %copy.42), calls=%async_computation | async-start | bytes 3932160 | tf_op jit(solution)/shard_map/all_to_all | solution.py:94
  112.8 0.6 copy_convert_fusion
  113.3 180.2 %all-to-all-done = bf16[32,2,60,256]{3,1,2,0:T(2,128)(2,1)} async-done(((bf16[32,2,60,256]{3,1,2,0:T(2,128)(2,1)}), bf16[32,2,60,256]{3,1,2,0:T(2,128)(2,1)}, u32[]{:S(2)}, u32[]{:S(2)}) %all-to-all-start) | async-done | bytes 1966112 | tf_op jit(solution)/shard_map/all_to_all | solution.py:94
  293.6 2.4 convert_reduce_fusion
  296.1 159.9 %all-reduce.2 = (f32[2,60]{0,1:T(8,128)S(1)}, f32[2,60]{0,1:T(8,128)S(1)}) all-reduce(f32[2,60]{0,1:T(8,128)S(1)} %copy.45, f32[2,60]{0,1:T(8,128)S(1)} %convert_reduce_fusion.2), channel_id=1, replica_groups=mesh['sec'=2,'grp'=16,'blk'=32] {'sec','grp','blk'}, use_global_device_ids=true, to_apply=%region_7.8 | all-reduce | flops 240 | bytes 1920 | tf_op jit(solution)/shard_map/psum | solution.py:97
  458.9 2.4 copy.46
  (147 shorter events, 7.7 us)
Async XLA Ops:
  1.6 2.2 copy-start.3
  1.6 2.1 copy-start.4
  1.6 2.1 copy-start.6
  82.4 29.4 %copy-start.5 = (s32[256]{0:T(256)S(1)}, s32[256]{0:T(256)}, u32[]{:S(2)}) copy-start(s32[256]{0:T(256)} %param.23) | copy-start | bytes 3076
  82.4 29.4 %copy-start.2 = (f32[31,256]{1,0:T(8,128)S(1)}, f32[31,256]{1,0:T(8,128)}, u32[]{:S(2)}) copy-start(f32[31,256]{1,0:T(8,128)} %param.22) | copy-start | bytes 95236
  82.4 29.4 %copy-start = (bf16[2,60,2048]{2,0,1:T(2,128)(2,1)S(1)}, bf16[2,60,2048]{2,0,1:T(2,128)(2,1)}, u32[]{:S(2)}) copy-start(bf16[2,60,2048]{2,0,1:T(2,128)(2,1)} %param.15) | copy-start | bytes 1474564
  82.4 30.4 %copy-start.1 = (bf16[32,60,256]{2,0,1:T(8,128)(2,1)S(1)}, bf16[32,60,256]{2,0,1:T(8,128)(2,1)}, u32[]{:S(2)}) copy-start(bf16[32,60,256]{2,0,1:T(8,128)(2,1)} %param.21) | copy-start | bytes 2949124
  82.4 211.2 %all-to-all-start = ((bf16[32,2,60,256]{3,1,2,0:T(2,128)(2,1)}), bf16[32,2,60,256]{3,1,2,0:T(2,128)(2,1)}, u32[]{:S(2)}, u32[]{:S(2)}) async-start(bf16[32,2,60,256]{3,1,2,0:T(2,128)(2,1)} %copy.42), calls=%async_computation | async-start | bytes 3932160 | tf_op jit(solution)/shard_map/all_to_all | solution.py:94
where the time goes:
time: 463 us; the launch traced here: 461 us
  waiting for transfers between devices  180 us (39%)
  blocking collectives  160 us (35%)
  local copies, waits for them, and re-layouts  44.1 us (10%)
  other arithmetic  42.9 us (9%)
  starting transfers between devices  29.3 us (6%)
    all_to_all x1, waiting for transfers between devices, body(): lax.all_to_all(outgoing, 'blk', split_axis=0, concat_axis=0, tiled=True)  180 us
    psum x1, blocking collectives, body(): lax.psum((atm_part, ocean_late), ('sec', 'grp', 'blk'))  160 us
    all_to_all x1, starting transfers between devices, body(): lax.all_to_all(outgoing, 'blk', split_axis=0, concat_axis=0, tiled=True)  29.3 us
    scatter-add x8, other arithmetic, add_group(): slot_sums.at[targets // ocean_blocks, :, targets % ocean_blocks]  27.4 us
    gather x8, local copies, waits for them, and re-layouts, add_group(): chosen = jnp.take(tile_bank, tile_ids, axis=0)  22.7 us
  transfers between devices with their start and end apart: 1, of which 1 were waited for; matrix products, arithmetic and copies ran while one was open for 0% of the time, Pallas kernels for 0%

commit v1 on v0

v1 whole, which is shorter than its diff:
```python
import jax
import jax.numpy as jnp
from jax import lax
from jax.experimental import pallas as pl
from jax.experimental.pallas import tpu as pltpu
from jax.sharding import PartitionSpec as P

F32 = jnp.float32
BF16 = jnp.bfloat16
HALF = 64
ROWS = 128
TILE = 128
UNROLL = 4


def remap_kernel(count_ref, me_ref, source_ref, tile_ref, target_ref, flux_ref, bank_ref,
                 out_ref, part_ref, blocks, acc):
    subs, fields, atm_rows = flux_ref.shape
    source_blocks = atm_rows // TILE
    slots = out_ref.shape[1]
    blocks[...] = jnp.zeros(blocks.shape, BF16)
    atm = jnp.zeros((ROWS, TILE), F32)
    for s in range(source_blocks):
        for sub in range(subs):
            blocks[s, pl.ds(sub * HALF, fields)] = flux_ref[sub, :, pl.ds(s * TILE, TILE)]
        atm = atm + blocks[s].astype(F32)
    acc[...] = jnp.zeros(acc.shape, F32)
    count = count_ref[0]
    me = me_ref[0]

    def slot_of(p):
        target = target_ref[p]
        half = target & 1
        owner = target >> 1
        r = jnp.where(half == 0, owner - me, me - owner) & (slots - 1)
        r1 = r & 1
        r2 = (r >> 1) & 3
        r3 = ((r >> 3) + jnp.where(r2 == 3, 1, 0)) & 3
        place = half * slots + r1 * 16 + r2 * 4 + r3
        return jnp.where(p < count, place, 2 * slots)

    def group(g, carry):
        terms = []
        for j in range(UNROLL):
            p = g * UNROLL + j
            terms.append(jnp.dot(blocks[source_ref[p]], bank_ref[tile_ref[p]],
                                 preferred_element_type=F32))
        for j in range(UNROLL):
            place = slot_of(g * UNROLL + j)
            acc[place] = acc[place] + terms[j]
        return carry

    lax.fori_loop(0, (count + UNROLL - 1) // UNROLL, group, 0)

    def flush(i, ocean):
        for half in range(2):
            sent = acc[half * slots + i].astype(BF16)
            out_ref[half, i] = sent
            ocean = ocean + sent.astype(F32)
        return ocean

    ocean = lax.fori_loop(0, slots, flush, jnp.zeros((ROWS, TILE), F32), unroll=4)
    share = 2.0 * TILE / atm_rows
    part = atm * share - ocean
    part_ref[...] = lax.dot_general(jnp.ones((8, TILE), F32), part, (((1,), (1,)), ((), ())),
                                    precision=lax.Precision.HIGHEST, preferred_element_type=F32)


def remap(pair_count, me, pair_source, pair_tile, pair_target, flux, bank, slots):
    smem = pl.BlockSpec(memory_space=pltpu.SMEM)
    vmem = pl.BlockSpec(memory_space=pltpu.VMEM)
    source_blocks = flux.shape[2] // TILE
    return pl.pallas_call(
        remap_kernel,
        out_shape=(jax.ShapeDtypeStruct((2, slots, ROWS, TILE), BF16),
                   jax.ShapeDtypeStruct((8, ROWS), F32)),
        in_specs=[smem] * 5 + [vmem, vmem],
        out_specs=(vmem, vmem),
        scratch_shapes=[pltpu.VMEM((source_blocks, ROWS, TILE), BF16),
                        pltpu.VMEM((2 * slots + 1, ROWS, TILE), F32)],
        compiler_params=pltpu.CompilerParams(vmem_limit_bytes=40 << 20),
        cost_estimate=pl.CostEstimate(flops=2 * 128 * 128 ** 3, transcendentals=0,
                                      bytes_accessed=8 << 20),
        name="remap",
    )(pair_count, me, pair_source, pair_tile, pair_target, flux, bank)


def mix_kernel(tracer_ref, diff_ref, depth_ref, state_ref, unit_ref, ahead, lower, upper):
    levels, fields, columns = tracer_ref.shape
    depth = depth_ref[...]
    zero = jnp.zeros((1, columns), F32)
    one = jnp.ones((1, columns), F32)

    def coupling(k):
        if k == 0 or k == levels:
            return zero
        return jnp.where(depth > k, diff_ref[pl.ds(k - 1, 1), :], zero)

    ratio = None
    for k in range(levels):
        a, b = coupling(k), coupling(k + 1)
        pivot = 1.0 + a + b
        if k > 0:
            pivot = pivot - a * ratio
        inverse = 1.0 / pivot
        ratio = b * inverse
        wet = jnp.where(depth > k, one, zero)
        ahead[pl.ds(k, 1), :] = wet * inverse
        lower[pl.ds(k, 1), :] = a * inverse
        upper[pl.ds(k, 1), :] = ratio
    unit = [jnp.where(depth > 0, one, zero)] + [zero] * (levels - 1)
    for sweep in range(2):
        carried = None
        unit_carried = None
        for k in range(levels):
            if sweep == 0:
                x = tracer_ref[k].astype(F32)
            else:
                x = state_ref[k]
            scale = ahead[pl.ds(k, 1), :]
            below = lower[pl.ds(k, 1), :]
            if k == 0:
                carried = x * scale
                unit_carried = unit[k] * scale
            else:
                carried = x * scale + carried * below
                unit_carried = unit[k] * scale + unit_carried * below
            state_ref[k] = carried
            unit[k] = unit_carried
        for k in range(levels - 2, -1, -1):
            above = upper[pl.ds(k, 1), :]
            carried = state_ref[k] + carried * above
            state_ref[k] = carried
            unit[k] = unit[k] + unit[k + 1] * above
        for k in range(levels):
            unit_ref[sweep, pl.ds(k, 1), :] = unit[k]


def mix(tracers, diffusivity, column_depth):
    levels, fields, columns = tracers.shape
    vmem = pl.BlockSpec(memory_space=pltpu.VMEM)
    return pl.pallas_call(
        mix_kernel,
        out_shape=(jax.ShapeDtypeStruct((levels, fields, columns), F32),
                   jax.ShapeDtypeStruct((2, levels, columns), F32)),
        in_specs=[vmem] * 3,
        out_specs=(vmem, vmem),
        scratch_shapes=[pltpu.VMEM((levels, columns), F32)] * 3,
        compiler_params=pltpu.CompilerParams(vmem_limit_bytes=24 << 20),
        cost_estimate=pl.CostEstimate(flops=12 * levels * fields * columns, transcendentals=0,
                                      bytes_accessed=6 * levels * fields * columns),
        name="mix",
    )(tracers, diffusivity, column_depth.reshape(1, columns))


def finish_kernel(state_ref, unit_ref, own_ref, near_ref, back_ref, far_ref, total_ref, out_ref):
    levels, fields, columns = state_ref.shape
    eye = (lax.broadcasted_iota(jnp.int32, (ROWS, ROWS), 0)
           == lax.broadcasted_iota(jnp.int32, (ROWS, ROWS), 1))
    spread = jnp.where(eye, jnp.broadcast_to(total_ref[...], (ROWS, ROWS)), 0.0)
    fix = jnp.sum(spread, axis=1, keepdims=True)
    for o in range(2):
        lanes = pl.ds(o * TILE, TILE)
        surface = (own_ref[o] + near_ref[o].astype(F32) + back_ref[o].astype(F32)
                   + far_ref[o].astype(F32)) + fix
        first = surface[0:fields]
        second = surface[HALF:HALF + fields]
        for k in range(levels):
            out_ref[k, :, lanes] = (state_ref[k, :, lanes]
                                    + first * unit_ref[1, pl.ds(k, 1), lanes]
                                    + second * unit_ref[0, pl.ds(k, 1), lanes])


def finish(state, unit, own, near, back, far, total):
    vmem = pl.BlockSpec(memory_space=pltpu.VMEM)
    return pl.pallas_call(
        finish_kernel,
        out_shape=jax.ShapeDtypeStruct(state.shape, F32),
        in_specs=[vmem] * 7,
        out_specs=vmem,
        input_output_aliases={0: 0},
        compiler_params=pltpu.CompilerParams(vmem_limit_bytes=24 << 20),
        name="finish",
    )(state, unit, own, near, back, far, total)


def shift(x, by, ring):
    return lax.ppermute(x, "blk", [(i, (i + by) % ring) for i in range(ring)])


def pieces(total):
    high = lax.reduce_precision(total, 8, 7)
    middle = lax.reduce_precision(total - high, 8, 7)
    low = total - high - middle
    return jnp.stack([high, middle, low])


def with_total(chunks, total):
    row = lax.broadcasted_iota(jnp.int32, chunks.shape, chunks.ndim - 2)
    parts = pieces(total)
    for i in range(3):
        chunks = jnp.where(row == HALF - 4 + i, parts[i], chunks)
    return chunks


def total_in(chunk):
    rows = chunk[HALF - 4:HALF - 1].astype(F32)
    return rows[0] + rows[1] + rows[2]


def exchange(sums, total, step, ring):
    sent = [with_total(sums[0], total).astype(BF16), sums[1].astype(BF16)]
    near = shift(jnp.stack([sent[0][1], sent[1][3]]), step, ring)
    back = shift(jnp.stack([sent[0][3], sent[1][1]]), -step, ring)
    if 4 * step == ring:
        far = shift(jnp.stack([sent[0][2], sent[1][2]]), 2 * step, ring)
    else:
        far = jnp.stack([shift(sent[0][2], 2 * step, ring), shift(sent[1][2], -2 * step, ring)])
    return near, back, far


def body(
    atm_flux,
    tile_bank,
    pair_count,
    pair_source,
    pair_tile,
    pair_target,
    tracers,
    diffusivity,
    column_depth,
):
    ring = lax.axis_size("blk")
    plane = lax.axis_size("sec") * lax.axis_size("grp")
    columns = tracers.shape[2]
    me = lax.axis_index("blk").astype(jnp.int32).reshape(1)
    chunks, part = remap(pair_count, me, pair_source, pair_tile, pair_target, atm_flux, tile_bank,
                         ring)
    gathered = lax.all_to_all(jnp.broadcast_to(part[:1], (plane, ROWS)), ("sec", "grp"), 0, 0,
                              tiled=True)
    total = jnp.sum(gathered, axis=0)
    total = total + shift(total, 1, ring)
    chunks = chunks.reshape(2, 2, 4, 4, ROWS, TILE)
    arrived = [shift(chunks[0, 1], 1, ring), shift(chunks[1, 1], -1, ring)]
    state, unit = mix(tracers, diffusivity, column_depth)
    sums = [chunks[o, 0].astype(F32) + arrived[o].astype(F32) for o in range(2)]
    near, back, far = exchange(sums, total, 2, ring)
    total = total + total_in(near[0, 0]) + total_in(back[0, 0]) + total_in(far[0, 0])
    sums = [sums[o][0] + near[o].astype(F32) + back[o].astype(F32) + far[o].astype(F32)
            for o in range(2)]
    near, back, far = exchange(sums, total, 8, ring)
    total = total + total_in(near[0]) + total_in(back[0]) + total_in(far[0])
    own = jnp.stack([sums[0][0], sums[1][0]])
    fix = total / (columns * ring * plane)
    return finish(state, unit, own, near, back, far, fix.reshape(1, ROWS))


def solution(mesh):
    placed = (
        P(None, None, ("sec", "grp", "blk")),
        P(),
        P(("sec", "grp", "blk")),
        P(("sec", "grp", "blk")),
        P(("sec", "grp", "blk")),
        P(("sec", "grp", "blk")),
        P(None, None, ("sec", "grp", "blk")),
        P(None, ("sec", "grp", "blk")),
        P(("sec", "grp", "blk")),
    )
    return jax.shard_map(
        body,
        mesh=mesh,
        in_specs=placed,
        out_specs=P(None, None, ("sec", "grp", "blk")),
        check_vma=False,
    )
```

time: 463 us -> 136 us (0.29)
  the two profiles are of different devices: /device:TPU:1 before, /device:TPU:2 now
where the time goes in v1:
time: 136 us
  starting transfers between devices  84.3 us (62%)
  waiting for transfers between devices  30.7 us (23%)
  local copies, waits for them, and re-layouts  11.3 us (8%)
  Pallas kernels  4.94 us (4%)
  other arithmetic  3.4 us (2%)
    ppermute x10, starting transfers between devices, shift(): return lax.ppermute(x, 'blk', [(i, (i + by) % ring) for i in range(ring)])  67 us
    ppermute x10, waiting for transfers between devices, shift(): return lax.ppermute(x, 'blk', [(i, (i + by) % ring) for i in range(ring)])  30.7 us
    all_to_all x1, starting transfers between devices, body(): lax.all_to_all(jnp.broadcast_to(part[:1], (plane, ROWS)), ('sec', 'grp'),...  17.3 us
    unnamed x14, local copies, waits for them, and re-layouts  7.08 us
    pallas_call x1, Pallas kernels, remap(): pl.pallas_call(remap_kernel, out_shape=(jax.ShapeDtypeStruct((2, slots, R...  3.24 us
  transfers between devices with their start and end apart: 11, of which 6 were waited for; matrix products, arithmetic and copies ran while one was open for 3% of the time, Pallas kernels for 1%

profile of v1, /device:TPU:2, one launch (start us, length us, event | category | flops | bytes accessed | tf_op | source)
XLA Modules:
  0.0 135.6 jit_solution(3614369097767221210)
XLA Ops:
  0.0 1.2 copy.18.flux_ref
  1.8 0.0 copy-start
  1.8 2.2 %copy-done = bf16[128,128,128]{2,1,0:T(8,128)(2,1)S(1)} copy-done((bf16[128,128,128]{2,1,0:T(8,128)(2,1)S(1)}, bf16[128,128,128]{2,1,0:T(8,128)(2,1)}, u32[]{:S(2)}) %copy-start) | copy-done | bytes 4194328
  4.0 0.0 copy-start.3
  4.0 0.7 copy-done.3
  4.7 0.0 copy-start.4
  4.7 0.7 copy-done.4
  5.3 0.0 copy-start.5
  5.3 0.7 copy-done.5
  6.0 3.2 %remap.1 = (bf16[2,32,128,128]{3,2,1,0:T(8,128)(2,1)S(1)}, f32[8,128]{1,0:T(8,128)S(1)}) custom-call(s32[1]{0:T(128)S(6)} %copy.22.count_ref, s32[1]{0:T(128)} %bitcast.1.me_ref, s32[128]{0:T(128)S(1)} %copy-done.3, s32[128]{0:T(128)S(1)} %copy-done.4, s32[128]{0:T(128)S(1)} %copy-done.5, bf16[2,60,2048]{2,1,0:T(8,128)(2,1)S(1)} %copy.18.flux_ref, ...), custom_call_target="tpu_custom_call" | custom-call | flops 536870912 | bytes 8388608 | tf_op jit(solution)/shard_map/remap/pallas_call | solution.py:73
  9.2 0.6 broadcast_in_dim.25
  9.9 0.0 copy-start.1
  9.9 0.0 copy-start.2
  9.9 17.3 %all-to-all-start = ((f32[32,1,128]{2,1,0:T(1,128)}), f32[32,1,128]{2,1,0:T(1,128)S(1)}, u32[]{:S(2)}, u32[]{:S(2)}) async-start(f32[32,1,128]{2,1,0:T(1,128)} %broadcast_in_dim.25), calls=%async_computation | async-start | bytes 32768 | tf_op jit(solution)/shard_map/all_to_all | solution.py:239
  27.2 1.1 slice_bitcast_fusion.2
  28.3 1.9 %collective-permute-start = (bf16[4,4,128,128]{3,2,1,0:T(8,128)(2,1)}, bf16[4,4,128,128]{3,2,1,0:T(8,128)(2,1)}, u32[]{:S(2)}, u32[]{:S(2)}) collective-permute-start(bf16[4,4,128,128]{3,2,1,0:T(8,128)(2,1)} %get-tuple-element.24), channel_id=1, source_target_pairs={{0,1},{1,2},{2,3},{3,4},{4,5},{5,6},{6,7},{7,8},{8,9},{9,10},{10,1... | collective-permute-start | bytes 1572872 | tf_op jit(solution)/shard_map/ppermute | solution.py:188
  30.2 10.8 %collective-permute-start.2 = (bf16[4,4,128,128]{3,2,1,0:T(8,128)(2,1)}, bf16[4,4,128,128]{3,2,1,0:T(8,128)(2,1)}, u32[]{:S(2)}, u32[]{:S(2)}) collective-permute-start(bf16[4,4,128,128]{3,2,1,0:T(8,128)(2,1)} %get-tuple-element.25), channel_id=1, source_target_pairs={{0,31},{1,0},{2,1},{3,2},{4,3},{5,4},{6,5},{7,6},{8,7},{9,8},{10,9... | collective-permute-start | bytes 1572872 | tf_op jit(solution)/shard_map/ppermute | solution.py:188
  41.0 1.8 %copy.17.tracer_ref = bf16[32,60,256]{2,1,0:T(8,128)(2,1)S(1)} copy(bf16[32,60,256]{2,0,1:T(8,128)(2,1)} %param.15) | data formatting | bytes 1966080 | tf_op args[6]
  42.7 0.0 all-to-all-done
  42.8 1.9 %collective-permute-start.1 = (f32[128]{0:T(128)S(1)}, f32[128]{0:T(128)S(1)}, u32[]{:S(2)}, u32[]{:S(2)}) collective-permute-start(f32[128]{0:T(128)S(1)} %reduce_sum.9), channel_id=1, source_target_pairs={{0,1},{1,2},{2,3},{3,4},{4,5},{5,6},{6,7},{7,8},{8,9},{9,10},{10,1... | collective-permute-start | bytes 1544 | tf_op jit(solution)/shard_map/ppermute | solution.py:188
  44.7 0.0 copy-done.1
  44.7 0.0 copy-done.2
  44.7 1.1 mix.1
  45.8 5.7 %collective-permute-done.1 = f32[128]{0:T(128)S(1)} collective-permute-done((f32[128]{0:T(128)S(1)}, f32[128]{0:T(128)S(1)}, u32[]{:S(2)}, u32[]{:S(2)}) %collective-permute-start.1) | collective-permute-done | bytes 544 | tf_op jit(solution)/shard_map/ppermute | solution.py:188
  51.6 0.0 collective-permute-done
  51.6 1.4 %select_convert_fusion = bf16[4,4,128,128]{3,2,1,0:T(8,128)(2,1)S(1)} fusion(bf16[128]{0:T(256)(128)(2,1)S(1)} %get-tuple-element.41, bf16[128]{0:T(256)(128)(2,1)S(1)} %get-tuple-element.40, bf16[128]{0:T(256)(128)(2,1)S(1)} %get-tuple-element.19, pred[128]{0:T(512)(128)(4,1)S(1)} %get-tuple-element.42, pred[128]{0:T(512)(128)(4,1)S(1)} %get-tuple-element.43, ...), kind=kLoop, calls=%fused_computation.2 | loop fusion | flops 1572864 | bytes 1574016 | tf_op jit(solution)/shard_map/convert_element_type | solution.py:212
  53.1 0.0 collective-permute-done.2
  53.1 1.6 %convert_add_fusion = (f32[4,4,128,128]{3,2,1,0:T(8,128)S(1)}, bf16[4,4,128,128]{3,2,1,0:T(8,128)(2,1)S(1)}, f32[4,4,128,128]{3,2,1,0:T(8,128)S(1)}) fusion(bf16[4,4,128,128]{3,2,1,0:T(8,128)(2,1)} %collective-permute-done.2, bf16[2,2,4,4,128,128]{5,4,3,2,1,0:T(8,128)(2,1)S(1)} %bitcast.70, bf16[4,4,128,128]{3,2,1,0:T(8,128)(2,1)} %collective-permute-done), kind=kLoop, calls=%fused_computation | loop fusion | flops 1835008 | bytes 4718592 | tf_op jit(solution)/shard_map/add | solution.py:246
  54.7 1.9 %collective-permute-start.5 = (bf16[4,128,128]{2,1,0:T(8,128)(2,1)S(1)}, bf16[4,128,128]{2,1,0:T(8,128)(2,1)S(1)}, u32[]{:S(2)}, u32[]{:S(2)}) collective-permute-start(bf16[4,128,128]{2,1,0:T(8,128)(2,1)S(1)} %get-tuple-element.26), channel_id=1, source_target_pairs={{0,4},{1,5},{2,6},{3,7},{4,8},{5,9},{6,10},{7,11},{8,12},{9,13},{1... | collective-permute-start | bytes 393224 | tf_op jit(solution)/shard_map/ppermute | solution.py:188
  56.7 2.6 %collective-permute-start.3 = (bf16[2,4,128,128]{3,2,1,0:T(8,128)(2,1)S(1)}, bf16[2,4,128,128]{3,2,1,0:T(8,128)(2,1)S(1)}, u32[]{:S(2)}, u32[]{:S(2)}) collective-permute-start(bf16[2,4,128,128]{3,2,1,0:T(8,128)(2,1)S(1)} %pad_maximum_fusion), channel_id=1, source_target_pairs={{0,2},{1,3},{2,4},{3,5},{4,6},{5,7},{6,8},{7,9},{8,10},{9,11},{10,... | collective-permute-start | bytes 786440 | tf_op jit(solution)/shard_map/ppermute | solution.py:188
  59.3 5.4 %collective-permute-start.4 = (bf16[2,4,128,128]{3,2,1,0:T(8,128)(2,1)S(1)}, bf16[2,4,128,128]{3,2,1,0:T(8,128)(2,1)S(1)}, u32[]{:S(2)}, u32[]{:S(2)}) collective-permute-start(bf16[2,4,128,128]{3,2,1,0:T(8,128)(2,1)S(1)} %pad_maximum_fusion.1), channel_id=1, source_target_pairs={{0,30},{1,31},{2,0},{3,1},{4,2},{5,3},{6,4},{7,5},{8,6},{9,7},{10,... | collective-permute-start | bytes 786440 | tf_op jit(solution)/shard_map/ppermute | solution.py:188
  64.7 7.8 %collective-permute-start.6 = (bf16[4,128,128]{2,1,0:T(8,128)(2,1)S(1)}, bf16[4,128,128]{2,1,0:T(8,128)(2,1)S(1)}, u32[]{:S(2)}, u32[]{:S(2)}) collective-permute-start(bf16[4,128,128]{2,1,0:T(8,128)(2,1)S(1)} %get-tuple-element.30), channel_id=1, source_target_pairs={{0,28},{1,29},{2,30},{3,31},{4,0},{5,1},{6,2},{7,3},{8,4},{9,5},{1... | collective-permute-start | bytes 393224 | tf_op jit(solution)/shard_map/ppermute | solution.py:188
  72.5 0.0 collective-permute-done.5
  72.5 4.1 %collective-permute-done.3 = bf16[2,4,128,128]{3,2,1,0:T(8,128)(2,1)S(1)} collective-permute-done((bf16[2,4,128,128]{3,2,1,0:T(8,128)(2,1)S(1)}, bf16[2,4,128,128]{3,2,1,0:T(8,128)(2,1)S(1)}, u32[]{:S(2)}, u32[]{:S(2)}) %collective-permute-start.3) | collective-permute-done | bytes 262176 | tf_op jit(solution)/shard_map/ppermute | solution.py:188
  76.6 1.7 %collective-permute-done.4 = bf16[2,4,128,128]{3,2,1,0:T(8,128)(2,1)S(1)} collective-permute-done((bf16[2,4,128,128]{3,2,1,0:T(8,128)(2,1)S(1)}, bf16[2,4,128,128]{3,2,1,0:T(8,128)(2,1)S(1)}, u32[]{:S(2)}, u32[]{:S(2)}) %collective-permute-start.4) | collective-permute-done | bytes 262176 | tf_op jit(solution)/shard_map/ppermute | solution.py:188
  78.4 0.1 select_convert_fusion.1
  78.5 8.1 %collective-permute-done.6 = bf16[4,128,128]{2,1,0:T(8,128)(2,1)S(1)} collective-permute-done((bf16[4,128,128]{2,1,0:T(8,128)(2,1)S(1)}, bf16[4,128,128]{2,1,0:T(8,128)(2,1)S(1)}, u32[]{:S(2)}, u32[]{:S(2)}) %collective-permute-start.6) | collective-permute-done | bytes 131104 | tf_op jit(solution)/shard_map/ppermute | solution.py:188
  86.6 0.1 fusion.10
  86.7 20.2 %collective-permute-start.9 = (bf16[2,128,128]{2,1,0:T(8,128)(2,1)S(1)}, bf16[2,128,128]{2,1,0:T(8,128)(2,1)S(1)}, u32[]{:S(2)}, u32[]{:S(2)}) collective-permute-start(bf16[2,128,128]{2,1,0:T(8,128)(2,1)S(1)} %pad_maximum_fusion.5), channel_id=1, source_target_pairs={{0,16},{1,17},{2,18},{3,19},{4,20},{5,21},{6,22},{7,23},{8,24},{9,... | collective-permute-start | bytes 196616 | tf_op jit(solution)/shard_map/ppermute | solution.py:188
  106.9 8.3 %collective-permute-start.8 = (bf16[2,128,128]{2,1,0:T(8,128)(2,1)S(1)}, bf16[2,128,128]{2,1,0:T(8,128)(2,1)S(1)}, u32[]{:S(2)}, u32[]{:S(2)}) collective-permute-start(bf16[2,128,128]{2,1,0:T(8,128)(2,1)S(1)} %pad_maximum_fusion.4), channel_id=1, source_target_pairs={{0,24},{1,25},{2,26},{3,27},{4,28},{5,29},{6,30},{7,31},{8,0},{9,1... | collective-permute-start | bytes 196616 | tf_op jit(solution)/shard_map/ppermute | solution.py:188
  115.2 6.2 %collective-permute-start.7 = (bf16[2,128,128]{2,1,0:T(8,128)(2,1)S(1)}, bf16[2,128,128]{2,1,0:T(8,128)(2,1)S(1)}, u32[]{:S(2)}, u32[]{:S(2)}) collective-permute-start(bf16[2,128,128]{2,1,0:T(8,128)(2,1)S(1)} %pad_maximum_fusion.3), channel_id=1, source_target_pairs={{0,8},{1,9},{2,10},{3,11},{4,12},{5,13},{6,14},{7,15},{8,16},{9,17... | collective-permute-start | bytes 196616 | tf_op jit(solution)/shard_map/ppermute | solution.py:188
  121.5 0.0 collective-permute-done.9.far_ref
  121.5 2.2 %collective-permute-done.8.back_ref = bf16[2,128,128]{2,1,0:T(8,128)(2,1)S(1)} collective-permute-done((bf16[2,128,128]{2,1,0:T(8,128)(2,1)S(1)}, bf16[2,128,128]{2,1,0:T(8,128)(2,1)S(1)}, u32[]{:S(2)}, u32[]{:S(2)}) %collective-permute-start.8) | collective-permute-done | bytes 65568 | tf_op jit(solution)/shard_map/ppermute | solution.py:188
  123.8 8.8 %collective-permute-done.7.near_ref = bf16[2,128,128]{2,1,0:T(8,128)(2,1)S(1)} collective-permute-done((bf16[2,128,128]{2,1,0:T(8,128)(2,1)S(1)}, bf16[2,128,128]{2,1,0:T(8,128)(2,1)S(1)}, u32[]{:S(2)}, u32[]{:S(2)}) %collective-permute-start.7) | collective-permute-done | bytes 65568 | tf_op jit(solution)/shard_map/ppermute | solution.py:188
  132.6 0.6 finish.1
  133.2 2.4 %copy.20 = f32[32,60,256]{2,0,1:T(8,128)} copy(f32[32,60,256]{2,1,0:T(8,128)S(1)} %finish.1) | data formatting | bytes 3932160 | tf_op jit(solution)/shard_map/finish/pallas_call | solution.py:176
  (27 shorter events, 0.3 us)
Async XLA Ops:
  1.8 2.2 %copy-start = (bf16[128,128,128]{2,1,0:T(8,128)(2,1)S(1)}, bf16[128,128,128]{2,1,0:T(8,128)(2,1)}, u32[]{:S(2)}) copy-start(bf16[128,128,128]{2,1,0:T(8,128)(2,1)} %bank_ref.1) | copy-start | bytes 12582916
  4.0 0.7 copy-start.3
  4.7 0.7 copy-start.4
  5.3 0.7 copy-start.5
  9.9 34.8 %copy-start.1 = (f32[31,256]{1,0:T(8,128)S(1)}, f32[31,256]{1,0:T(8,128)}, u32[]{:S(2)}) copy-start(f32[31,256]{1,0:T(8,128)} %diff_ref.1) | copy-start | bytes 95236
  9.9 34.8 %copy-start.2 = (s32[256]{0:T(256)S(1)}, s32[256]{0:T(256)}, u32[]{:S(2)}) copy-start(s32[256]{0:T(256)} %param.17) | copy-start | bytes 3076
  9.9 32.9 %all-to-all-start = ((f32[32,1,128]{2,1,0:T(1,128)}), f32[32,1,128]{2,1,0:T(1,128)S(1)}, u32[]{:S(2)}, u32[]{:S(2)}) async-start(f32[32,1,128]{2,1,0:T(1,128)} %broadcast_in_dim.25), calls=%async_computation | async-start | bytes 32768 | tf_op jit(solution)/shard_map/all_to_all | solution.py:239
  28.3 23.3 %collective-permute-start = (bf16[4,4,128,128]{3,2,1,0:T(8,128)(2,1)}, bf16[4,4,128,128]{3,2,1,0:T(8,128)(2,1)}, u32[]{:S(2)}, u32[]{:S(2)}) collective-permute-start(bf16[4,4,128,128]{3,2,1,0:T(8,128)(2,1)} %get-tuple-element.24), channel_id=1, source_target_pairs={{0,1},{1,2},{2,3},{3,4},{4,5},{5,6},{6,7},{7,8},{8,9},{9,10},{10,1... | collective-permute-start | bytes 1572872 | tf_op jit(solution)/shard_map/ppermute | solution.py:188
  30.2 22.9 %collective-permute-start.2 = (bf16[4,4,128,128]{3,2,1,0:T(8,128)(2,1)}, bf16[4,4,128,128]{3,2,1,0:T(8,128)(2,1)}, u32[]{:S(2)}, u32[]{:S(2)}) collective-permute-start(bf16[4,4,128,128]{3,2,1,0:T(8,128)(2,1)} %get-tuple-element.25), channel_id=1, source_target_pairs={{0,31},{1,0},{2,1},{3,2},{4,3},{5,4},{6,5},{7,6},{8,7},{9,8},{10,9... | collective-permute-start | bytes 1572872 | tf_op jit(solution)/shard_map/ppermute | solution.py:188
  42.8 8.8 %collective-permute-start.1 = (f32[128]{0:T(128)S(1)}, f32[128]{0:T(128)S(1)}, u32[]{:S(2)}, u32[]{:S(2)}) collective-permute-start(f32[128]{0:T(128)S(1)} %reduce_sum.9), channel_id=1, source_target_pairs={{0,1},{1,2},{2,3},{3,4},{4,5},{5,6},{6,7},{7,8},{8,9},{9,10},{10,1... | collective-permute-start | bytes 1544 | tf_op jit(solution)/shard_map/ppermute | solution.py:188
  54.7 17.8 %collective-permute-start.5 = (bf16[4,128,128]{2,1,0:T(8,128)(2,1)S(1)}, bf16[4,128,128]{2,1,0:T(8,128)(2,1)S(1)}, u32[]{:S(2)}, u32[]{:S(2)}) collective-permute-start(bf16[4,128,128]{2,1,0:T(8,128)(2,1)S(1)} %get-tuple-element.26), channel_id=1, source_target_pairs={{0,4},{1,5},{2,6},{3,7},{4,8},{5,9},{6,10},{7,11},{8,12},{9,13},{1... | collective-permute-start | bytes 393224 | tf_op jit(solution)/shard_map/ppermute | solution.py:188
  56.7 19.9 %collective-permute-start.3 = (bf16[2,4,128,128]{3,2,1,0:T(8,128)(2,1)S(1)}, bf16[2,4,128,128]{3,2,1,0:T(8,128)(2,1)S(1)}, u32[]{:S(2)}, u32[]{:S(2)}) collective-permute-start(bf16[2,4,128,128]{3,2,1,0:T(8,128)(2,1)S(1)} %pad_maximum_fusion), channel_id=1, source_target_pairs={{0,2},{1,3},{2,4},{3,5},{4,6},{5,7},{6,8},{7,9},{8,10},{9,11},{10,... | collective-permute-start | bytes 786440 | tf_op jit(solution)/shard_map/ppermute | solution.py:188
  59.3 19.0 %collective-permute-start.4 = (bf16[2,4,128,128]{3,2,1,0:T(8,128)(2,1)S(1)}, bf16[2,4,128,128]{3,2,1,0:T(8,128)(2,1)S(1)}, u32[]{:S(2)}, u32[]{:S(2)}) collective-permute-start(bf16[2,4,128,128]{3,2,1,0:T(8,128)(2,1)S(1)} %pad_maximum_fusion.1), channel_id=1, source_target_pairs={{0,30},{1,31},{2,0},{3,1},{4,2},{5,3},{6,4},{7,5},{8,6},{9,7},{10,... | collective-permute-start | bytes 786440 | tf_op jit(solution)/shard_map/ppermute | solution.py:188
  64.7 21.9 %collective-permute-start.6 = (bf16[4,128,128]{2,1,0:T(8,128)(2,1)S(1)}, bf16[4,128,128]{2,1,0:T(8,128)(2,1)S(1)}, u32[]{:S(2)}, u32[]{:S(2)}) collective-permute-start(bf16[4,128,128]{2,1,0:T(8,128)(2,1)S(1)} %get-tuple-element.30), channel_id=1, source_target_pairs={{0,28},{1,29},{2,30},{3,31},{4,0},{5,1},{6,2},{7,3},{8,4},{9,5},{1... | collective-permute-start | bytes 393224 | tf_op jit(solution)/shard_map/ppermute | solution.py:188
  86.7 34.8 %collective-permute-start.9 = (bf16[2,128,128]{2,1,0:T(8,128)(2,1)S(1)}, bf16[2,128,128]{2,1,0:T(8,128)(2,1)S(1)}, u32[]{:S(2)}, u32[]{:S(2)}) collective-permute-start(bf16[2,128,128]{2,1,0:T(8,128)(2,1)S(1)} %pad_maximum_fusion.5), channel_id=1, source_target_pairs={{0,16},{1,17},{2,18},{3,19},{4,20},{5,21},{6,22},{7,23},{8,24},{9,... | collective-permute-start | bytes 196616 | tf_op jit(solution)/shard_map/ppermute | solution.py:188
  106.9 16.9 %collective-permute-start.8 = (bf16[2,128,128]{2,1,0:T(8,128)(2,1)S(1)}, bf16[2,128,128]{2,1,0:T(8,128)(2,1)S(1)}, u32[]{:S(2)}, u32[]{:S(2)}) collective-permute-start(bf16[2,128,128]{2,1,0:T(8,128)(2,1)S(1)} %pad_maximum_fusion.4), channel_id=1, source_target_pairs={{0,24},{1,25},{2,26},{3,27},{4,28},{5,29},{6,30},{7,31},{8,0},{9,1... | collective-permute-start | bytes 196616 | tf_op jit(solution)/shard_map/ppermute | solution.py:188
  115.2 17.4 %collective-permute-start.7 = (bf16[2,128,128]{2,1,0:T(8,128)(2,1)S(1)}, bf16[2,128,128]{2,1,0:T(8,128)(2,1)S(1)}, u32[]{:S(2)}, u32[]{:S(2)}) collective-permute-start(bf16[2,128,128]{2,1,0:T(8,128)(2,1)S(1)} %pad_maximum_fusion.3), channel_id=1, source_target_pairs={{0,8},{1,9},{2,10},{3,11},{4,12},{5,13},{6,14},{7,15},{8,16},{9,17... | collective-permute-start | bytes 196616 | tf_op jit(solution)/shard_map/ppermute | solution.py:188

commit v2 on v1

v2 whole, which is shorter than its diff:
```python
import functools

import jax
import jax.numpy as jnp
from jax import lax
from jax.experimental import pallas as pl
from jax.experimental.pallas import tpu as pltpu
from jax.sharding import PartitionSpec as P

F32 = jnp.float32
BF16 = jnp.bfloat16
HALF = 64
ROWS = 128
TILE = 128
UNROLL = 4
BANK_COPIES = 8
FIELD_CHUNK = 15


def remap_kernel(count_ref, me_ref, source_hbm, tile_hbm, target_hbm, flux_ref, bank_hbm,
                 right_ref, left_ref, keep_ref, part_ref,
                 source_ref, tile_ref, target_ref, bank_ref, blocks, acc, list_sem, bank_sem):
    subs, fields, atm_rows = flux_ref.shape
    source_blocks = atm_rows // TILE
    sent_slots = right_ref.shape[0]
    slots = 2 * sent_slots
    lists = [pltpu.make_async_copy(src, dst, list_sem.at[i]) for i, (src, dst) in enumerate(
        ((source_hbm, source_ref), (tile_hbm, tile_ref), (target_hbm, target_ref)))]
    span = bank_ref.shape[0] // BANK_COPIES
    loads = [pltpu.make_async_copy(bank_hbm.at[pl.ds(i * span, span)],
                                   bank_ref.at[pl.ds(i * span, span)], bank_sem.at[i])
             for i in range(BANK_COPIES)]
    for copy in lists + loads:
        copy.start()
    blocks[...] = jnp.zeros(blocks.shape, BF16)
    atm = jnp.zeros((ROWS, TILE), F32)
    for s in range(source_blocks):
        for sub in range(subs):
            blocks[s, pl.ds(sub * HALF, fields)] = flux_ref[sub, :, pl.ds(s * TILE, TILE)]
        atm = atm + blocks[s].astype(F32)
    acc[...] = jnp.zeros(acc.shape, F32)
    count = count_ref[0]
    me = me_ref[0]
    for copy in lists + loads:
        copy.wait()

    def slot_of(p):
        target = target_ref[p]
        half = target & 1
        owner = target >> 1
        r = jnp.where(half == 0, owner - me, me - owner) & (slots - 1)
        r1 = r & 1
        r2 = (r >> 1) & 3
        r3 = ((r >> 3) + jnp.where(r2 == 3, 1, 0)) & 3
        place = half * slots + r1 * sent_slots + r2 * 4 + r3
        return jnp.where(p < count, place, 2 * slots)

    def group(g, carry):
        terms = []
        for j in range(UNROLL):
            p = g * UNROLL + j
            terms.append(jnp.dot(blocks[source_ref[p]], bank_ref[tile_ref[p]],
                                 preferred_element_type=F32))
        for j in range(UNROLL):
            place = slot_of(g * UNROLL + j)
            acc[place] = acc[place] + terms[j]
        return carry

    lax.fori_loop(0, (count + UNROLL - 1) // UNROLL, group, 0)

    def flush(i, ocean):
        for half in range(2):
            kept = acc[half * slots + i].astype(BF16)
            sent = acc[half * slots + sent_slots + i].astype(BF16)
            keep_ref[half, i] = kept
            if half == 0:
                right_ref[i] = sent
            else:
                left_ref[i] = sent
            ocean = ocean + kept.astype(F32) + sent.astype(F32)
        return ocean

    ocean = lax.fori_loop(0, sent_slots, flush, jnp.zeros((ROWS, TILE), F32), unroll=4)
    share = 2.0 * TILE / atm_rows
    part = atm * share - ocean
    part_ref[...] = lax.dot_general(jnp.ones((8, TILE), F32), part, (((1,), (1,)), ((), ())),
                                    precision=lax.Precision.HIGHEST, preferred_element_type=F32)


def remap(pair_count, me, pair_source, pair_tile, pair_target, flux, bank, slots):
    smem = pl.BlockSpec(memory_space=pltpu.SMEM)
    vmem = pl.BlockSpec(memory_space=pltpu.VMEM)
    hbm = pl.BlockSpec(memory_space=pltpu.HBM)
    source_blocks = flux.shape[2] // TILE
    half = slots // 2
    return pl.pallas_call(
        remap_kernel,
        out_shape=(jax.ShapeDtypeStruct((half, ROWS, TILE), BF16),
                   jax.ShapeDtypeStruct((half, ROWS, TILE), BF16),
                   jax.ShapeDtypeStruct((2, half, ROWS, TILE), BF16),
                   jax.ShapeDtypeStruct((8, ROWS), F32)),
        in_specs=[smem] * 2 + [hbm] * 3 + [vmem, hbm],
        out_specs=(vmem,) * 4,
        scratch_shapes=[pltpu.SMEM(pair_source.shape, jnp.int32)] * 3
        + [pltpu.VMEM(bank.shape, BF16),
           pltpu.VMEM((source_blocks, ROWS, TILE), BF16),
           pltpu.VMEM((2 * slots + 1, ROWS, TILE), F32),
           pltpu.SemaphoreType.DMA((3,)),
           pltpu.SemaphoreType.DMA((BANK_COPIES,))],
        compiler_params=pltpu.CompilerParams(vmem_limit_bytes=40 << 20),
        cost_estimate=pl.CostEstimate(flops=2 * 128 * 128 ** 3, transcendentals=0,
                                      bytes_accessed=8 << 20),
        name="remap",
    )(pair_count, me, *(pltpu.with_memory_space_constraint(x, pltpu.HBM)
                        for x in (pair_source, pair_tile, pair_target)), flux,
      pltpu.with_memory_space_constraint(bank, pltpu.HBM))


def combine_kernel(keep_ref, right_ref, left_ref, own_ref, near_ref, back_ref, far_ref, other_ref):
    for code in range(4):
        for i in range(4):
            place = code * 4 + i
            first = keep_ref[0, place].astype(F32) + right_ref[place].astype(F32)
            second = keep_ref[1, place].astype(F32) + left_ref[place].astype(F32)
            if code == 0:
                own_ref[0, i] = first
                own_ref[1, i] = second
            elif code == 1:
                near_ref[0, i] = first.astype(BF16)
                back_ref[1, i] = second.astype(BF16)
            elif code == 3:
                back_ref[0, i] = first.astype(BF16)
                near_ref[1, i] = second.astype(BF16)
            else:
                far_ref[i] = first.astype(BF16)
                other_ref[i] = second.astype(BF16)


def combine(keep, right, left):
    vmem = pl.BlockSpec(memory_space=pltpu.VMEM)
    pair = jax.ShapeDtypeStruct((2, 4, ROWS, TILE), BF16)
    single = jax.ShapeDtypeStruct((4, ROWS, TILE), BF16)
    return pl.pallas_call(
        combine_kernel,
        out_shape=(jax.ShapeDtypeStruct((2, 4, ROWS, TILE), F32), pair, pair, single, single),
        in_specs=[vmem] * 3,
        out_specs=(vmem,) * 5,
        compiler_params=pltpu.CompilerParams(vmem_limit_bytes=16 << 20),
        name="combine",
    )(keep, right, left)


def with_total(chunk, total):
    row = lax.broadcasted_iota(jnp.int32, chunk.shape, 0)
    for i in range(3):
        piece = total.astype(BF16).astype(F32)
        chunk = jnp.where(row == HALF - 4 + i, piece, chunk)
        total = total - piece
    return chunk.astype(BF16)


def total_in(chunk):
    rows = chunk.astype(F32)
    place = HALF - 4
    return rows[place:place + 1] + rows[place + 1:place + 2] + rows[place + 2:place + 3]


def gather_kernel(own_ref, near_ref, back_ref, far_ref, other_ref, total_ref,
                  outer_ref, mirror_ref, rest_ref):
    for o in range(2):
        for at, code in enumerate((2, 0, 1, 3)):
            last = (far_ref, other_ref)[o]
            value = (own_ref[o, code] + near_ref[o, code].astype(F32)
                     + back_ref[o, code].astype(F32) + last[code].astype(F32))
            if at > 0:
                rest_ref[o, at - 1] = value
            elif o == 0:
                outer_ref[...] = with_total(value, total_ref[...])
            else:
                mirror_ref[...] = value.astype(BF16)


def gather(own, near, back, far, other, total):
    vmem = pl.BlockSpec(memory_space=pltpu.VMEM)
    chunk = jax.ShapeDtypeStruct((ROWS, TILE), BF16)
    return pl.pallas_call(
        gather_kernel,
        out_shape=(chunk, chunk, jax.ShapeDtypeStruct((2, 3, ROWS, TILE), F32)),
        in_specs=[vmem] * 6,
        out_specs=(vmem,) * 3,
        compiler_params=pltpu.CompilerParams(vmem_limit_bytes=16 << 20),
        name="gather",
    )(own, near, back, far, other, total)


def relay_kernel(rest_ref, outer_ref, mirror_ref, total_ref, near_ref, back_ref):
    total = total_ref[...]
    near_ref[0] = with_total(rest_ref[0, 1] + outer_ref[...].astype(F32),
                             total + total_in(outer_ref[...]))
    near_ref[1] = rest_ref[1, 2].astype(BF16)
    back_ref[0] = with_total(rest_ref[0, 2], total)
    back_ref[1] = (rest_ref[1, 1] + mirror_ref[...].astype(F32)).astype(BF16)


def relay(rest, outer, mirror, total):
    vmem = pl.BlockSpec(memory_space=pltpu.VMEM)
    pair = jax.ShapeDtypeStruct((2, ROWS, TILE), BF16)
    return pl.pallas_call(
        relay_kernel,
        out_shape=(pair, pair),
        in_specs=[vmem] * 4,
        out_specs=(vmem,) * 2,
        compiler_params=pltpu.CompilerParams(vmem_limit_bytes=16 << 20),
        name="relay",
    )(rest, outer, mirror, total)


def mix_kernel(tracer_ref, diff_ref, depth_ref, solved_ref, unit_ref, state_ref, ahead, lower, upper):
    levels, fields, columns = tracer_ref.shape
    depth = depth_ref[...]
    zero = jnp.zeros((1, columns), F32)
    one = jnp.ones((1, columns), F32)

    def coupling(k):
        if k == 0 or k == levels:
            return zero
        return jnp.where(depth > k, diff_ref[pl.ds(k - 1, 1), :], zero)

    ratio = None
    for k in range(levels):
        a, b = coupling(k), coupling(k + 1)
        pivot = 1.0 + a + b
        if k > 0:
            pivot = pivot - a * ratio
        inverse = 1.0 / pivot
        ratio = b * inverse
        wet = jnp.where(depth > k, one, zero)
        ahead[pl.ds(k, 1), :] = wet * inverse
        lower[pl.ds(k, 1), :] = a * inverse
        upper[pl.ds(k, 1), :] = ratio
    unit = [jnp.where(depth > 0, one, zero)] + [zero] * (levels - 1)
    for sweep in range(2):
        carried = None
        unit_carried = None
        for k in range(levels):
            if sweep == 0:
                x = tracer_ref[k].astype(F32)
            else:
                x = state_ref[k]
            scale = ahead[pl.ds(k, 1), :]
            below = lower[pl.ds(k, 1), :]
            if k == 0:
                carried = x * scale
                unit_carried = unit[k] * scale
            else:
                carried = x * scale + carried * below
                unit_carried = unit[k] * scale + unit_carried * below
            if sweep == 1 and k == levels - 1:
                solved_ref[:, k, :] = carried
            else:
                state_ref[k] = carried
            unit[k] = unit_carried
        for k in range(levels - 2, -1, -1):
            above = upper[pl.ds(k, 1), :]
            carried = state_ref[k] + carried * above
            if sweep == 1:
                solved_ref[:, k, :] = carried
            else:
                state_ref[k] = carried
            unit[k] = unit[k] + unit[k + 1] * above
        for k in range(levels):
            unit_ref[sweep, pl.ds(k, 1), :] = unit[k]


def mix(tracers, diffusivity, column_depth):
    levels, fields, columns = tracers.shape
    vmem = pl.BlockSpec(memory_space=pltpu.VMEM)
    return pl.pallas_call(
        mix_kernel,
        out_shape=(jax.ShapeDtypeStruct((fields, levels, columns), F32),
                   jax.ShapeDtypeStruct((2, levels, columns), F32)),
        in_specs=[vmem] * 3,
        out_specs=(vmem, vmem),
        scratch_shapes=[pltpu.VMEM(tracers.shape, F32)] + [pltpu.VMEM((levels, columns), F32)] * 3,
        compiler_params=pltpu.CompilerParams(vmem_limit_bytes=24 << 20),
        cost_estimate=pl.CostEstimate(flops=12 * levels * fields * columns, transcendentals=0,
                                      bytes_accessed=6 * levels * fields * columns),
        name="mix",
    )(tracers, diffusivity, column_depth.reshape(1, columns))


def finish_kernel(scale, state_ref, unit_ref, rest_ref, near_ref, back_ref, total_ref, out_hbm,
                  surface, result, sems):
    fields, levels, columns = state_ref.shape
    eye = (lax.broadcasted_iota(jnp.int32, (ROWS, ROWS), 0)
           == lax.broadcasted_iota(jnp.int32, (ROWS, ROWS), 1))
    total = (total_ref[...] + total_in(near_ref[0]) + total_in(back_ref[0])) * scale
    spread = jnp.where(eye, jnp.broadcast_to(total, (ROWS, ROWS)), 0.0)
    fix = jnp.sum(spread, axis=1, keepdims=True)
    for o in range(2):
        surface[:, pl.ds(o * TILE, TILE)] = (rest_ref[o, 0] + near_ref[o].astype(F32)
                                             + back_ref[o].astype(F32)) + fix
    once = unit_ref[0]
    twice = unit_ref[1]
    copies = []
    for start in range(0, fields, FIELD_CHUNK):
        for f in range(start, start + FIELD_CHUNK):
            result[f] = (state_ref[f] + surface[pl.ds(f, 1), :] * twice
                         + surface[pl.ds(HALF + f, 1), :] * once)
        part = pl.ds(start, FIELD_CHUNK)
        copies.append(pltpu.make_async_copy(result.at[part], out_hbm.at[part],
                                            sems.at[start // FIELD_CHUNK]))
        copies[-1].start()
    for copy in copies:
        copy.wait()


def finish(state, unit, rest, near, back, total, scale):
    vmem = pl.BlockSpec(memory_space=pltpu.VMEM)
    fields, levels, columns = state.shape
    return pl.pallas_call(
        functools.partial(finish_kernel, scale),
        out_shape=jax.ShapeDtypeStruct(state.shape, F32),
        in_specs=[vmem] * 6,
        out_specs=pl.BlockSpec(memory_space=pltpu.HBM),
        scratch_shapes=[pltpu.VMEM((ROWS, columns), F32), pltpu.VMEM(state.shape, F32),
                        pltpu.SemaphoreType.DMA((fields // FIELD_CHUNK,))],
        compiler_params=pltpu.CompilerParams(vmem_limit_bytes=24 << 20),
        name="finish",
    )(state, unit, rest, near, back, total)


def shift(x, by, ring):
    return lax.ppermute(x, "blk", [(i, (i + by) % ring) for i in range(ring)])


def body(
    atm_flux,
    tile_bank,
    pair_count,
    pair_source,
    pair_tile,
    pair_target,
    tracers,
    diffusivity,
    column_depth,
):
    ring = lax.axis_size("blk")
    plane = lax.axis_size("sec") * lax.axis_size("grp")
    columns = tracers.shape[2]
    me = lax.axis_index("blk").astype(jnp.int32).reshape(1)
    right, left, keep, part = remap(pair_count, me, pair_source, pair_tile, pair_target, atm_flux,
                                    tile_bank, ring)
    right = shift(right, 1, ring)
    left = shift(left, -1, ring)
    column_depth, part = lax.optimization_barrier((column_depth, part))
    state, unit = mix(tracers, diffusivity, column_depth)
    part, unit = lax.optimization_barrier((part, unit))
    gathered = lax.all_to_all(jnp.broadcast_to(part[:1], (plane, ROWS)), ("sec", "grp"), 0, 0,
                              tiled=True)
    gathered, right = lax.optimization_barrier((gathered, right))
    own, near, back, far, other = combine(keep, right, left)
    group = ring // 4
    total = jnp.broadcast_to(jnp.sum(gathered, axis=0, keepdims=True), (group, ROWS))
    total = lax.all_to_all(total, "blk", 0, 0, tiled=True,
                           axis_index_groups=[[g * group + i for i in range(group)]
                                              for g in range(4)])
    near = shift(near, 2, ring)
    back = shift(back, -2, ring)
    far = shift(far, 4, ring)
    other = shift(other, -4, ring)
    total, near = lax.optimization_barrier((total, near))
    total = jnp.sum(total, axis=0, keepdims=True)
    outer, mirror, rest = gather(own, near, back, far, other, total)
    outer = shift(outer, 8, ring)
    mirror = shift(mirror, -8, ring)
    near, back = relay(rest, outer, mirror, total)
    near = shift(near, 8, ring)
    back = shift(back, -8, ring)
    result = finish(state, unit, rest, near, back, total, 1.0 / (columns * ring * plane))
    return jnp.transpose(result, (1, 0, 2))


def solution(mesh):
    placed = (
        P(None, None, ("sec", "grp", "blk")),
        P(),
        P(("sec", "grp", "blk")),
        P(("sec", "grp", "blk")),
        P(("sec", "grp", "blk")),
        P(("sec", "grp", "blk")),
        P(None, None, ("sec", "grp", "blk")),
        P(None, ("sec", "grp", "blk")),
        P(("sec", "grp", "blk")),
    )
    return jax.shard_map(
        body,
        mesh=mesh,
        in_specs=placed,
        out_specs=P(None, None, ("sec", "grp", "blk")),
        check_vma=False,
    )
```

time: 136 us -> 136 us (level)
  the two profiles are of different devices: /device:TPU:2 before, /device:TPU:1 now
where the time goes in v2:
time: 136 us; the launch traced here: 135 us
  starting transfers between devices  65.2 us (48%)
  blocking collectives  28.4 us (21%)
  waiting for transfers between devices  27.4 us (20%)
  Pallas kernels  11.5 us (8%)
  local copies, waits for them, and re-layouts  1.77 us (1%)
    ppermute x10, starting transfers between devices, shift(): return lax.ppermute(x, 'blk', [(i, (i + by) % ring) for i in range(ring)])  65.2 us
    ppermute x10, waiting for transfers between devices, shift(): return lax.ppermute(x, 'blk', [(i, (i + by) % ring) for i in range(ring)])  27.4 us
    all_to_all x1, blocking collectives, body(): lax.all_to_all(jnp.broadcast_to(part[:1], (plane, ROWS)), ('sec', 'grp'),...  15.3 us
    all_to_all x1, blocking collectives, body(): lax.all_to_all(total, 'blk', 0, 0, tiled=True, axis_index_groups=[[g * gr...  13.2 us
    pallas_call x1, Pallas kernels, remap(): pl.pallas_call(remap_kernel, out_shape=(jax.ShapeDtypeStruct((half, ROWS,...  6.92 us
  transfers between devices with their start and end apart: 10, of which 3 were waited for; matrix products, arithmetic and copies ran while one was open for 0% of the time, Pallas kernels for 1%

profile of v2, /device:TPU:1, one launch (start us, length us, event | category | flops | bytes accessed | tf_op | source)
XLA Modules:
  0.0 135.2 jit_solution(12814018496907209027)
XLA Ops:
  0.7 1.2 copy.10.flux_ref
  1.8 0.0 copy-start.2
  1.9 6.9 %remap.1 = (bf16[16,128,128]{2,1,0:T(8,128)(2,1)S(1)}, bf16[16,128,128]{2,1,0:T(8,128)(2,1)S(1)}, bf16[2,16,128,128]{3,2,1,0:T(8,128)(2,1)S(1)}, f32[8,128]{1,0:T(8,128)S(1)}) custom-call(s32[1]{0:T(128)S(6)} %copy.12.count_ref, s32[1]{0:T(128)} %bitcast.me_ref, s32[128]{0:T(128)} %source_hbm.1, s32[128]{0:T(128)} %tile_hbm.1, s32[128]{0:T(128)} %target_hbm.1, ...), custom_call_target="tpu_custom_call" | custom-call | flops 536870912 | bytes 8388608 | tf_op jit(solution)/shard_map/remap/pallas_call | solution.py:96
  8.8 0.0 copy-start
  8.8 0.0 copy-start.1
  8.8 2.0 %collective-permute-start = (bf16[16,128,128]{2,1,0:T(8,128)(2,1)S(1)}, bf16[16,128,128]{2,1,0:T(8,128)(2,1)S(1)}, u32[]{:S(2)}, u32[]{:S(2)}) collective-permute-start(bf16[16,128,128]{2,1,0:T(8,128)(2,1)S(1)} %get-tuple-element.37), channel_id=1, source_target_pairs={{0,1},{1,2},{2,3},{3,4},{4,5},{5,6},{6,7},{7,8},{8,9},{9,10},{10,1... | collective-permute-start | bytes 1572872 | tf_op jit(solution)/shard_map/ppermute | solution.py:334
  10.8 18.6 %collective-permute-start.1 = (bf16[16,128,128]{2,1,0:T(8,128)(2,1)S(1)}, bf16[16,128,128]{2,1,0:T(8,128)(2,1)S(1)}, u32[]{:S(2)}, u32[]{:S(2)}) collective-permute-start(bf16[16,128,128]{2,1,0:T(8,128)(2,1)S(1)} %get-tuple-element.39), channel_id=1, source_target_pairs={{0,31},{1,0},{2,1},{3,2},{4,3},{5,4},{6,5},{7,6},{8,7},{9,8},{10,9... | collective-permute-start | bytes 1572872 | tf_op jit(solution)/shard_map/ppermute | solution.py:334
  29.4 0.0 copy-done.2
  29.4 0.6 copy.11.tracer_ref
  30.0 0.0 copy-done
  30.0 0.0 copy-done.1
  30.0 2.0 %mix.1 = (f32[60,32,256]{2,1,0:T(8,128)S(1)}, f32[2,32,256]{2,1,0:T(8,128)S(1)}) custom-call(bf16[32,60,256]{2,1,0:T(8,128)(2,1)S(1)} %copy.11.tracer_ref, f32[31,256]{1,0:T(8,128)S(1)} %copy-done, s32[1,256]{1,0:T(1,128)S(1)} %bitcast.11), custom_call_target="tpu_custom_call" | custom-call | flops 5898240 | bytes 2949120 | tf_op jit(solution)/shard_map/mix/pallas_call | solution.py:278
  32.1 15.3 %all_to_all.18 = f32[32,1,128]{2,1,0:T(1,128)S(1)} all-to-all(f32[32,1,128]{2,1,0:T(1,128)S(1)} %broadcast_in_dim.6), channel_id=1, replica_groups=mesh['sec'=2,'grp'=16,'blk'=32] {'sec','grp'}, dimensions={0} | all-to-all | bytes 32768 | tf_op jit(solution)/shard_map/all_to_all | solution.py:359
  47.3 0.0 collective-permute-done.right_ref
  47.3 0.0 collective-permute-done.1.left_ref
  47.3 0.9 combine.1
  48.2 1.9 %collective-permute-start.2 = (bf16[2,4,128,128]{3,2,1,0:T(8,128)(2,1)}, bf16[2,4,128,128]{3,2,1,0:T(8,128)(2,1)S(1)}, u32[]{:S(2)}, u32[]{:S(2)}) collective-permute-start(bf16[2,4,128,128]{3,2,1,0:T(8,128)(2,1)} %get-tuple-element.42), channel_id=1, source_target_pairs={{0,2},{1,3},{2,4},{3,5},{4,6},{5,7},{6,8},{7,9},{8,10},{9,11},{10,... | collective-permute-start | bytes 786440 | tf_op jit(solution)/shard_map/ppermute | solution.py:334
  50.2 5.5 %collective-permute-start.3 = (bf16[2,4,128,128]{3,2,1,0:T(8,128)(2,1)}, bf16[2,4,128,128]{3,2,1,0:T(8,128)(2,1)S(1)}, u32[]{:S(2)}, u32[]{:S(2)}) collective-permute-start(bf16[2,4,128,128]{3,2,1,0:T(8,128)(2,1)} %get-tuple-element.44), channel_id=1, source_target_pairs={{0,30},{1,31},{2,0},{3,1},{4,2},{5,3},{6,4},{7,5},{8,6},{9,7},{10,... | collective-permute-start | bytes 786440 | tf_op jit(solution)/shard_map/ppermute | solution.py:334
  55.6 1.9 %collective-permute-start.4 = (bf16[4,128,128]{2,1,0:T(8,128)(2,1)}, bf16[4,128,128]{2,1,0:T(8,128)(2,1)S(1)}, u32[]{:S(2)}, u32[]{:S(2)}) collective-permute-start(bf16[4,128,128]{2,1,0:T(8,128)(2,1)} %get-tuple-element.45), channel_id=1, source_target_pairs={{0,4},{1,5},{2,6},{3,7},{4,8},{5,9},{6,10},{7,11},{8,12},{9,13},{1... | collective-permute-start | bytes 393224 | tf_op jit(solution)/shard_map/ppermute | solution.py:334
  57.6 7.3 %collective-permute-start.5 = (bf16[4,128,128]{2,1,0:T(8,128)(2,1)S(1)}, bf16[4,128,128]{2,1,0:T(8,128)(2,1)S(1)}, u32[]{:S(2)}, u32[]{:S(2)}) collective-permute-start(bf16[4,128,128]{2,1,0:T(8,128)(2,1)S(1)} %get-tuple-element.46), channel_id=1, source_target_pairs={{0,28},{1,29},{2,30},{3,31},{4,0},{5,1},{6,2},{7,3},{8,4},{9,5},{1... | collective-permute-start | bytes 393224 | tf_op jit(solution)/shard_map/ppermute | solution.py:334
  64.9 13.2 %all_to_all.19 = f32[8,1,128]{2,1,0:T(1,128)S(1)} all-to-all(f32[8,1,128]{2,1,0:T(1,128)S(1)} %broadcast_in_dim.7), channel_id=1, replica_groups={{0,1,2,3,4,5,6,7},{8,9,10,11,12,13,14,15},{16,17,18,19,20,21,22,23},{24..., dimensions={0} | all-to-all | bytes 8192 | tf_op jit(solution)/shard_map/all_to_all | solution.py:365
  78.0 0.0 collective-permute-done.2.near_ref
  78.1 0.0 collective-permute-done.4.far_ref
  78.1 0.0 collective-permute-done.5.other_ref
  78.1 0.0 collective-permute-done.3.back_ref
  78.1 0.1 gather.1
  78.2 10.8 %collective-permute-start.6 = (bf16[128,128]{1,0:T(8,128)(2,1)S(1)}, bf16[128,128]{1,0:T(8,128)(2,1)S(1)}, u32[]{:S(2)}, u32[]{:S(2)}) collective-permute-start(bf16[128,128]{1,0:T(8,128)(2,1)S(1)} %get-tuple-element.49), channel_id=1, source_target_pairs={{0,8},{1,9},{2,10},{3,11},{4,12},{5,13},{6,14},{7,15},{8,16},{9,17... | collective-permute-start | bytes 98312 | tf_op jit(solution)/shard_map/ppermute | solution.py:334
  89.0 3.3 %collective-permute-start.7 = (bf16[128,128]{1,0:T(8,128)(2,1)S(1)}, bf16[128,128]{1,0:T(8,128)(2,1)S(1)}, u32[]{:S(2)}, u32[]{:S(2)}) collective-permute-start(bf16[128,128]{1,0:T(8,128)(2,1)S(1)} %get-tuple-element.50), channel_id=1, source_target_pairs={{0,24},{1,25},{2,26},{3,27},{4,28},{5,29},{6,30},{7,31},{8,0},{9,1... | collective-permute-start | bytes 98312 | tf_op jit(solution)/shard_map/ppermute | solution.py:334
  92.3 0.0 collective-permute-done.6.outer_ref
  92.3 11.5 %collective-permute-done.7.mirror_ref = bf16[128,128]{1,0:T(8,128)(2,1)S(1)} collective-permute-done((bf16[128,128]{1,0:T(8,128)(2,1)S(1)}, bf16[128,128]{1,0:T(8,128)(2,1)S(1)}, u32[]{:S(2)}, u32[]{:S(2)}) %collective-permute-start.7) | collective-permute-done | bytes 32800 | tf_op jit(solution)/shard_map/ppermute | solution.py:334
  103.8 11.0 %collective-permute-start.8 = (bf16[2,128,128]{2,1,0:T(8,128)(2,1)S(1)}, bf16[2,128,128]{2,1,0:T(8,128)(2,1)S(1)}, u32[]{:S(2)}, u32[]{:S(2)}) collective-permute-start(bf16[2,128,128]{2,1,0:T(8,128)(2,1)S(1)} %get-tuple-element.51), channel_id=1, source_target_pairs={{0,8},{1,9},{2,10},{3,11},{4,12},{5,13},{6,14},{7,15},{8,16},{9,17... | collective-permute-start | bytes 196616 | tf_op jit(solution)/shard_map/ppermute | solution.py:334
  114.8 3.0 %collective-permute-start.9 = (bf16[2,128,128]{2,1,0:T(8,128)(2,1)S(1)}, bf16[2,128,128]{2,1,0:T(8,128)(2,1)S(1)}, u32[]{:S(2)}, u32[]{:S(2)}) collective-permute-start(bf16[2,128,128]{2,1,0:T(8,128)(2,1)S(1)} %get-tuple-element.52), channel_id=1, source_target_pairs={{0,24},{1,25},{2,26},{3,27},{4,28},{5,29},{6,30},{7,31},{8,0},{9,1... | collective-permute-start | bytes 196616 | tf_op jit(solution)/shard_map/ppermute | solution.py:334
  117.8 2.5 %collective-permute-done.8.near_ref = bf16[2,128,128]{2,1,0:T(8,128)(2,1)S(1)} collective-permute-done((bf16[2,128,128]{2,1,0:T(8,128)(2,1)S(1)}, bf16[2,128,128]{2,1,0:T(8,128)(2,1)S(1)}, u32[]{:S(2)}, u32[]{:S(2)}) %collective-permute-start.8) | collective-permute-done | bytes 65568 | tf_op jit(solution)/shard_map/ppermute | solution.py:334
  120.3 13.5 %collective-permute-done.9.back_ref = bf16[2,128,128]{2,1,0:T(8,128)(2,1)S(1)} collective-permute-done((bf16[2,128,128]{2,1,0:T(8,128)(2,1)S(1)}, bf16[2,128,128]{2,1,0:T(8,128)(2,1)S(1)}, u32[]{:S(2)}, u32[]{:S(2)}) %collective-permute-start.9) | collective-permute-done | bytes 65568 | tf_op jit(solution)/shard_map/ppermute | solution.py:334
  133.8 1.5 %finish.1 = f32[60,32,256]{2,1,0:T(8,128)} custom-call(f32[60,32,256]{2,1,0:T(8,128)S(1)} %get-tuple-element.31.state_ref, f32[2,32,256]{2,1,0:T(8,128)S(1)} %get-tuple-element.34.unit_ref, f32[2,3,128,128]{3,2,1,0:T(8,128)S(1)} %get-tuple-element.48.rest_ref, bf16[2,128,128]{2,1,0:T(8,128)(2,1)S(1)} %collective-permute-done.8.near_ref, ...), custom_call_target="tpu_custom_call" | custom-call | tf_op jit(solution)/shard_map/finish/pallas_call | solution.py:321
  (6 shorter events, 0.1 us)
Async XLA Ops:
  1.8 27.6 %copy-start.2 = (bf16[32,60,256]{2,0,1:T(8,128)(2,1)S(1)}, bf16[32,60,256]{2,0,1:T(8,128)(2,1)}, u32[]{:S(2)}) copy-start(bf16[32,60,256]{2,0,1:T(8,128)(2,1)} %param.15) | copy-start | bytes 2949124
  8.8 21.2 %copy-start = (f32[31,256]{1,0:T(8,128)S(1)}, f32[31,256]{1,0:T(8,128)}, u32[]{:S(2)}) copy-start(f32[31,256]{1,0:T(8,128)} %diff_ref.1) | copy-start | bytes 95236
  8.8 21.2 %copy-start.1 = (s32[256]{0:T(256)S(1)}, s32[256]{0:T(256)}, u32[]{:S(2)}) copy-start(s32[256]{0:T(256)} %param.17) | copy-start | bytes 3076
  8.8 38.5 %collective-permute-start = (bf16[16,128,128]{2,1,0:T(8,128)(2,1)S(1)}, bf16[16,128,128]{2,1,0:T(8,128)(2,1)S(1)}, u32[]{:S(2)}, u32[]{:S(2)}) collective-permute-start(bf16[16,128,128]{2,1,0:T(8,128)(2,1)S(1)} %get-tuple-element.37), channel_id=1, source_target_pairs={{0,1},{1,2},{2,3},{3,4},{4,5},{5,6},{6,7},{7,8},{8,9},{9,10},{10,1... | collective-permute-start | bytes 1572872 | tf_op jit(solution)/shard_map/ppermute | solution.py:334
  10.8 36.5 %collective-permute-start.1 = (bf16[16,128,128]{2,1,0:T(8,128)(2,1)S(1)}, bf16[16,128,128]{2,1,0:T(8,128)(2,1)S(1)}, u32[]{:S(2)}, u32[]{:S(2)}) collective-permute-start(bf16[16,128,128]{2,1,0:T(8,128)(2,1)S(1)} %get-tuple-element.39), channel_id=1, source_target_pairs={{0,31},{1,0},{2,1},{3,2},{4,3},{5,4},{6,5},{7,6},{8,7},{9,8},{10,9... | collective-permute-start | bytes 1572872 | tf_op jit(solution)/shard_map/ppermute | solution.py:334
  48.2 29.8 %collective-permute-start.2 = (bf16[2,4,128,128]{3,2,1,0:T(8,128)(2,1)}, bf16[2,4,128,128]{3,2,1,0:T(8,128)(2,1)S(1)}, u32[]{:S(2)}, u32[]{:S(2)}) collective-permute-start(bf16[2,4,128,128]{3,2,1,0:T(8,128)(2,1)} %get-tuple-element.42), channel_id=1, source_target_pairs={{0,2},{1,3},{2,4},{3,5},{4,6},{5,7},{6,8},{7,9},{8,10},{9,11},{10,... | collective-permute-start | bytes 786440 | tf_op jit(solution)/shard_map/ppermute | solution.py:334
  50.2 27.9 %collective-permute-start.3 = (bf16[2,4,128,128]{3,2,1,0:T(8,128)(2,1)}, bf16[2,4,128,128]{3,2,1,0:T(8,128)(2,1)S(1)}, u32[]{:S(2)}, u32[]{:S(2)}) collective-permute-start(bf16[2,4,128,128]{3,2,1,0:T(8,128)(2,1)} %get-tuple-element.44), channel_id=1, source_target_pairs={{0,30},{1,31},{2,0},{3,1},{4,2},{5,3},{6,4},{7,5},{8,6},{9,7},{10,... | collective-permute-start | bytes 786440 | tf_op jit(solution)/shard_map/ppermute | solution.py:334
  55.6 22.4 %collective-permute-start.4 = (bf16[4,128,128]{2,1,0:T(8,128)(2,1)}, bf16[4,128,128]{2,1,0:T(8,128)(2,1)S(1)}, u32[]{:S(2)}, u32[]{:S(2)}) collective-permute-start(bf16[4,128,128]{2,1,0:T(8,128)(2,1)} %get-tuple-element.45), channel_id=1, source_target_pairs={{0,4},{1,5},{2,6},{3,7},{4,8},{5,9},{6,10},{7,11},{8,12},{9,13},{1... | collective-permute-start | bytes 393224 | tf_op jit(solution)/shard_map/ppermute | solution.py:334
  57.6 20.5 %collective-permute-start.5 = (bf16[4,128,128]{2,1,0:T(8,128)(2,1)S(1)}, bf16[4,128,128]{2,1,0:T(8,128)(2,1)S(1)}, u32[]{:S(2)}, u32[]{:S(2)}) collective-permute-start(bf16[4,128,128]{2,1,0:T(8,128)(2,1)S(1)} %get-tuple-element.46), channel_id=1, source_target_pairs={{0,28},{1,29},{2,30},{3,31},{4,0},{5,1},{6,2},{7,3},{8,4},{9,5},{1... | collective-permute-start | bytes 393224 | tf_op jit(solution)/shard_map/ppermute | solution.py:334
  78.2 14.1 %collective-permute-start.6 = (bf16[128,128]{1,0:T(8,128)(2,1)S(1)}, bf16[128,128]{1,0:T(8,128)(2,1)S(1)}, u32[]{:S(2)}, u32[]{:S(2)}) collective-permute-start(bf16[128,128]{1,0:T(8,128)(2,1)S(1)} %get-tuple-element.49), channel_id=1, source_target_pairs={{0,8},{1,9},{2,10},{3,11},{4,12},{5,13},{6,14},{7,15},{8,16},{9,17... | collective-permute-start | bytes 98312 | tf_op jit(solution)/shard_map/ppermute | solution.py:334
  89.0 14.8 %collective-permute-start.7 = (bf16[128,128]{1,0:T(8,128)(2,1)S(1)}, bf16[128,128]{1,0:T(8,128)(2,1)S(1)}, u32[]{:S(2)}, u32[]{:S(2)}) collective-permute-start(bf16[128,128]{1,0:T(8,128)(2,1)S(1)} %get-tuple-element.50), channel_id=1, source_target_pairs={{0,24},{1,25},{2,26},{3,27},{4,28},{5,29},{6,30},{7,31},{8,0},{9,1... | collective-permute-start | bytes 98312 | tf_op jit(solution)/shard_map/ppermute | solution.py:334
  103.8 16.5 %collective-permute-start.8 = (bf16[2,128,128]{2,1,0:T(8,128)(2,1)S(1)}, bf16[2,128,128]{2,1,0:T(8,128)(2,1)S(1)}, u32[]{:S(2)}, u32[]{:S(2)}) collective-permute-start(bf16[2,128,128]{2,1,0:T(8,128)(2,1)S(1)} %get-tuple-element.51), channel_id=1, source_target_pairs={{0,8},{1,9},{2,10},{3,11},{4,12},{5,13},{6,14},{7,15},{8,16},{9,17... | collective-permute-start | bytes 196616 | tf_op jit(solution)/shard_map/ppermute | solution.py:334
  114.8 18.9 %collective-permute-start.9 = (bf16[2,128,128]{2,1,0:T(8,128)(2,1)S(1)}, bf16[2,128,128]{2,1,0:T(8,128)(2,1)S(1)}, u32[]{:S(2)}, u32[]{:S(2)}) collective-permute-start(bf16[2,128,128]{2,1,0:T(8,128)(2,1)S(1)} %get-tuple-element.52), channel_id=1, source_target_pairs={{0,24},{1,25},{2,26},{3,27},{4,28},{5,29},{6,30},{7,31},{8,0},{9,1... | collective-permute-start | bytes 196616 | tf_op jit(solution)/shard_map/ppermute | solution.py:334

commit v3 on v2

--- a/solution.py
+++ b/solution.py
@@ -15,6 +15,9 @@
 UNROLL = 4
 BANK_COPIES = 8
 FIELD_CHUNK = 15
+AHEAD = 13
+PLUS = 10
+MINUS = 11
 
 
 def remap_kernel(count_ref, me_ref, source_hbm, tile_hbm, target_hbm, flux_ref, bank_hbm,
@@ -22,8 +25,7 @@
                  source_ref, tile_ref, target_ref, bank_ref, blocks, acc, list_sem, bank_sem):
     subs, fields, atm_rows = flux_ref.shape
     source_blocks = atm_rows // TILE
-    sent_slots = right_ref.shape[0]
-    slots = 2 * sent_slots
+    slots = (acc.shape[0] - 1) // 2
     lists = [pltpu.make_async_copy(src, dst, list_sem.at[i]) for i, (src, dst) in enumerate(
         ((source_hbm, source_ref), (tile_hbm, tile_ref), (target_hbm, target_ref)))]
     span = bank_ref.shape[0] // BANK_COPIES
@@ -48,12 +50,8 @@
         target = target_ref[p]
         half = target & 1
         owner = target >> 1
-        r = jnp.where(half == 0, owner - me, me - owner) & (slots - 1)
-        r1 = r & 1
-        r2 = (r >> 1) & 3
-        r3 = ((r >> 3) + jnp.where(r2 == 3, 1, 0)) & 3
-        place = half * slots + r1 * sent_slots + r2 * 4 + r3
-        return jnp.where(p < count, place, 2 * slots)
+        away = (jnp.where(half == 0, owner - me, me - owner) + AHEAD) & (slots - 1)
+        return jnp.where(p < count, half * slots + away, 2 * slots)
 
     def group(g, carry):
         terms = []
@@ -68,19 +66,18 @@
 
     lax.fori_loop(0, (count + UNROLL - 1) // UNROLL, group, 0)
 
-    def flush(i, ocean):
-        for half in range(2):
-            kept = acc[half * slots + i].astype(BF16)
-            sent = acc[half * slots + sent_slots + i].astype(BF16)
-            keep_ref[half, i] = kept
-            if half == 0:
-                right_ref[i] = sent
-            else:
-                left_ref[i] = sent
-            ocean = ocean + kept.astype(F32) + sent.astype(F32)
-        return ocean
-
-    ocean = lax.fori_loop(0, sent_slots, flush, jnp.zeros((ROWS, TILE), F32), unroll=4)
+    ocean = jnp.zeros((ROWS, TILE), F32)
+    for half in range(2):
+        for away in range(slots):
+            value = acc[half * slots + away].astype(BF16)
+            ocean = ocean + value.astype(F32)
+            place, digit = away // 3, away % 3
+            if digit == 1:
+                keep_ref[half, place] = value
+            elif (digit == 2) == (half == 0):
+                right_ref[place + (0 if half == 0 else PLUS)] = value
+            else:
+                left_ref[place + (0 if half == 0 else MINUS)] = value
     share = 2.0 * TILE / atm_rows
     part = atm * share - ocean
     part_ref[...] = lax.dot_general(jnp.ones((8, TILE), F32), part, (((1,), (1,)), ((), ())),
@@ -92,12 +89,11 @@
     vmem = pl.BlockSpec(memory_space=pltpu.VMEM)
     hbm = pl.BlockSpec(memory_space=pltpu.HBM)
     source_blocks = flux.shape[2] // TILE
-    half = slots // 2
     return pl.pallas_call(
         remap_kernel,
-        out_shape=(jax.ShapeDtypeStruct((half, ROWS, TILE), BF16),
-                   jax.ShapeDtypeStruct((half, ROWS, TILE), BF16),
-                   jax.ShapeDtypeStruct((2, half, ROWS, TILE), BF16),
+        out_shape=(jax.ShapeDtypeStruct((PLUS + MINUS, ROWS, TILE), BF16),
+                   jax.ShapeDtypeStruct((PLUS + MINUS, ROWS, TILE), BF16),
+                   jax.ShapeDtypeStruct((2, MINUS, ROWS, TILE), BF16),
                    jax.ShapeDtypeStruct((8, ROWS), F32)),
         in_specs=[smem] * 2 + [hbm] * 3 + [vmem, hbm],
         out_specs=(vmem,) * 4,
@@ -116,35 +112,31 @@
       pltpu.with_memory_space_constraint(bank, pltpu.HBM))
 
 
-def combine_kernel(keep_ref, right_ref, left_ref, own_ref, near_ref, back_ref, far_ref, other_ref):
-    for code in range(4):
-        for i in range(4):
-            place = code * 4 + i
-            first = keep_ref[0, place].astype(F32) + right_ref[place].astype(F32)
-            second = keep_ref[1, place].astype(F32) + left_ref[place].astype(F32)
-            if code == 0:
-                own_ref[0, i] = first
-                own_ref[1, i] = second
-            elif code == 1:
-                near_ref[0, i] = first.astype(BF16)
-                back_ref[1, i] = second.astype(BF16)
-            elif code == 3:
-                back_ref[0, i] = first.astype(BF16)
-                near_ref[1, i] = second.astype(BF16)
-            else:
-                far_ref[i] = first.astype(BF16)
-                other_ref[i] = second.astype(BF16)
+def combine_kernel(keep_ref, right_ref, left_ref, own_ref, near_ref, back_ref):
+    for o in range(2):
+        for place in range(MINUS):
+            value = keep_ref[o, place].astype(F32)
+            plus, minus = (right_ref, left_ref) if o == 0 else (left_ref, right_ref)
+            if place < PLUS:
+                value = value + plus[place + (0 if o == 0 else MINUS)].astype(F32)
+            value = value + minus[place + (0 if o == 0 else PLUS)].astype(F32)
+            code, digit = place // 3, place % 3
+            if digit == 1:
+                own_ref[o, code] = value
+            elif (digit == 2) == (o == 0):
+                near_ref[code + (0 if o == 0 else 3)] = value.astype(BF16)
+            else:
+                back_ref[code + (0 if o == 0 else 4)] = value.astype(BF16)
 
 
 def combine(keep, right, left):
     vmem = pl.BlockSpec(memory_space=pltpu.VMEM)
-    pair = jax.ShapeDtypeStruct((2, 4, ROWS, TILE), BF16)
-    single = jax.ShapeDtypeStruct((4, ROWS, TILE), BF16)
+    sent = jax.ShapeDtypeStruct((7, ROWS, TILE), BF16)
     return pl.pallas_call(
         combine_kernel,
-        out_shape=(jax.ShapeDtypeStruct((2, 4, ROWS, TILE), F32), pair, pair, single, single),
+        out_shape=(jax.ShapeDtypeStruct((2, 4, ROWS, TILE), F32), sent, sent),
         in_specs=[vmem] * 3,
-        out_specs=(vmem,) * 5,
+        out_specs=(vmem,) * 3,
         compiler_params=pltpu.CompilerParams(vmem_limit_bytes=16 << 20),
         name="combine",
     )(keep, right, left)
@@ -165,54 +157,41 @@
     return rows[place:place + 1] + rows[place + 1:place + 2] + rows[place + 2:place + 3]
 
 
-def gather_kernel(own_ref, near_ref, back_ref, far_ref, other_ref, total_ref,
-                  outer_ref, mirror_ref, rest_ref):
+def gather_kernel(own_ref, near_ref, back_ref, window_ref, tail_ref,
+                  rest_ref, plus_ref, minus_ref, far_ref, other_ref):
     for o in range(2):
-        for at, code in enumerate((2, 0, 1, 3)):
-            last = (far_ref, other_ref)[o]
-            value = (own_ref[o, code] + near_ref[o, code].astype(F32)
-                     + back_ref[o, code].astype(F32) + last[code].astype(F32))
-            if at > 0:
-                rest_ref[o, at - 1] = value
-            elif o == 0:
-                outer_ref[...] = with_total(value, total_ref[...])
-            else:
-                mirror_ref[...] = value.astype(BF16)
-
-
-def gather(own, near, back, far, other, total):
+        for code in range(4):
+            value = own_ref[o, code]
+            up, down = (near_ref, back_ref) if o == 0 else (back_ref, near_ref)
+            if code < 3:
+                value = value + up[code + (0 if o == 0 else 4)].astype(F32)
+            value = value + down[code + (0 if o == 0 else 3)].astype(F32)
+            if code == 1:
+                rest_ref[o] = value
+            elif code == 3 and o == 0:
+                far_ref[...] = with_total(value, tail_ref[...])
+            elif code == 3:
+                other_ref[...] = value.astype(BF16)
+            else:
+                sent = with_total(value, window_ref[...]) if o == 0 else value.astype(BF16)
+                if (code == 2) == (o == 0):
+                    plus_ref[o] = sent
+                else:
+                    minus_ref[o] = sent
+
+
+def gather(own, near, back, window, tail):
     vmem = pl.BlockSpec(memory_space=pltpu.VMEM)
     chunk = jax.ShapeDtypeStruct((ROWS, TILE), BF16)
+    pair = jax.ShapeDtypeStruct((2, ROWS, TILE), BF16)
     return pl.pallas_call(
         gather_kernel,
-        out_shape=(chunk, chunk, jax.ShapeDtypeStruct((2, 3, ROWS, TILE), F32)),
-        in_specs=[vmem] * 6,
-        out_specs=(vmem,) * 3,
+        out_shape=(jax.ShapeDtypeStruct((2, ROWS, TILE), F32), pair, pair, chunk, chunk),
+        in_specs=[vmem] * 5,
+        out_specs=(vmem,) * 5,
         compiler_params=pltpu.CompilerParams(vmem_limit_bytes=16 << 20),
         name="gather",
-    )(own, near, back, far, other, total)
-
-
-def relay_kernel(rest_ref, outer_ref, mirror_ref, total_ref, near_ref, back_ref):
-    total = total_ref[...]
-    near_ref[0] = with_total(rest_ref[0, 1] + outer_ref[...].astype(F32),
-                             total + total_in(outer_ref[...]))
-    near_ref[1] = rest_ref[1, 2].astype(BF16)
-    back_ref[0] = with_total(rest_ref[0, 2], total)
-    back_ref[1] = (rest_ref[1, 1] + mirror_ref[...].astype(F32)).astype(BF16)
-
-
-def relay(rest, outer, mirror, total):
-    vmem = pl.BlockSpec(memory_space=pltpu.VMEM)
-    pair = jax.ShapeDtypeStruct((2, ROWS, TILE), BF16)
-    return pl.pallas_call(
-        relay_kernel,
-        out_shape=(pair, pair),
-        in_specs=[vmem] * 4,
-        out_specs=(vmem,) * 2,
-        compiler_params=pltpu.CompilerParams(vmem_limit_bytes=16 << 20),
-        name="relay",
-    )(rest, outer, mirror, total)
+    )(own, near, back, window, tail)
 
 
 def mix_kernel(tracer_ref, diff_ref, depth_ref, solved_ref, unit_ref, state_ref, ahead, lower, upper):
@@ -289,17 +268,21 @@
     )(tracers, diffusivity, column_depth.reshape(1, columns))
 
 
-def finish_kernel(scale, state_ref, unit_ref, rest_ref, near_ref, back_ref, total_ref, out_hbm,
+def finish_kernel(scale, state_ref, unit_ref, rest_ref, plus_ref, minus_ref, far_ref, other_ref,
+                  total_ref, out_hbm,
                   surface, result, sems):
     fields, levels, columns = state_ref.shape
     eye = (lax.broadcasted_iota(jnp.int32, (ROWS, ROWS), 0)
            == lax.broadcasted_iota(jnp.int32, (ROWS, ROWS), 1))
-    total = (total_ref[...] + total_in(near_ref[0]) + total_in(back_ref[0])) * scale
+    total = (total_ref[...] + total_in(plus_ref[0]) + total_in(minus_ref[0])
+             + total_in(far_ref[...])) * scale
     spread = jnp.where(eye, jnp.broadcast_to(total, (ROWS, ROWS)), 0.0)
     fix = jnp.sum(spread, axis=1, keepdims=True)
     for o in range(2):
-        surface[:, pl.ds(o * TILE, TILE)] = (rest_ref[o, 0] + near_ref[o].astype(F32)
-                                             + back_ref[o].astype(F32)) + fix
+        last = (far_ref, other_ref)[o]
+        surface[:, pl.ds(o * TILE, TILE)] = (rest_ref[o] + plus_ref[o].astype(F32)
+                                             + minus_ref[o].astype(F32)
+                                             + last[...].astype(F32)) + fix
     once = unit_ref[0]
     twice = unit_ref[1]
     copies = []
@@ -315,19 +298,19 @@
         copy.wait()
 
 
-def finish(state, unit, rest, near, back, total, scale):
+def finish(state, unit, rest, plus, minus, far, other, total, scale):
     vmem = pl.BlockSpec(memory_space=pltpu.VMEM)
     fields, levels, columns = state.shape
     return pl.pallas_call(
         functools.partial(finish_kernel, scale),
         out_shape=jax.ShapeDtypeStruct(state.shape, F32),
-        in_specs=[vmem] * 6,
+        in_specs=[vmem] * 8,
         out_specs=pl.BlockSpec(memory_space=pltpu.HBM),
         scratch_shapes=[pltpu.VMEM((ROWS, columns), F32), pltpu.VMEM(state.shape, F32),
                         pltpu.SemaphoreType.DMA((fields // FIELD_CHUNK,))],
         compiler_params=pltpu.CompilerParams(vmem_limit_bytes=24 << 20),
         name="finish",
-    )(state, unit, rest, near, back, total)
+    )(state, unit, rest, plus, minus, far, other, total)
 
 
 def shift(x, by, ring):
@@ -353,31 +336,29 @@
                                     tile_bank, ring)
     right = shift(right, 1, ring)
     left = shift(left, -1, ring)
-    column_depth, part = lax.optimization_barrier((column_depth, part))
-    state, unit = mix(tracers, diffusivity, column_depth)
-    part, unit = lax.optimization_barrier((part, unit))
     gathered = lax.all_to_all(jnp.broadcast_to(part[:1], (plane, ROWS)), ("sec", "grp"), 0, 0,
                               tiled=True)
     gathered, right = lax.optimization_barrier((gathered, right))
-    own, near, back, far, other = combine(keep, right, left)
-    group = ring // 4
-    total = jnp.broadcast_to(jnp.sum(gathered, axis=0, keepdims=True), (group, ROWS))
-    total = lax.all_to_all(total, "blk", 0, 0, tiled=True,
-                           axis_index_groups=[[g * group + i for i in range(group)]
-                                              for g in range(4)])
-    near = shift(near, 2, ring)
-    back = shift(back, -2, ring)
-    far = shift(far, 4, ring)
-    other = shift(other, -4, ring)
-    total, near = lax.optimization_barrier((total, near))
-    total = jnp.sum(total, axis=0, keepdims=True)
-    outer, mirror, rest = gather(own, near, back, far, other, total)
-    outer = shift(outer, 8, ring)
-    mirror = shift(mirror, -8, ring)
-    near, back = relay(rest, outer, mirror, total)
-    near = shift(near, 8, ring)
-    back = shift(back, -8, ring)
-    result = finish(state, unit, rest, near, back, total, 1.0 / (columns * ring * plane))
+    own, near, back = combine(keep, right, left)
+    near = shift(near, 3, ring)
+    back = shift(back, -3, ring)
+    gathered, own = lax.optimization_barrier((gathered, own))
+    column_depth, own = lax.optimization_barrier((column_depth, own))
+    state, unit = mix(tracers, diffusivity, column_depth)
+    level = jnp.sum(gathered, axis=0, keepdims=True)
+    before, after = shift(level, 1, ring), shift(level, -1, ring)
+    three = level + before + after
+    behind, beyond = shift(three, 3, ring), shift(three, -3, ring)
+    window = three + behind + beyond
+    tail = level + after + beyond
+    window, tail, near, back = lax.optimization_barrier((window, tail, near, back))
+    rest, plus, minus, far, other = gather(own, near, back, window, tail)
+    far = shift(far, -14, ring)
+    other = shift(other, 14, ring)
+    plus = shift(plus, 9, ring)
+    minus = shift(minus, -9, ring)
+    result = finish(state, unit, rest, plus, minus, far, other, window,
+                    1.0 / (columns * ring * plane))
     return jnp.transpose(result, (1, 0, 2))
 
 

time: 136 us -> 132 us (0.971)
  the two profiles are of different devices: /device:TPU:1 before, /device:TPU:46 now
where the time goes in v3:
time: 132 us
  starting transfers between devices  78.1 us (59%)
  waiting for transfers between devices  25.5 us (19%)
  blocking collectives  17.2 us (13%)
  Pallas kernels  8.17 us (6%)
  local copies, waits for them, and re-layouts  1.76 us (1%)
    ppermute x12, starting transfers between devices, shift(): return lax.ppermute(x, 'blk', [(i, (i + by) % ring) for i in range(ring)])  78.1 us
    ppermute x12, waiting for transfers between devices, shift(): return lax.ppermute(x, 'blk', [(i, (i + by) % ring) for i in range(ring)])  25.5 us
    all_to_all x1, blocking collectives, body(): lax.all_to_all(jnp.broadcast_to(part[:1], (plane, ROWS)), ('sec', 'grp'),...  17.2 us
    pallas_call x1, Pallas kernels, remap(): pl.pallas_call(remap_kernel, out_shape=(jax.ShapeDtypeStruct((PLUS + MINU...  4.35 us
  transfers between devices with their start and end apart: 12, of which 4 were waited for; matrix products, arithmetic and copies ran while one was open for 0% of the time, Pallas kernels for 2%

profile of v3, /device:TPU:46, one launch (start us, length us, event | category | flops | bytes accessed | tf_op | source)
XLA Modules:
  0.0 131.7 jit_solution(4447183570885121983)
XLA Ops:
  0.7 1.2 copy.10.flux_ref
  1.8 4.3 %remap.1 = (bf16[21,128,128]{2,1,0:T(8,128)(2,1)S(1)}, bf16[21,128,128]{2,1,0:T(8,128)(2,1)S(1)}, bf16[2,11,128,128]{3,2,1,0:T(8,128)(2,1)S(1)}, f32[8,128]{1,0:T(8,128)S(1)}) custom-call(s32[1]{0:T(128)S(6)} %copy.12.count_ref, s32[1]{0:T(128)} %bitcast.me_ref, s32[128]{0:T(128)} %source_hbm.1, s32[128]{0:T(128)} %tile_hbm.1, s32[128]{0:T(128)} %target_hbm.1, ...), custom_call_target="tpu_custom_call" | custom-call | flops 536870912 | bytes 8388608 | tf_op jit(solution)/shard_map/remap/pallas_call | solution.py:92
  6.2 0.0 copy-start.2
  6.2 6.0 %collective-permute-start = (bf16[21,128,128]{2,1,0:T(8,128)(2,1)S(1)}, bf16[21,128,128]{2,1,0:T(8,128)(2,1)S(1)}, u32[]{:S(2)}, u32[]{:S(2)}) collective-permute-start(bf16[21,128,128]{2,1,0:T(8,128)(2,1)S(1)} %get-tuple-element.30), channel_id=1, source_target_pairs={{0,1},{1,2},{2,3},{3,4},{4,5},{5,6},{6,7},{7,8},{8,9},{9,10},{10,1... | collective-permute-start | bytes 2064392 | tf_op jit(solution)/shard_map/ppermute | solution.py:317
  12.2 1.9 %collective-permute-start.1 = (bf16[21,128,128]{2,1,0:T(8,128)(2,1)S(1)}, bf16[21,128,128]{2,1,0:T(8,128)(2,1)S(1)}, u32[]{:S(2)}, u32[]{:S(2)}) collective-permute-start(bf16[21,128,128]{2,1,0:T(8,128)(2,1)S(1)} %get-tuple-element.34), channel_id=1, source_target_pairs={{0,31},{1,0},{2,1},{3,2},{4,3},{5,4},{6,5},{7,6},{8,7},{9,8},{10,9... | collective-permute-start | bytes 2064392 | tf_op jit(solution)/shard_map/ppermute | solution.py:317
  14.1 17.2 %all_to_all.9 = f32[32,1,128]{2,1,0:T(1,128)S(1)} all-to-all(f32[32,1,128]{2,1,0:T(1,128)S(1)} %broadcast_in_dim.8), channel_id=1, replica_groups=mesh['sec'=2,'grp'=16,'blk'=32] {'sec','grp'}, dimensions={0} | all-to-all | bytes 32768 | tf_op jit(solution)/shard_map/all_to_all | solution.py:339
  31.3 0.0 collective-permute-done.right_ref
  31.3 0.0 collective-permute-done.1.left_ref
  31.3 0.2 combine.1
  31.6 0.0 copy-start
  31.6 0.0 copy-start.1
  31.6 12.9 %collective-permute-start.3 = (f32[1,128]{1,0:T(1,128)S(1)}, f32[1,128]{1,0:T(1,128)S(1)}, u32[]{:S(2)}, u32[]{:S(2)}) collective-permute-start(f32[1,128]{1,0:T(1,128)S(1)} %bitcast.11), channel_id=1, source_target_pairs={{0,31},{1,0},{2,1},{3,2},{4,3},{5,4},{6,5},{7,6},{8,7},{9,8},{10,9... | collective-permute-start | bytes 1544 | tf_op jit(solution)/shard_map/ppermute | solution.py:317
  44.5 1.9 %collective-permute-start.2 = (f32[1,128]{1,0:T(1,128)S(1)}, f32[1,128]{1,0:T(1,128)S(1)}, u32[]{:S(2)}, u32[]{:S(2)}) collective-permute-start(f32[1,128]{1,0:T(1,128)S(1)} %bitcast.12), channel_id=1, source_target_pairs={{0,1},{1,2},{2,3},{3,4},{4,5},{5,6},{6,7},{7,8},{8,9},{9,10},{10,1... | collective-permute-start | bytes 1544 | tf_op jit(solution)/shard_map/ppermute | solution.py:317
  46.4 1.9 %collective-permute-start.6 = (bf16[7,128,128]{2,1,0:T(8,128)(2,1)S(1)}, bf16[7,128,128]{2,1,0:T(8,128)(2,1)S(1)}, u32[]{:S(2)}, u32[]{:S(2)}) collective-permute-start(bf16[7,128,128]{2,1,0:T(8,128)(2,1)S(1)} %get-tuple-element.42), channel_id=1, source_target_pairs={{0,3},{1,4},{2,5},{3,6},{4,7},{5,8},{6,9},{7,10},{8,11},{9,12},{10... | collective-permute-start | bytes 688136 | tf_op jit(solution)/shard_map/ppermute | solution.py:317
  48.3 7.0 %collective-permute-start.7 = (bf16[7,128,128]{2,1,0:T(8,128)(2,1)S(1)}, bf16[7,128,128]{2,1,0:T(8,128)(2,1)S(1)}, u32[]{:S(2)}, u32[]{:S(2)}) collective-permute-start(bf16[7,128,128]{2,1,0:T(8,128)(2,1)S(1)} %get-tuple-element.43), channel_id=1, source_target_pairs={{0,29},{1,30},{2,31},{3,0},{4,1},{5,2},{6,3},{7,4},{8,5},{9,6},{10... | collective-permute-start | bytes 688136 | tf_op jit(solution)/shard_map/ppermute | solution.py:317
  55.4 0.0 collective-permute-done.3
  55.4 0.0 collective-permute-done.2
  55.4 7.4 %collective-permute-start.5 = (f32[1,128]{1,0:T(1,128)S(1)}, f32[1,128]{1,0:T(1,128)S(1)}, u32[]{:S(2)}, u32[]{:S(2)}) collective-permute-start(f32[1,128]{1,0:T(1,128)S(1)} %add_add_fusion.2), channel_id=1, source_target_pairs={{0,29},{1,30},{2,31},{3,0},{4,1},{5,2},{6,3},{7,4},{8,5},{9,6},{10... | collective-permute-start | bytes 1544 | tf_op jit(solution)/shard_map/ppermute | solution.py:317
  62.8 1.9 %collective-permute-start.4 = (f32[1,128]{1,0:T(1,128)S(1)}, f32[1,128]{1,0:T(1,128)S(1)}, u32[]{:S(2)}, u32[]{:S(2)}) collective-permute-start(f32[1,128]{1,0:T(1,128)S(1)} %add_add_fusion.2), channel_id=1, source_target_pairs={{0,3},{1,4},{2,5},{3,6},{4,7},{5,8},{6,9},{7,10},{8,11},{9,12},{10... | collective-permute-start | bytes 1544 | tf_op jit(solution)/shard_map/ppermute | solution.py:317
  64.8 3.7 %collective-permute-done.5 = f32[1,128]{1,0:T(1,128)S(1)} collective-permute-done((f32[1,128]{1,0:T(1,128)S(1)}, f32[1,128]{1,0:T(1,128)S(1)}, u32[]{:S(2)}, u32[]{:S(2)}) %collective-permute-start.5) | collective-permute-done | bytes 544 | tf_op jit(solution)/shard_map/ppermute | solution.py:317
  68.4 2.8 %collective-permute-done.4 = f32[1,128]{1,0:T(1,128)S(1)} collective-permute-done((f32[1,128]{1,0:T(1,128)S(1)}, f32[1,128]{1,0:T(1,128)S(1)}, u32[]{:S(2)}, u32[]{:S(2)}) %collective-permute-start.4) | collective-permute-done | bytes 544 | tf_op jit(solution)/shard_map/ppermute | solution.py:317
  71.3 0.0 collective-permute-done.6.near_ref
  71.3 0.0 collective-permute-done.7.back_ref
  71.3 0.1 gather.1
  71.4 14.1 %collective-permute-start.8 = (bf16[2,128,128]{2,1,0:T(8,128)(2,1)S(1)}, bf16[2,128,128]{2,1,0:T(8,128)(2,1)S(1)}, u32[]{:S(2)}, u32[]{:S(2)}) collective-permute-start(bf16[2,128,128]{2,1,0:T(8,128)(2,1)S(1)} %get-tuple-element.49), channel_id=1, source_target_pairs={{0,9},{1,10},{2,11},{3,12},{4,13},{5,14},{6,15},{7,16},{8,17},{9,1... | collective-permute-start | bytes 196616 | tf_op jit(solution)/shard_map/ppermute | solution.py:317
  85.5 1.9 %collective-permute-start.9 = (bf16[2,128,128]{2,1,0:T(8,128)(2,1)S(1)}, bf16[2,128,128]{2,1,0:T(8,128)(2,1)S(1)}, u32[]{:S(2)}, u32[]{:S(2)}) collective-permute-start(bf16[2,128,128]{2,1,0:T(8,128)(2,1)S(1)} %get-tuple-element.50), channel_id=1, source_target_pairs={{0,23},{1,24},{2,25},{3,26},{4,27},{5,28},{6,29},{7,30},{8,31},{9,... | collective-permute-start | bytes 196616 | tf_op jit(solution)/shard_map/ppermute | solution.py:317
  87.4 16.8 %collective-permute-start.10 = (bf16[128,128]{1,0:T(8,128)(2,1)S(1)}, bf16[128,128]{1,0:T(8,128)(2,1)S(1)}, u32[]{:S(2)}, u32[]{:S(2)}) collective-permute-start(bf16[128,128]{1,0:T(8,128)(2,1)S(1)} %get-tuple-element.51), channel_id=1, source_target_pairs={{0,18},{1,19},{2,20},{3,21},{4,22},{5,23},{6,24},{7,25},{8,26},{9,... | collective-permute-start | bytes 98312 | tf_op jit(solution)/shard_map/ppermute | solution.py:317
  104.2 4.4 %collective-permute-start.11 = (bf16[128,128]{1,0:T(8,128)(2,1)S(1)}, bf16[128,128]{1,0:T(8,128)(2,1)S(1)}, u32[]{:S(2)}, u32[]{:S(2)}) collective-permute-start(bf16[128,128]{1,0:T(8,128)(2,1)S(1)} %get-tuple-element.52), channel_id=1, source_target_pairs={{0,14},{1,15},{2,16},{3,17},{4,18},{5,19},{6,20},{7,21},{8,22},{9,... | collective-permute-start | bytes 98312 | tf_op jit(solution)/shard_map/ppermute | solution.py:317
  108.6 0.0 copy-done.2
  108.6 0.6 copy.11.tracer_ref
  109.2 0.0 copy-done
  109.2 0.0 copy-done.1
  109.2 2.0 %mix.1 = (f32[60,32,256]{2,1,0:T(8,128)S(1)}, f32[2,32,256]{2,1,0:T(8,128)S(1)}) custom-call(bf16[32,60,256]{2,1,0:T(8,128)(2,1)S(1)} %copy.11.tracer_ref, f32[31,256]{1,0:T(8,128)S(1)} %copy-done, s32[1,256]{1,0:T(1,128)S(1)} %bitcast.9), custom_call_target="tpu_custom_call" | custom-call | flops 5898240 | bytes 2949120 | tf_op jit(solution)/shard_map/mix/pallas_call | solution.py:257
  111.2 11.5 %collective-permute-done.10.far_ref = bf16[128,128]{1,0:T(8,128)(2,1)S(1)} collective-permute-done((bf16[128,128]{1,0:T(8,128)(2,1)S(1)}, bf16[128,128]{1,0:T(8,128)(2,1)S(1)}, u32[]{:S(2)}, u32[]{:S(2)}) %collective-permute-start.10) | collective-permute-done | bytes 32800 | tf_op jit(solution)/shard_map/ppermute | solution.py:317
  122.7 7.5 %collective-permute-done.11.other_ref = bf16[128,128]{1,0:T(8,128)(2,1)S(1)} collective-permute-done((bf16[128,128]{1,0:T(8,128)(2,1)S(1)}, bf16[128,128]{1,0:T(8,128)(2,1)S(1)}, u32[]{:S(2)}, u32[]{:S(2)}) %collective-permute-start.11) | collective-permute-done | bytes 32800 | tf_op jit(solution)/shard_map/ppermute | solution.py:317
  130.2 0.0 collective-permute-done.8.plus_ref
  130.2 0.0 collective-permute-done.9.minus_ref
  130.2 1.5 %finish.1 = f32[60,32,256]{2,1,0:T(8,128)} custom-call(f32[60,32,256]{2,1,0:T(8,128)S(1)} %get-tuple-element.38.state_ref, f32[2,32,256]{2,1,0:T(8,128)S(1)} %get-tuple-element.39.unit_ref, f32[2,128,128]{2,1,0:T(8,128)S(1)} %get-tuple-element.48.rest_ref, bf16[2,128,128]{2,1,0:T(8,128)(2,1)S(1)} %collective-permute-done.8.plus_ref, ...), custom_call_target="tpu_custom_call" | custom-call | tf_op jit(solution)/shard_map/finish/pallas_call | solution.py:304
  (5 shorter events, 0.0 us)
Async XLA Ops:
  6.2 102.4 %copy-start.2 = (bf16[32,60,256]{2,0,1:T(8,128)(2,1)S(1)}, bf16[32,60,256]{2,0,1:T(8,128)(2,1)}, u32[]{:S(2)}) copy-start(bf16[32,60,256]{2,0,1:T(8,128)(2,1)} %param.15) | copy-start | bytes 2949124
  6.2 25.1 %collective-permute-start = (bf16[21,128,128]{2,1,0:T(8,128)(2,1)S(1)}, bf16[21,128,128]{2,1,0:T(8,128)(2,1)S(1)}, u32[]{:S(2)}, u32[]{:S(2)}) collective-permute-start(bf16[21,128,128]{2,1,0:T(8,128)(2,1)S(1)} %get-tuple-element.30), channel_id=1, source_target_pairs={{0,1},{1,2},{2,3},{3,4},{4,5},{5,6},{6,7},{7,8},{8,9},{9,10},{10,1... | collective-permute-start | bytes 2064392 | tf_op jit(solution)/shard_map/ppermute | solution.py:317
  12.2 19.1 %collective-permute-start.1 = (bf16[21,128,128]{2,1,0:T(8,128)(2,1)S(1)}, bf16[21,128,128]{2,1,0:T(8,128)(2,1)S(1)}, u32[]{:S(2)}, u32[]{:S(2)}) collective-permute-start(bf16[21,128,128]{2,1,0:T(8,128)(2,1)S(1)} %get-tuple-element.34), channel_id=1, source_target_pairs={{0,31},{1,0},{2,1},{3,2},{4,3},{5,4},{6,5},{7,6},{8,7},{9,8},{10,9... | collective-permute-start | bytes 2064392 | tf_op jit(solution)/shard_map/ppermute | solution.py:317
  31.6 77.6 %copy-start = (f32[31,256]{1,0:T(8,128)S(1)}, f32[31,256]{1,0:T(8,128)}, u32[]{:S(2)}) copy-start(f32[31,256]{1,0:T(8,128)} %diff_ref.1) | copy-start | bytes 95236
  31.6 77.6 %copy-start.1 = (s32[256]{0:T(256)S(1)}, s32[256]{0:T(256)}, u32[]{:S(2)}) copy-start(s32[256]{0:T(256)} %param.17) | copy-start | bytes 3076
  31.6 23.8 %collective-permute-start.3 = (f32[1,128]{1,0:T(1,128)S(1)}, f32[1,128]{1,0:T(1,128)S(1)}, u32[]{:S(2)}, u32[]{:S(2)}) collective-permute-start(f32[1,128]{1,0:T(1,128)S(1)} %bitcast.11), channel_id=1, source_target_pairs={{0,31},{1,0},{2,1},{3,2},{4,3},{5,4},{6,5},{7,6},{8,7},{9,8},{10,9... | collective-permute-start | bytes 1544 | tf_op jit(solution)/shard_map/ppermute | solution.py:317
  44.5 10.9 %collective-permute-start.2 = (f32[1,128]{1,0:T(1,128)S(1)}, f32[1,128]{1,0:T(1,128)S(1)}, u32[]{:S(2)}, u32[]{:S(2)}) collective-permute-start(f32[1,128]{1,0:T(1,128)S(1)} %bitcast.12), channel_id=1, source_target_pairs={{0,1},{1,2},{2,3},{3,4},{4,5},{5,6},{6,7},{7,8},{8,9},{9,10},{10,1... | collective-permute-start | bytes 1544 | tf_op jit(solution)/shard_map/ppermute | solution.py:317
  46.4 24.9 %collective-permute-start.6 = (bf16[7,128,128]{2,1,0:T(8,128)(2,1)S(1)}, bf16[7,128,128]{2,1,0:T(8,128)(2,1)S(1)}, u32[]{:S(2)}, u32[]{:S(2)}) collective-permute-start(bf16[7,128,128]{2,1,0:T(8,128)(2,1)S(1)} %get-tuple-element.42), channel_id=1, source_target_pairs={{0,3},{1,4},{2,5},{3,6},{4,7},{5,8},{6,9},{7,10},{8,11},{9,12},{10... | collective-permute-start | bytes 688136 | tf_op jit(solution)/shard_map/ppermute | solution.py:317
  48.3 23.0 %collective-permute-start.7 = (bf16[7,128,128]{2,1,0:T(8,128)(2,1)S(1)}, bf16[7,128,128]{2,1,0:T(8,128)(2,1)S(1)}, u32[]{:S(2)}, u32[]{:S(2)}) collective-permute-start(bf16[7,128,128]{2,1,0:T(8,128)(2,1)S(1)} %get-tuple-element.43), channel_id=1, source_target_pairs={{0,29},{1,30},{2,31},{3,0},{4,1},{5,2},{6,3},{7,4},{8,5},{9,6},{10... | collective-permute-start | bytes 688136 | tf_op jit(solution)/shard_map/ppermute | solution.py:317
  55.4 13.0 %collective-permute-start.5 = (f32[1,128]{1,0:T(1,128)S(1)}, f32[1,128]{1,0:T(1,128)S(1)}, u32[]{:S(2)}, u32[]{:S(2)}) collective-permute-start(f32[1,128]{1,0:T(1,128)S(1)} %add_add_fusion.2), channel_id=1, source_target_pairs={{0,29},{1,30},{2,31},{3,0},{4,1},{5,2},{6,3},{7,4},{8,5},{9,6},{10... | collective-permute-start | bytes 1544 | tf_op jit(solution)/shard_map/ppermute | solution.py:317
  62.8 8.4 %collective-permute-start.4 = (f32[1,128]{1,0:T(1,128)S(1)}, f32[1,128]{1,0:T(1,128)S(1)}, u32[]{:S(2)}, u32[]{:S(2)}) collective-permute-start(f32[1,128]{1,0:T(1,128)S(1)} %add_add_fusion.2), channel_id=1, source_target_pairs={{0,3},{1,4},{2,5},{3,6},{4,7},{5,8},{6,9},{7,10},{8,11},{9,12},{10... | collective-permute-start | bytes 1544 | tf_op jit(solution)/shard_map/ppermute | solution.py:317
  71.4 58.8 %collective-permute-start.8 = (bf16[2,128,128]{2,1,0:T(8,128)(2,1)S(1)}, bf16[2,128,128]{2,1,0:T(8,128)(2,1)S(1)}, u32[]{:S(2)}, u32[]{:S(2)}) collective-permute-start(bf16[2,128,128]{2,1,0:T(8,128)(2,1)S(1)} %get-tuple-element.49), channel_id=1, source_target_pairs={{0,9},{1,10},{2,11},{3,12},{4,13},{5,14},{6,15},{7,16},{8,17},{9,1... | collective-permute-start | bytes 196616 | tf_op jit(solution)/shard_map/ppermute | solution.py:317
  85.5 44.7 %collective-permute-start.9 = (bf16[2,128,128]{2,1,0:T(8,128)(2,1)S(1)}, bf16[2,128,128]{2,1,0:T(8,128)(2,1)S(1)}, u32[]{:S(2)}, u32[]{:S(2)}) collective-permute-start(bf16[2,128,128]{2,1,0:T(8,128)(2,1)S(1)} %get-tuple-element.50), channel_id=1, source_target_pairs={{0,23},{1,24},{2,25},{3,26},{4,27},{5,28},{6,29},{7,30},{8,31},{9,... | collective-permute-start | bytes 196616 | tf_op jit(solution)/shard_map/ppermute | solution.py:317
  87.4 35.3 %collective-permute-start.10 = (bf16[128,128]{1,0:T(8,128)(2,1)S(1)}, bf16[128,128]{1,0:T(8,128)(2,1)S(1)}, u32[]{:S(2)}, u32[]{:S(2)}) collective-permute-start(bf16[128,128]{1,0:T(8,128)(2,1)S(1)} %get-tuple-element.51), channel_id=1, source_target_pairs={{0,18},{1,19},{2,20},{3,21},{4,22},{5,23},{6,24},{7,25},{8,26},{9,... | collective-permute-start | bytes 98312 | tf_op jit(solution)/shard_map/ppermute | solution.py:317
  104.2 26.0 %collective-permute-start.11 = (bf16[128,128]{1,0:T(8,128)(2,1)S(1)}, bf16[128,128]{1,0:T(8,128)(2,1)S(1)}, u32[]{:S(2)}, u32[]{:S(2)}) collective-permute-start(bf16[128,128]{1,0:T(8,128)(2,1)S(1)} %get-tuple-element.52), channel_id=1, source_target_pairs={{0,14},{1,15},{2,16},{3,17},{4,18},{5,19},{6,20},{7,21},{8,22},{9,... | collective-permute-start | bytes 98312 | tf_op jit(solution)/shard_map/ppermute | solution.py:317

commit v4 on v3

--- a/solution.py
+++ b/solution.py
@@ -15,13 +15,16 @@
 UNROLL = 4
 BANK_COPIES = 8
 FIELD_CHUNK = 15
-AHEAD = 13
-PLUS = 10
-MINUS = 11
+FAR_STEP = 11
+MID_STEP = 4
+AHEAD = FAR_STEP + MID_STEP + 1
+PLUS = 8
+MINUS = 9
+TWO = 6
 
 
 def remap_kernel(count_ref, me_ref, source_hbm, tile_hbm, target_hbm, flux_ref, bank_hbm,
-                 right_ref, left_ref, keep_ref, part_ref,
+                 right_ref, left_ref, ahead_ref, astern_ref, keep_ref, part_ref,
                  source_ref, tile_ref, target_ref, bank_ref, blocks, acc, list_sem, bank_sem):
     subs, fields, atm_rows = flux_ref.shape
     source_blocks = atm_rows // TILE
@@ -71,9 +74,13 @@
         for away in range(slots):
             value = acc[half * slots + away].astype(BF16)
             ocean = ocean + value.astype(F32)
-            place, digit = away // 3, away % 3
+            far, rest = divmod(away, FAR_STEP)
+            mid, digit = divmod(rest, MID_STEP)
+            place = 3 * far + mid
             if digit == 1:
                 keep_ref[half, place] = value
+            elif digit == 3:
+                (ahead_ref, astern_ref)[half][2 * far + mid] = value
             elif (digit == 2) == (half == 0):
                 right_ref[place + (0 if half == 0 else PLUS)] = value
             else:
@@ -93,10 +100,12 @@
         remap_kernel,
         out_shape=(jax.ShapeDtypeStruct((PLUS + MINUS, ROWS, TILE), BF16),
                    jax.ShapeDtypeStruct((PLUS + MINUS, ROWS, TILE), BF16),
+                   jax.ShapeDtypeStruct((TWO, ROWS, TILE), BF16),
+                   jax.ShapeDtypeStruct((TWO, ROWS, TILE), BF16),
                    jax.ShapeDtypeStruct((2, MINUS, ROWS, TILE), BF16),
                    jax.ShapeDtypeStruct((8, ROWS), F32)),
         in_specs=[smem] * 2 + [hbm] * 3 + [vmem, hbm],
-        out_specs=(vmem,) * 4,
+        out_specs=(vmem,) * 6,
         scratch_shapes=[pltpu.SMEM(pair_source.shape, jnp.int32)] * 3
         + [pltpu.VMEM(bank.shape, BF16),
            pltpu.VMEM((source_blocks, ROWS, TILE), BF16),
@@ -112,34 +121,37 @@
       pltpu.with_memory_space_constraint(bank, pltpu.HBM))
 
 
-def combine_kernel(keep_ref, right_ref, left_ref, own_ref, near_ref, back_ref):
+def combine_kernel(keep_ref, right_ref, left_ref, ahead_ref, astern_ref,
+                   own_ref, near_ref, back_ref):
     for o in range(2):
+        plus, minus = (right_ref, left_ref) if o == 0 else (left_ref, right_ref)
         for place in range(MINUS):
+            far, mid = divmod(place, 3)
             value = keep_ref[o, place].astype(F32)
-            plus, minus = (right_ref, left_ref) if o == 0 else (left_ref, right_ref)
             if place < PLUS:
                 value = value + plus[place + (0 if o == 0 else MINUS)].astype(F32)
             value = value + minus[place + (0 if o == 0 else PLUS)].astype(F32)
-            code, digit = place // 3, place % 3
-            if digit == 1:
-                own_ref[o, code] = value
-            elif (digit == 2) == (o == 0):
-                near_ref[code + (0 if o == 0 else 3)] = value.astype(BF16)
-            else:
-                back_ref[code + (0 if o == 0 else 4)] = value.astype(BF16)
-
-
-def combine(keep, right, left):
-    vmem = pl.BlockSpec(memory_space=pltpu.VMEM)
-    sent = jax.ShapeDtypeStruct((7, ROWS, TILE), BF16)
+            if mid < 2:
+                value = value + (ahead_ref, astern_ref)[o][2 * far + mid].astype(F32)
+            if mid == 1:
+                own_ref[o, far] = value
+            elif (mid == 2) == (o == 0):
+                near_ref[far + 3 * o] = value.astype(BF16)
+            else:
+                back_ref[far + 3 * o] = value.astype(BF16)
+
+
+def combine(keep, right, left, ahead, astern):
+    vmem = pl.BlockSpec(memory_space=pltpu.VMEM)
+    sent = jax.ShapeDtypeStruct((6, ROWS, TILE), BF16)
     return pl.pallas_call(
         combine_kernel,
-        out_shape=(jax.ShapeDtypeStruct((2, 4, ROWS, TILE), F32), sent, sent),
-        in_specs=[vmem] * 3,
+        out_shape=(jax.ShapeDtypeStruct((2, 3, ROWS, TILE), F32), sent, sent),
+        in_specs=[vmem] * 5,
         out_specs=(vmem,) * 3,
         compiler_params=pltpu.CompilerParams(vmem_limit_bytes=16 << 20),
         name="combine",
-    )(keep, right, left)
+    )(keep, right, left, ahead, astern)
 
 
 def with_total(chunk, total):
@@ -157,41 +169,32 @@
     return rows[place:place + 1] + rows[place + 1:place + 2] + rows[place + 2:place + 3]
 
 
-def gather_kernel(own_ref, near_ref, back_ref, window_ref, tail_ref,
-                  rest_ref, plus_ref, minus_ref, far_ref, other_ref):
+def gather_kernel(own_ref, near_ref, back_ref, total_ref, rest_ref, plus_ref, minus_ref):
     for o in range(2):
-        for code in range(4):
-            value = own_ref[o, code]
-            up, down = (near_ref, back_ref) if o == 0 else (back_ref, near_ref)
-            if code < 3:
-                value = value + up[code + (0 if o == 0 else 4)].astype(F32)
-            value = value + down[code + (0 if o == 0 else 3)].astype(F32)
-            if code == 1:
+        for far in range(3):
+            value = (own_ref[o, far] + near_ref[far + 3 * o].astype(F32)
+                     + back_ref[far + 3 * o].astype(F32))
+            if far == 1:
                 rest_ref[o] = value
-            elif code == 3 and o == 0:
-                far_ref[...] = with_total(value, tail_ref[...])
-            elif code == 3:
-                other_ref[...] = value.astype(BF16)
-            else:
-                sent = with_total(value, window_ref[...]) if o == 0 else value.astype(BF16)
-                if (code == 2) == (o == 0):
-                    plus_ref[o] = sent
-                else:
-                    minus_ref[o] = sent
-
-
-def gather(own, near, back, window, tail):
-    vmem = pl.BlockSpec(memory_space=pltpu.VMEM)
-    chunk = jax.ShapeDtypeStruct((ROWS, TILE), BF16)
+                continue
+            sent = with_total(value, total_ref[...]) if o == 0 else value.astype(BF16)
+            if (far == 2) == (o == 0):
+                plus_ref[o] = sent
+            else:
+                minus_ref[o] = sent
+
+
+def gather(own, near, back, total):
+    vmem = pl.BlockSpec(memory_space=pltpu.VMEM)
     pair = jax.ShapeDtypeStruct((2, ROWS, TILE), BF16)
     return pl.pallas_call(
         gather_kernel,
-        out_shape=(jax.ShapeDtypeStruct((2, ROWS, TILE), F32), pair, pair, chunk, chunk),
-        in_specs=[vmem] * 5,
-        out_specs=(vmem,) * 5,
+        out_shape=(jax.ShapeDtypeStruct((2, ROWS, TILE), F32), pair, pair),
+        in_specs=[vmem] * 4,
+        out_specs=(vmem,) * 3,
         compiler_params=pltpu.CompilerParams(vmem_limit_bytes=16 << 20),
         name="gather",
-    )(own, near, back, window, tail)
+    )(own, near, back, total)
 
 
 def mix_kernel(tracer_ref, diff_ref, depth_ref, solved_ref, unit_ref, state_ref, ahead, lower, upper):
@@ -268,21 +271,22 @@
     )(tracers, diffusivity, column_depth.reshape(1, columns))
 
 
-def finish_kernel(scale, state_ref, unit_ref, rest_ref, plus_ref, minus_ref, far_ref, other_ref,
+def finish_kernel(scale, ring, me_ref, state_ref, unit_ref, rest_ref, plus_ref, minus_ref,
                   total_ref, out_hbm,
                   surface, result, sems):
     fields, levels, columns = state_ref.shape
     eye = (lax.broadcasted_iota(jnp.int32, (ROWS, ROWS), 0)
            == lax.broadcasted_iota(jnp.int32, (ROWS, ROWS), 1))
-    total = (total_ref[...] + total_in(plus_ref[0]) + total_in(minus_ref[0])
-             + total_in(far_ref[...])) * scale
+    me = me_ref[0]
+    half = ring // 2
+    crossed = ((me - FAR_STEP) & (ring - 1)) // half != me // half
+    total = (total_ref[...] + jnp.where(crossed, total_in(plus_ref[0]),
+                                        total_in(minus_ref[0]))) * scale
     spread = jnp.where(eye, jnp.broadcast_to(total, (ROWS, ROWS)), 0.0)
     fix = jnp.sum(spread, axis=1, keepdims=True)
     for o in range(2):
-        last = (far_ref, other_ref)[o]
         surface[:, pl.ds(o * TILE, TILE)] = (rest_ref[o] + plus_ref[o].astype(F32)
-                                             + minus_ref[o].astype(F32)
-                                             + last[...].astype(F32)) + fix
+                                             + minus_ref[o].astype(F32)) + fix
     once = unit_ref[0]
     twice = unit_ref[1]
     copies = []
@@ -298,19 +302,19 @@
         copy.wait()
 
 
-def finish(state, unit, rest, plus, minus, far, other, total, scale):
+def finish(me, state, unit, rest, plus, minus, total, scale, ring):
     vmem = pl.BlockSpec(memory_space=pltpu.VMEM)
     fields, levels, columns = state.shape
     return pl.pallas_call(
-        functools.partial(finish_kernel, scale),
+        functools.partial(finish_kernel, scale, ring),
         out_shape=jax.ShapeDtypeStruct(state.shape, F32),
-        in_specs=[vmem] * 8,
+        in_specs=[pl.BlockSpec(memory_space=pltpu.SMEM)] + [vmem] * 6,
         out_specs=pl.BlockSpec(memory_space=pltpu.HBM),
         scratch_shapes=[pltpu.VMEM((ROWS, columns), F32), pltpu.VMEM(state.shape, F32),
                         pltpu.SemaphoreType.DMA((fields // FIELD_CHUNK,))],
         compiler_params=pltpu.CompilerParams(vmem_limit_bytes=24 << 20),
         name="finish",
-    )(state, unit, rest, plus, minus, far, other, total)
+    )(me, state, unit, rest, plus, minus, total)
 
 
 def shift(x, by, ring):
@@ -332,33 +336,30 @@
     plane = lax.axis_size("sec") * lax.axis_size("grp")
     columns = tracers.shape[2]
     me = lax.axis_index("blk").astype(jnp.int32).reshape(1)
-    right, left, keep, part = remap(pair_count, me, pair_source, pair_tile, pair_target, atm_flux,
-                                    tile_bank, ring)
+    right, left, ahead, astern, keep, part = remap(
+        pair_count, me, pair_source, pair_tile, pair_target, atm_flux, tile_bank, ring)
+    ahead = shift(ahead, 2, ring)
+    astern = shift(astern, -2, ring)
     right = shift(right, 1, ring)
     left = shift(left, -1, ring)
     gathered = lax.all_to_all(jnp.broadcast_to(part[:1], (plane, ROWS)), ("sec", "grp"), 0, 0,
                               tiled=True)
     gathered, right = lax.optimization_barrier((gathered, right))
-    own, near, back = combine(keep, right, left)
-    near = shift(near, 3, ring)
-    back = shift(back, -3, ring)
-    gathered, own = lax.optimization_barrier((gathered, own))
-    column_depth, own = lax.optimization_barrier((column_depth, own))
+    own, near, back = combine(keep, right, left, ahead, astern)
+    near = shift(near, MID_STEP, ring)
+    back = shift(back, -MID_STEP, ring)
+    gathered, column_depth, own = lax.optimization_barrier((gathered, column_depth, own))
     state, unit = mix(tracers, diffusivity, column_depth)
-    level = jnp.sum(gathered, axis=0, keepdims=True)
-    before, after = shift(level, 1, ring), shift(level, -1, ring)
-    three = level + before + after
-    behind, beyond = shift(three, 3, ring), shift(three, -3, ring)
-    window = three + behind + beyond
-    tail = level + after + beyond
-    window, tail, near, back = lax.optimization_barrier((window, tail, near, back))
-    rest, plus, minus, far, other = gather(own, near, back, window, tail)
-    far = shift(far, -14, ring)
-    other = shift(other, 14, ring)
-    plus = shift(plus, 9, ring)
-    minus = shift(minus, -9, ring)
-    result = finish(state, unit, rest, plus, minus, far, other, window,
-                    1.0 / (columns * ring * plane))
+    group = ring // 2
+    total = jnp.broadcast_to(jnp.sum(gathered, axis=0, keepdims=True), (group, ROWS))
+    total = lax.all_to_all(total, "blk", 0, 0, tiled=True,
+                           axis_index_groups=[list(range(group)), list(range(group, ring))])
+    total, near = lax.optimization_barrier((total, near))
+    total = jnp.sum(total, axis=0, keepdims=True)
+    rest, plus, minus = gather(own, near, back, total)
+    plus = shift(plus, FAR_STEP, ring)
+    minus = shift(minus, -FAR_STEP, ring)
+    result = finish(me, state, unit, rest, plus, minus, total, 1.0 / (columns * ring * plane), ring)
     return jnp.transpose(result, (1, 0, 2))
 
 

time: 132 us -> 129 us (0.977)
  the two profiles are of different devices: /device:TPU:46 before, /device:TPU:160 now
where the time goes in v4:
time: 129 us
  blocking collectives  48.9 us (38%)
  starting transfers between devices  48.5 us (38%)
  waiting for transfers between devices  19.9 us (15%)
  Pallas kernels  8.71 us (7%)
  local copies, waits for them, and re-layouts  1.77 us (1%)
    ppermute x8, starting transfers between devices, shift(): return lax.ppermute(x, 'blk', [(i, (i + by) % ring) for i in range(ring)])  48.5 us
    all_to_all x1, blocking collectives, body(): lax.all_to_all(total, 'blk', 0, 0, tiled=True, axis_index_groups=[list(ra...  33.3 us
    ppermute x8, waiting for transfers between devices, shift(): return lax.ppermute(x, 'blk', [(i, (i + by) % ring) for i in range(ring)])  19.9 us
    all_to_all x1, blocking collectives, body(): lax.all_to_all(jnp.broadcast_to(part[:1], (plane, ROWS)), ('sec', 'grp'),...  15.6 us
    pallas_call x1, Pallas kernels, remap(): pl.pallas_call(remap_kernel, out_shape=(jax.ShapeDtypeStruct((PLUS + MINU...  4.9 us
  transfers between devices with their start and end apart: 8, of which 2 were waited for; matrix products, arithmetic and copies ran while one was open for 0% of the time, Pallas kernels for 2%

profile of v4, /device:TPU:160, one launch (start us, length us, event | category | flops | bytes accessed | tf_op | source)
XLA Modules:
  0.0 128.7 jit_solution(12100389031741670408)
XLA Ops:
  0.7 1.2 copy.10.flux_ref
  1.8 4.9 %remap.1 = (bf16[17,128,128]{2,1,0:T(8,128)(2,1)S(1)}, bf16[17,128,128]{2,1,0:T(8,128)(2,1)S(1)}, bf16[6,128,128]{2,1,0:T(8,128)(2,1)S(1)}, bf16[6,128,128]{2,1,...) custom-call(s32[1]{0:T(128)S(6)} %copy.12.count_ref, s32[1]{0:T(128)} %bitcast.me_ref, ...), custom_call_target="tpu_custom_call" | custom-call | flops 536870912 | bytes 8388608 | tf_op jit(solution)/shard_map/remap/pallas_call | solution.py:99
  6.7 0.0 copy-start.2
  6.8 4.0 %collective-permute-start = (bf16[17,128,128]{2,1,0:T(8,128)(2,1)S(1)}, bf16[17,128,128]{2,1,0:T(8,128)(2,1)S(1)}, u32[]{:S(2)}, u32[]{:S(2)}) collective-permute-start(bf16[17,128,128]{2,1,0:T(8,128)(2,1)S(1)} %get-tuple-element.27), channel_id=1, source_target_pairs={{0,1},{1,2},{2,3},{3,4},{4,5},{5,6},{6,7},{7,8},{8,9},{9,10},{10,1... | collective-permute-start | bytes 1671176 | tf_op jit(solution)/shard_map/ppermute | solution.py:321
  10.7 2.0 %collective-permute-start.1 = (bf16[17,128,128]{2,1,0:T(8,128)(2,1)S(1)}, bf16[17,128,128]{2,1,0:T(8,128)(2,1)S(1)}, u32[]{:S(2)}, u32[]{:S(2)}) collective-permute-start(bf16[17,128,128]{2,1,0:T(8,128)(2,1)S(1)} %get-tuple-element.31), channel_id=1, source_target_pairs={{0,31},{1,0},{2,1},{3,2},{4,3},{5,4},{6,5},{7,6},{8,7},{9,8},{10,9... | collective-permute-start | bytes 1671176 | tf_op jit(solution)/shard_map/ppermute | solution.py:321
  12.7 7.0 %collective-permute-start.2 = (bf16[6,128,128]{2,1,0:T(8,128)(2,1)S(1)}, bf16[6,128,128]{2,1,0:T(8,128)(2,1)S(1)}, u32[]{:S(2)}, u32[]{:S(2)}) collective-permute-start(bf16[6,128,128]{2,1,0:T(8,128)(2,1)S(1)} %get-tuple-element.32), channel_id=1, source_target_pairs={{0,2},{1,3},{2,4},{3,5},{4,6},{5,7},{6,8},{7,9},{8,10},{9,11},{10,... | collective-permute-start | bytes 589832 | tf_op jit(solution)/shard_map/ppermute | solution.py:321
  19.8 1.9 %collective-permute-start.3 = (bf16[6,128,128]{2,1,0:T(8,128)(2,1)S(1)}, bf16[6,128,128]{2,1,0:T(8,128)(2,1)S(1)}, u32[]{:S(2)}, u32[]{:S(2)}) collective-permute-start(bf16[6,128,128]{2,1,0:T(8,128)(2,1)S(1)} %get-tuple-element.33), channel_id=1, source_target_pairs={{0,30},{1,31},{2,0},{3,1},{4,2},{5,3},{6,4},{7,5},{8,6},{9,7},{10,... | collective-permute-start | bytes 589832 | tf_op jit(solution)/shard_map/ppermute | solution.py:321
  21.7 15.6 %all_to_all.18 = f32[32,1,128]{2,1,0:T(1,128)S(1)} all-to-all(f32[32,1,128]{2,1,0:T(1,128)S(1)} %broadcast_in_dim.6), channel_id=1, replica_groups=mesh['sec'=2,'grp'=16,'blk'=32] {'sec','grp'}, dimensions={0} | all-to-all | bytes 32768 | tf_op jit(solution)/shard_map/all_to_all | solution.py:345
  37.3 0.0 collective-permute-done.right_ref
  37.3 0.0 collective-permute-done.2.ahead_ref
  37.3 0.0 collective-permute-done.3.astern_ref
  37.3 0.0 collective-permute-done.1.left_ref
  37.3 0.3 combine.1
  37.6 0.0 copy-start
  37.6 0.0 copy-start.1
  37.6 9.5 %collective-permute-start.4 = (bf16[6,128,128]{2,1,0:T(8,128)(2,1)S(1)}, bf16[6,128,128]{2,1,0:T(8,128)(2,1)S(1)}, u32[]{:S(2)}, u32[]{:S(2)}) collective-permute-start(bf16[6,128,128]{2,1,0:T(8,128)(2,1)S(1)} %get-tuple-element.40), channel_id=1, source_target_pairs={{0,4},{1,5},{2,6},{3,7},{4,8},{5,9},{6,10},{7,11},{8,12},{9,13},{1... | collective-permute-start | bytes 589832 | tf_op jit(solution)/shard_map/ppermute | solution.py:321
  47.1 5.7 %collective-permute-start.5 = (bf16[6,128,128]{2,1,0:T(8,128)(2,1)S(1)}, bf16[6,128,128]{2,1,0:T(8,128)(2,1)S(1)}, u32[]{:S(2)}, u32[]{:S(2)}) collective-permute-start(bf16[6,128,128]{2,1,0:T(8,128)(2,1)S(1)} %get-tuple-element.42), channel_id=1, source_target_pairs={{0,28},{1,29},{2,30},{3,31},{4,0},{5,1},{6,2},{7,3},{8,4},{9,5},{1... | collective-permute-start | bytes 589832 | tf_op jit(solution)/shard_map/ppermute | solution.py:321
  52.8 33.3 %all_to_all.19 = f32[16,1,128]{2,1,0:T(1,128)S(1)} all-to-all(f32[16,1,128]{2,1,0:T(1,128)S(1)} %broadcast_in_dim.7), channel_id=1, replica_groups={{0,1,2,3,4,5,6,7,8,9,10,11,12,13,14,15},{16,17,18,19,20,21,22,23,24,25,..., dimensions={0} | all-to-all | bytes 16384 | tf_op jit(solution)/shard_map/all_to_all | solution.py:355
  86.1 0.0 collective-permute-done.4.near_ref
  86.1 0.0 collective-permute-done.5.back_ref
  86.1 0.1 gather.1
  86.2 11.1 %collective-permute-start.6 = (bf16[2,128,128]{2,1,0:T(8,128)(2,1)S(1)}, bf16[2,128,128]{2,1,0:T(8,128)(2,1)S(1)}, u32[]{:S(2)}, u32[]{:S(2)}) collective-permute-start(bf16[2,128,128]{2,1,0:T(8,128)(2,1)S(1)} %get-tuple-element.45), channel_id=1, source_target_pairs={{0,11},{1,12},{2,13},{3,14},{4,15},{5,16},{6,17},{7,18},{8,19},{9,... | collective-permute-start | bytes 196616 | tf_op jit(solution)/shard_map/ppermute | solution.py:321
  97.3 7.4 %collective-permute-start.7 = (bf16[2,128,128]{2,1,0:T(8,128)(2,1)S(1)}, bf16[2,128,128]{2,1,0:T(8,128)(2,1)S(1)}, u32[]{:S(2)}, u32[]{:S(2)}) collective-permute-start(bf16[2,128,128]{2,1,0:T(8,128)(2,1)S(1)} %get-tuple-element.46), channel_id=1, source_target_pairs={{0,21},{1,22},{2,23},{3,24},{4,25},{5,26},{6,27},{7,28},{8,29},{9,... | collective-permute-start | bytes 196616 | tf_op jit(solution)/shard_map/ppermute | solution.py:321
  104.7 0.0 copy-done.2
  104.7 0.6 copy.11.tracer_ref
  105.3 0.0 copy-done
  105.3 0.0 copy-done.1
  105.3 2.0 %mix.1 = (f32[60,32,256]{2,1,0:T(8,128)S(1)}, f32[2,32,256]{2,1,0:T(8,128)S(1)}) custom-call(bf16[32,60,256]{2,1,0:T(8,128)(2,1)S(1)} %copy.11.tracer_ref, f32[31,256]{1,0:T(8,128)S(1)} %copy-done, s32[1,256]{1,0:T(1,128)S(1)} %bitcast.10), custom_call_target="tpu_custom_call" | custom-call | flops 5898240 | bytes 2949120 | tf_op jit(solution)/shard_map/mix/pallas_call | solution.py:260
  107.3 1.2 collective-permute-done.6.plus_ref
  108.5 18.7 %collective-permute-done.7.minus_ref = bf16[2,128,128]{2,1,0:T(8,128)(2,1)S(1)} collective-permute-done((bf16[2,128,128]{2,1,0:T(8,128)(2,1)S(1)}, bf16[2,128,128]{2,1,0:T(8,128)(2,1)S(1)}, u32[]{:S(2)}, u32[]{:S(2)}) %collective-permute-start.7) | collective-permute-done | bytes 65568 | tf_op jit(solution)/shard_map/ppermute | solution.py:321
  127.2 1.5 %finish.1 = f32[60,32,256]{2,1,0:T(8,128)} custom-call(s32[1]{0:T(128)} %bitcast.me_ref, f32[60,32,256]{2,1,0:T(8,128)S(1)} %get-tuple-element.36.state_ref, f32[2,32,256]{2,1,0:T(8,128)S(1)} %get-tuple-element.37.unit_ref, f32[2,128,128]{2,1,0:T(8,128)S(1)} %get-tuple-element.44.rest_ref, bf16[2,128,128]{2,1,0:T(8,128)(2,1)S(1)} %collective-permute-done.6.plus_ref, ...), custom_call_target="tpu_custom_call" | custom-call | tf_op jit(solution)/shard_map/finish/pallas_call | solution.py:308
  (5 shorter events, 0.1 us)
Async XLA Ops:
  6.7 97.9 %copy-start.2 = (bf16[32,60,256]{2,0,1:T(8,128)(2,1)S(1)}, bf16[32,60,256]{2,0,1:T(8,128)(2,1)}, u32[]{:S(2)}) copy-start(bf16[32,60,256]{2,0,1:T(8,128)(2,1)} %param.15) | copy-start | bytes 2949124
  6.8 30.5 %collective-permute-start = (bf16[17,128,128]{2,1,0:T(8,128)(2,1)S(1)}, bf16[17,128,128]{2,1,0:T(8,128)(2,1)S(1)}, u32[]{:S(2)}, u32[]{:S(2)}) collective-permute-start(bf16[17,128,128]{2,1,0:T(8,128)(2,1)S(1)} %get-tuple-element.27), channel_id=1, source_target_pairs={{0,1},{1,2},{2,3},{3,4},{4,5},{5,6},{6,7},{7,8},{8,9},{9,10},{10,1... | collective-permute-start | bytes 1671176 | tf_op jit(solution)/shard_map/ppermute | solution.py:321
  10.7 26.6 %collective-permute-start.1 = (bf16[17,128,128]{2,1,0:T(8,128)(2,1)S(1)}, bf16[17,128,128]{2,1,0:T(8,128)(2,1)S(1)}, u32[]{:S(2)}, u32[]{:S(2)}) collective-permute-start(bf16[17,128,128]{2,1,0:T(8,128)(2,1)S(1)} %get-tuple-element.31), channel_id=1, source_target_pairs={{0,31},{1,0},{2,1},{3,2},{4,3},{5,4},{6,5},{7,6},{8,7},{9,8},{10,9... | collective-permute-start | bytes 1671176 | tf_op jit(solution)/shard_map/ppermute | solution.py:321
  12.7 24.6 %collective-permute-start.2 = (bf16[6,128,128]{2,1,0:T(8,128)(2,1)S(1)}, bf16[6,128,128]{2,1,0:T(8,128)(2,1)S(1)}, u32[]{:S(2)}, u32[]{:S(2)}) collective-permute-start(bf16[6,128,128]{2,1,0:T(8,128)(2,1)S(1)} %get-tuple-element.32), channel_id=1, source_target_pairs={{0,2},{1,3},{2,4},{3,5},{4,6},{5,7},{6,8},{7,9},{8,10},{9,11},{10,... | collective-permute-start | bytes 589832 | tf_op jit(solution)/shard_map/ppermute | solution.py:321
  19.8 17.5 %collective-permute-start.3 = (bf16[6,128,128]{2,1,0:T(8,128)(2,1)S(1)}, bf16[6,128,128]{2,1,0:T(8,128)(2,1)S(1)}, u32[]{:S(2)}, u32[]{:S(2)}) collective-permute-start(bf16[6,128,128]{2,1,0:T(8,128)(2,1)S(1)} %get-tuple-element.33), channel_id=1, source_target_pairs={{0,30},{1,31},{2,0},{3,1},{4,2},{5,3},{6,4},{7,5},{8,6},{9,7},{10,... | collective-permute-start | bytes 589832 | tf_op jit(solution)/shard_map/ppermute | solution.py:321
  37.6 67.7 %copy-start = (f32[31,256]{1,0:T(8,128)S(1)}, f32[31,256]{1,0:T(8,128)}, u32[]{:S(2)}) copy-start(f32[31,256]{1,0:T(8,128)} %diff_ref.1) | copy-start | bytes 95236
  37.6 67.7 %copy-start.1 = (s32[256]{0:T(256)S(1)}, s32[256]{0:T(256)}, u32[]{:S(2)}) copy-start(s32[256]{0:T(256)} %param.17) | copy-start | bytes 3076
  37.6 48.5 %collective-permute-start.4 = (bf16[6,128,128]{2,1,0:T(8,128)(2,1)S(1)}, bf16[6,128,128]{2,1,0:T(8,128)(2,1)S(1)}, u32[]{:S(2)}, u32[]{:S(2)}) collective-permute-start(bf16[6,128,128]{2,1,0:T(8,128)(2,1)S(1)} %get-tuple-element.40), channel_id=1, source_target_pairs={{0,4},{1,5},{2,6},{3,7},{4,8},{5,9},{6,10},{7,11},{8,12},{9,13},{1... | collective-permute-start | bytes 589832 | tf_op jit(solution)/shard_map/ppermute | solution.py:321
  47.1 39.0 %collective-permute-start.5 = (bf16[6,128,128]{2,1,0:T(8,128)(2,1)S(1)}, bf16[6,128,128]{2,1,0:T(8,128)(2,1)S(1)}, u32[]{:S(2)}, u32[]{:S(2)}) collective-permute-start(bf16[6,128,128]{2,1,0:T(8,128)(2,1)S(1)} %get-tuple-element.42), channel_id=1, source_target_pairs={{0,28},{1,29},{2,30},{3,31},{4,0},{5,1},{6,2},{7,3},{8,4},{9,5},{1... | collective-permute-start | bytes 589832 | tf_op jit(solution)/shard_map/ppermute | solution.py:321
  86.2 22.3 %collective-permute-start.6 = (bf16[2,128,128]{2,1,0:T(8,128)(2,1)S(1)}, bf16[2,128,128]{2,1,0:T(8,128)(2,1)S(1)}, u32[]{:S(2)}, u32[]{:S(2)}) collective-permute-start(bf16[2,128,128]{2,1,0:T(8,128)(2,1)S(1)} %get-tuple-element.45), channel_id=1, source_target_pairs={{0,11},{1,12},{2,13},{3,14},{4,15},{5,16},{6,17},{7,18},{8,19},{9,... | collective-permute-start | bytes 196616 | tf_op jit(solution)/shard_map/ppermute | solution.py:321
  97.3 29.9 %collective-permute-start.7 = (bf16[2,128,128]{2,1,0:T(8,128)(2,1)S(1)}, bf16[2,128,128]{2,1,0:T(8,128)(2,1)S(1)}, u32[]{:S(2)}, u32[]{:S(2)}) collective-permute-start(bf16[2,128,128]{2,1,0:T(8,128)(2,1)S(1)} %get-tuple-element.46), channel_id=1, source_target_pairs={{0,21},{1,22},{2,23},{3,24},{4,25},{5,26},{6,27},{7,28},{8,29},{9,... | collective-permute-start | bytes 196616 | tf_op jit(solution)/shard_map/ppermute | solution.py:321

commit v5 on v4

--- a/solution.py
+++ b/solution.py
@@ -9,10 +9,10 @@
 
 F32 = jnp.float32
 BF16 = jnp.bfloat16
-HALF = 64
-ROWS = 128
+ROWS = 120
+FINAL_ROWS = 128
 TILE = 128
-UNROLL = 4
+UNROLL = 8
 BANK_COPIES = 8
 FIELD_CHUNK = 15
 FAR_STEP = 11
@@ -41,7 +41,7 @@
     atm = jnp.zeros((ROWS, TILE), F32)
     for s in range(source_blocks):
         for sub in range(subs):
-            blocks[s, pl.ds(sub * HALF, fields)] = flux_ref[sub, :, pl.ds(s * TILE, TILE)]
+            blocks[s, pl.ds(sub * fields, fields)] = flux_ref[sub, :, pl.ds(s * TILE, TILE)]
         atm = atm + blocks[s].astype(F32)
     acc[...] = jnp.zeros(acc.shape, F32)
     count = count_ref[0]
@@ -86,7 +86,7 @@
             else:
                 left_ref[place + (0 if half == 0 else MINUS)] = value
     share = 2.0 * TILE / atm_rows
-    part = atm * share - ocean
+    part = jnp.concatenate([atm * share - ocean, jnp.zeros((TILE - ROWS, TILE), F32)], axis=0)
     part_ref[...] = lax.dot_general(jnp.ones((8, TILE), F32), part, (((1,), (1,)), ((), ())),
                                     precision=lax.Precision.HIGHEST, preferred_element_type=F32)
 
@@ -103,7 +103,7 @@
                    jax.ShapeDtypeStruct((TWO, ROWS, TILE), BF16),
                    jax.ShapeDtypeStruct((TWO, ROWS, TILE), BF16),
                    jax.ShapeDtypeStruct((2, MINUS, ROWS, TILE), BF16),
-                   jax.ShapeDtypeStruct((8, ROWS), F32)),
+                   jax.ShapeDtypeStruct((8, TILE), F32)),
         in_specs=[smem] * 2 + [hbm] * 3 + [vmem, hbm],
         out_specs=(vmem,) * 6,
         scratch_shapes=[pltpu.SMEM(pair_source.shape, jnp.int32)] * 3
@@ -155,18 +155,18 @@
 
 
 def with_total(chunk, total):
-    row = lax.broadcasted_iota(jnp.int32, chunk.shape, 0)
+    row = lax.broadcasted_iota(jnp.int32, (FINAL_ROWS - ROWS, TILE), 0)
+    tail = jnp.zeros((FINAL_ROWS - ROWS, TILE), F32)
     for i in range(3):
         piece = total.astype(BF16).astype(F32)
-        chunk = jnp.where(row == HALF - 4 + i, piece, chunk)
+        tail = jnp.where(row == i, piece, tail)
         total = total - piece
-    return chunk.astype(BF16)
+    return jnp.concatenate([chunk, tail], axis=0).astype(BF16)
 
 
 def total_in(chunk):
     rows = chunk.astype(F32)
-    place = HALF - 4
-    return rows[place:place + 1] + rows[place + 1:place + 2] + rows[place + 2:place + 3]
+    return rows[ROWS:ROWS + 1] + rows[ROWS + 1:ROWS + 2] + rows[ROWS + 2:ROWS + 3]
 
 
 def gather_kernel(own_ref, near_ref, back_ref, total_ref, rest_ref, plus_ref, minus_ref):
@@ -177,7 +177,7 @@
             if far == 1:
                 rest_ref[o] = value
                 continue
-            sent = with_total(value, total_ref[...]) if o == 0 else value.astype(BF16)
+            sent = with_total(value, total_ref[...])
             if (far == 2) == (o == 0):
                 plus_ref[o] = sent
             else:
@@ -186,7 +186,7 @@
 
 def gather(own, near, back, total):
     vmem = pl.BlockSpec(memory_space=pltpu.VMEM)
-    pair = jax.ShapeDtypeStruct((2, ROWS, TILE), BF16)
+    pair = jax.ShapeDtypeStruct((2, FINAL_ROWS, TILE), BF16)
     return pl.pallas_call(
         gather_kernel,
         out_shape=(jax.ShapeDtypeStruct((2, ROWS, TILE), F32), pair, pair),
@@ -275,25 +275,25 @@
                   total_ref, out_hbm,
                   surface, result, sems):
     fields, levels, columns = state_ref.shape
-    eye = (lax.broadcasted_iota(jnp.int32, (ROWS, ROWS), 0)
-           == lax.broadcasted_iota(jnp.int32, (ROWS, ROWS), 1))
+    eye = (lax.broadcasted_iota(jnp.int32, (ROWS, TILE), 0)
+           == lax.broadcasted_iota(jnp.int32, (ROWS, TILE), 1))
     me = me_ref[0]
     half = ring // 2
     crossed = ((me - FAR_STEP) & (ring - 1)) // half != me // half
     total = (total_ref[...] + jnp.where(crossed, total_in(plus_ref[0]),
                                         total_in(minus_ref[0]))) * scale
-    spread = jnp.where(eye, jnp.broadcast_to(total, (ROWS, ROWS)), 0.0)
+    spread = jnp.where(eye, jnp.broadcast_to(total, (ROWS, TILE)), 0.0)
     fix = jnp.sum(spread, axis=1, keepdims=True)
     for o in range(2):
-        surface[:, pl.ds(o * TILE, TILE)] = (rest_ref[o] + plus_ref[o].astype(F32)
-                                             + minus_ref[o].astype(F32)) + fix
+        surface[:, pl.ds(o * TILE, TILE)] = (rest_ref[o] + plus_ref[o].astype(F32)[:ROWS]
+                                             + minus_ref[o].astype(F32)[:ROWS]) + fix
     once = unit_ref[0]
     twice = unit_ref[1]
     copies = []
     for start in range(0, fields, FIELD_CHUNK):
         for f in range(start, start + FIELD_CHUNK):
             result[f] = (state_ref[f] + surface[pl.ds(f, 1), :] * twice
-                         + surface[pl.ds(HALF + f, 1), :] * once)
+                         + surface[pl.ds(fields + f, 1), :] * once)
         part = pl.ds(start, FIELD_CHUNK)
         copies.append(pltpu.make_async_copy(result.at[part], out_hbm.at[part],
                                             sems.at[start // FIELD_CHUNK]))
@@ -342,7 +342,7 @@
     astern = shift(astern, -2, ring)
     right = shift(right, 1, ring)
     left = shift(left, -1, ring)
-    gathered = lax.all_to_all(jnp.broadcast_to(part[:1], (plane, ROWS)), ("sec", "grp"), 0, 0,
+    gathered = lax.all_to_all(jnp.broadcast_to(part[:1], (plane, TILE)), ("sec", "grp"), 0, 0,
                               tiled=True)
     gathered, right = lax.optimization_barrier((gathered, right))
     own, near, back = combine(keep, right, left, ahead, astern)
@@ -351,7 +351,7 @@
     gathered, column_depth, own = lax.optimization_barrier((gathered, column_depth, own))
     state, unit = mix(tracers, diffusivity, column_depth)
     group = ring // 2
-    total = jnp.broadcast_to(jnp.sum(gathered, axis=0, keepdims=True), (group, ROWS))
+    total = jnp.broadcast_to(jnp.sum(gathered, axis=0, keepdims=True), (group, TILE))
     total = lax.all_to_all(total, "blk", 0, 0, tiled=True,
                            axis_index_groups=[list(range(group)), list(range(group, ring))])
     total, near = lax.optimization_barrier((total, near))

time: 129 us -> 127 us (0.984)
  the two profiles are of different devices: /device:TPU:160 before, /device:TPU:161 now
where the time goes in v5:
time: 127 us; the launch traced here: 126 us
  blocking collectives  46.9 us (37%)
  starting transfers between devices  44.9 us (35%)
  waiting for transfers between devices  22.3 us (18%)
  Pallas kernels  9.53 us (8%)
  local copies, waits for them, and re-layouts  1.77 us (1%)
    ppermute x8, starting transfers between devices, shift(): return lax.ppermute(x, 'blk', [(i, (i + by) % ring) for i in range(ring)])  44.9 us
    all_to_all x1, blocking collectives, body(): lax.all_to_all(total, 'blk', 0, 0, tiled=True, axis_index_groups=[list(ra...  31.8 us
    ppermute x8, waiting for transfers between devices, shift(): return lax.ppermute(x, 'blk', [(i, (i + by) % ring) for i in range(ring)])  22.3 us
    all_to_all x1, blocking collectives, body(): lax.all_to_all(jnp.broadcast_to(part[:1], (plane, TILE)), ('sec', 'grp'),...  15.2 us
    pallas_call x1, Pallas kernels, remap(): pl.pallas_call(remap_kernel, out_shape=(jax.ShapeDtypeStruct((PLUS + MINU...  5.69 us
  transfers between devices with their start and end apart: 8, of which 2 were waited for; matrix products, arithmetic and copies ran while one was open for 0% of the time, Pallas kernels for 2%

profile of v5, /device:TPU:161, one launch (start us, length us, event | category | flops | bytes accessed | tf_op | source)
XLA Modules:
  0.0 126.3 jit_solution(11050770008982223873)
XLA Ops:
  0.7 1.2 copy.10.flux_ref
  1.8 5.7 %remap.1 = (bf16[17,120,128]{2,1,0:T(8,128)(2,1)S(1)}, bf16[17,120,128]{2,1,0:T(8,128)(2,1)S(1)}, bf16[6,120,128]{2,1,0:T(8,128)(2,1)S(1)}, bf16[6,120,128]{2,1,...) custom-call(s32[1]{0:T(128)S(6)} %copy.12.count_ref, s32[1]{0:T(128)} %bitcast.me_ref, ...), custom_call_target="tpu_custom_call" | custom-call | flops 536870912 | bytes 8388608 | tf_op jit(solution)/shard_map/remap/pallas_call | solution.py:99
  7.5 0.0 copy-start.2
  7.5 2.1 %collective-permute-start = (bf16[17,120,128]{2,1,0:T(8,128)(2,1)S(1)}, bf16[17,120,128]{2,1,0:T(8,128)(2,1)S(1)}, u32[]{:S(2)}, u32[]{:S(2)}) collective-permute-start(bf16[17,120,128]{2,1,0:T(8,128)(2,1)S(1)} %get-tuple-element.27), channel_id=1, source_target_pairs={{0,1},{1,2},{2,3},{3,4},{4,5},{5,6},{6,7},{7,8},{8,9},{9,10},{10,1... | collective-permute-start | bytes 1566728 | tf_op jit(solution)/shard_map/ppermute | solution.py:321
  9.6 3.4 %collective-permute-start.1 = (bf16[17,120,128]{2,1,0:T(8,128)(2,1)S(1)}, bf16[17,120,128]{2,1,0:T(8,128)(2,1)S(1)}, u32[]{:S(2)}, u32[]{:S(2)}) collective-permute-start(bf16[17,120,128]{2,1,0:T(8,128)(2,1)S(1)} %get-tuple-element.31), channel_id=1, source_target_pairs={{0,31},{1,0},{2,1},{3,2},{4,3},{5,4},{6,5},{7,6},{8,7},{9,8},{10,9... | collective-permute-start | bytes 1566728 | tf_op jit(solution)/shard_map/ppermute | solution.py:321
  13.0 4.7 %collective-permute-start.2 = (bf16[6,120,128]{2,1,0:T(8,128)(2,1)S(1)}, bf16[6,120,128]{2,1,0:T(8,128)(2,1)S(1)}, u32[]{:S(2)}, u32[]{:S(2)}) collective-permute-start(bf16[6,120,128]{2,1,0:T(8,128)(2,1)S(1)} %get-tuple-element.32), channel_id=1, source_target_pairs={{0,2},{1,3},{2,4},{3,5},{4,6},{5,7},{6,8},{7,9},{8,10},{9,11},{10,... | collective-permute-start | bytes 552968 | tf_op jit(solution)/shard_map/ppermute | solution.py:321
  17.7 2.7 %collective-permute-start.3 = (bf16[6,120,128]{2,1,0:T(8,128)(2,1)S(1)}, bf16[6,120,128]{2,1,0:T(8,128)(2,1)S(1)}, u32[]{:S(2)}, u32[]{:S(2)}) collective-permute-start(bf16[6,120,128]{2,1,0:T(8,128)(2,1)S(1)} %get-tuple-element.33), channel_id=1, source_target_pairs={{0,30},{1,31},{2,0},{3,1},{4,2},{5,3},{6,4},{7,5},{8,6},{9,7},{10,... | collective-permute-start | bytes 552968 | tf_op jit(solution)/shard_map/ppermute | solution.py:321
  20.4 15.2 %all_to_all.18 = f32[32,1,128]{2,1,0:T(1,128)S(1)} all-to-all(f32[32,1,128]{2,1,0:T(1,128)S(1)} %broadcast_in_dim.6), channel_id=1, replica_groups=mesh['sec'=2,'grp'=16,'blk'=32] {'sec','grp'}, dimensions={0} | all-to-all | bytes 32768 | tf_op jit(solution)/shard_map/all_to_all | solution.py:345
  35.6 0.0 collective-permute-done.right_ref
  35.6 0.0 collective-permute-done.2.ahead_ref
  35.6 0.0 collective-permute-done.3.astern_ref
  35.6 0.0 collective-permute-done.1.left_ref
  35.6 0.0 copy-start
  35.6 0.0 copy-start.1
  35.6 0.3 combine.1
  35.9 9.8 %collective-permute-start.4 = (bf16[6,120,128]{2,1,0:T(8,128)(2,1)S(1)}, bf16[6,120,128]{2,1,0:T(8,128)(2,1)S(1)}, u32[]{:S(2)}, u32[]{:S(2)}) collective-permute-start(bf16[6,120,128]{2,1,0:T(8,128)(2,1)S(1)} %get-tuple-element.40), channel_id=1, source_target_pairs={{0,4},{1,5},{2,6},{3,7},{4,8},{5,9},{6,10},{7,11},{8,12},{9,13},{1... | collective-permute-start | bytes 552968 | tf_op jit(solution)/shard_map/ppermute | solution.py:321
  45.7 4.4 %collective-permute-start.5 = (bf16[6,120,128]{2,1,0:T(8,128)(2,1)S(1)}, bf16[6,120,128]{2,1,0:T(8,128)(2,1)S(1)}, u32[]{:S(2)}, u32[]{:S(2)}) collective-permute-start(bf16[6,120,128]{2,1,0:T(8,128)(2,1)S(1)} %get-tuple-element.42), channel_id=1, source_target_pairs={{0,28},{1,29},{2,30},{3,31},{4,0},{5,1},{6,2},{7,3},{8,4},{9,5},{1... | collective-permute-start | bytes 552968 | tf_op jit(solution)/shard_map/ppermute | solution.py:321
  50.1 31.8 %all_to_all.19 = f32[16,1,128]{2,1,0:T(1,128)S(1)} all-to-all(f32[16,1,128]{2,1,0:T(1,128)S(1)} %broadcast_in_dim.7), channel_id=1, replica_groups={{0,1,2,3,4,5,6,7,8,9,10,11,12,13,14,15},{16,17,18,19,20,21,22,23,24,25,..., dimensions={0} | all-to-all | bytes 16384 | tf_op jit(solution)/shard_map/all_to_all | solution.py:355
  81.9 0.0 collective-permute-done.4.near_ref
  81.9 0.0 collective-permute-done.5.back_ref
  81.9 0.1 gather.1
  82.0 10.7 %collective-permute-start.6 = (bf16[2,128,128]{2,1,0:T(8,128)(2,1)S(1)}, bf16[2,128,128]{2,1,0:T(8,128)(2,1)S(1)}, u32[]{:S(2)}, u32[]{:S(2)}) collective-permute-start(bf16[2,128,128]{2,1,0:T(8,128)(2,1)S(1)} %get-tuple-element.45), channel_id=1, source_target_pairs={{0,11},{1,12},{2,13},{3,14},{4,15},{5,16},{6,17},{7,18},{8,19},{9,... | collective-permute-start | bytes 196616 | tf_op jit(solution)/shard_map/ppermute | solution.py:321
  92.8 7.2 %collective-permute-start.7 = (bf16[2,128,128]{2,1,0:T(8,128)(2,1)S(1)}, bf16[2,128,128]{2,1,0:T(8,128)(2,1)S(1)}, u32[]{:S(2)}, u32[]{:S(2)}) collective-permute-start(bf16[2,128,128]{2,1,0:T(8,128)(2,1)S(1)} %get-tuple-element.46), channel_id=1, source_target_pairs={{0,21},{1,22},{2,23},{3,24},{4,25},{5,26},{6,27},{7,28},{8,29},{9,... | collective-permute-start | bytes 196616 | tf_op jit(solution)/shard_map/ppermute | solution.py:321
  99.9 0.0 copy-done.2
  100.0 0.5 copy.11.tracer_ref
  100.5 0.0 copy-done
  100.5 0.0 copy-done.1
  100.5 2.0 %mix.1 = (f32[60,32,256]{2,1,0:T(8,128)S(1)}, f32[2,32,256]{2,1,0:T(8,128)S(1)}) custom-call(bf16[32,60,256]{2,1,0:T(8,128)(2,1)S(1)} %copy.11.tracer_ref, f32[31,256]{1,0:T(8,128)S(1)} %copy-done, s32[1,256]{1,0:T(1,128)S(1)} %bitcast.10), custom_call_target="tpu_custom_call" | custom-call | flops 5898240 | bytes 2949120 | tf_op jit(solution)/shard_map/mix/pallas_call | solution.py:260
  102.6 3.8 %collective-permute-done.6.plus_ref = bf16[2,128,128]{2,1,0:T(8,128)(2,1)S(1)} collective-permute-done((bf16[2,128,128]{2,1,0:T(8,128)(2,1)S(1)}, bf16[2,128,128]{2,1,0:T(8,128)(2,1)S(1)}, u32[]{:S(2)}, u32[]{:S(2)}) %collective-permute-start.6) | collective-permute-done | bytes 65568 | tf_op jit(solution)/shard_map/ppermute | solution.py:321
  106.3 18.5 %collective-permute-done.7.minus_ref = bf16[2,128,128]{2,1,0:T(8,128)(2,1)S(1)} collective-permute-done((bf16[2,128,128]{2,1,0:T(8,128)(2,1)S(1)}, bf16[2,128,128]{2,1,0:T(8,128)(2,1)S(1)}, u32[]{:S(2)}, u32[]{:S(2)}) %collective-permute-start.7) | collective-permute-done | bytes 65568 | tf_op jit(solution)/shard_map/ppermute | solution.py:321
  124.8 1.5 %finish.1 = f32[60,32,256]{2,1,0:T(8,128)} custom-call(s32[1]{0:T(128)} %bitcast.me_ref, f32[60,32,256]{2,1,0:T(8,128)S(1)} %get-tuple-element.36.state_ref, f32[2,32,256]{2,1,0:T(8,128)S(1)} %get-tuple-element.37.unit_ref, f32[2,120,128]{2,1,0:T(8,128)S(1)} %get-tuple-element.44.rest_ref, bf16[2,128,128]{2,1,0:T(8,128)(2,1)S(1)} %collective-permute-done.6.plus_ref, ...), custom_call_target="tpu_custom_call" | custom-call | tf_op jit(solution)/shard_map/finish/pallas_call | solution.py:308
  (5 shorter events, 0.1 us)
Async XLA Ops:
  7.5 92.4 %copy-start.2 = (bf16[32,60,256]{2,0,1:T(8,128)(2,1)S(1)}, bf16[32,60,256]{2,0,1:T(8,128)(2,1)}, u32[]{:S(2)}) copy-start(bf16[32,60,256]{2,0,1:T(8,128)(2,1)} %param.15) | copy-start | bytes 2949124
  7.5 28.0 %collective-permute-start = (bf16[17,120,128]{2,1,0:T(8,128)(2,1)S(1)}, bf16[17,120,128]{2,1,0:T(8,128)(2,1)S(1)}, u32[]{:S(2)}, u32[]{:S(2)}) collective-permute-start(bf16[17,120,128]{2,1,0:T(8,128)(2,1)S(1)} %get-tuple-element.27), channel_id=1, source_target_pairs={{0,1},{1,2},{2,3},{3,4},{4,5},{5,6},{6,7},{7,8},{8,9},{9,10},{10,1... | collective-permute-start | bytes 1566728 | tf_op jit(solution)/shard_map/ppermute | solution.py:321
  9.6 26.0 %collective-permute-start.1 = (bf16[17,120,128]{2,1,0:T(8,128)(2,1)S(1)}, bf16[17,120,128]{2,1,0:T(8,128)(2,1)S(1)}, u32[]{:S(2)}, u32[]{:S(2)}) collective-permute-start(bf16[17,120,128]{2,1,0:T(8,128)(2,1)S(1)} %get-tuple-element.31), channel_id=1, source_target_pairs={{0,31},{1,0},{2,1},{3,2},{4,3},{5,4},{6,5},{7,6},{8,7},{9,8},{10,9... | collective-permute-start | bytes 1566728 | tf_op jit(solution)/shard_map/ppermute | solution.py:321
  13.0 22.6 %collective-permute-start.2 = (bf16[6,120,128]{2,1,0:T(8,128)(2,1)S(1)}, bf16[6,120,128]{2,1,0:T(8,128)(2,1)S(1)}, u32[]{:S(2)}, u32[]{:S(2)}) collective-permute-start(bf16[6,120,128]{2,1,0:T(8,128)(2,1)S(1)} %get-tuple-element.32), channel_id=1, source_target_pairs={{0,2},{1,3},{2,4},{3,5},{4,6},{5,7},{6,8},{7,9},{8,10},{9,11},{10,... | collective-permute-start | bytes 552968 | tf_op jit(solution)/shard_map/ppermute | solution.py:321
  17.7 17.9 %collective-permute-start.3 = (bf16[6,120,128]{2,1,0:T(8,128)(2,1)S(1)}, bf16[6,120,128]{2,1,0:T(8,128)(2,1)S(1)}, u32[]{:S(2)}, u32[]{:S(2)}) collective-permute-start(bf16[6,120,128]{2,1,0:T(8,128)(2,1)S(1)} %get-tuple-element.33), channel_id=1, source_target_pairs={{0,30},{1,31},{2,0},{3,1},{4,2},{5,3},{6,4},{7,5},{8,6},{9,7},{10,... | collective-permute-start | bytes 552968 | tf_op jit(solution)/shard_map/ppermute | solution.py:321
  35.6 64.9 %copy-start = (f32[31,256]{1,0:T(8,128)S(1)}, f32[31,256]{1,0:T(8,128)}, u32[]{:S(2)}) copy-start(f32[31,256]{1,0:T(8,128)} %diff_ref.1) | copy-start | bytes 95236
  35.6 64.9 %copy-start.1 = (s32[256]{0:T(256)S(1)}, s32[256]{0:T(256)}, u32[]{:S(2)}) copy-start(s32[256]{0:T(256)} %param.17) | copy-start | bytes 3076
  35.9 46.0 %collective-permute-start.4 = (bf16[6,120,128]{2,1,0:T(8,128)(2,1)S(1)}, bf16[6,120,128]{2,1,0:T(8,128)(2,1)S(1)}, u32[]{:S(2)}, u32[]{:S(2)}) collective-permute-start(bf16[6,120,128]{2,1,0:T(8,128)(2,1)S(1)} %get-tuple-element.40), channel_id=1, source_target_pairs={{0,4},{1,5},{2,6},{3,7},{4,8},{5,9},{6,10},{7,11},{8,12},{9,13},{1... | collective-permute-start | bytes 552968 | tf_op jit(solution)/shard_map/ppermute | solution.py:321
  45.7 36.3 %collective-permute-start.5 = (bf16[6,120,128]{2,1,0:T(8,128)(2,1)S(1)}, bf16[6,120,128]{2,1,0:T(8,128)(2,1)S(1)}, u32[]{:S(2)}, u32[]{:S(2)}) collective-permute-start(bf16[6,120,128]{2,1,0:T(8,128)(2,1)S(1)} %get-tuple-element.42), channel_id=1, source_target_pairs={{0,28},{1,29},{2,30},{3,31},{4,0},{5,1},{6,2},{7,3},{8,4},{9,5},{1... | collective-permute-start | bytes 552968 | tf_op jit(solution)/shard_map/ppermute | solution.py:321
  82.0 24.3 %collective-permute-start.6 = (bf16[2,128,128]{2,1,0:T(8,128)(2,1)S(1)}, bf16[2,128,128]{2,1,0:T(8,128)(2,1)S(1)}, u32[]{:S(2)}, u32[]{:S(2)}) collective-permute-start(bf16[2,128,128]{2,1,0:T(8,128)(2,1)S(1)} %get-tuple-element.45), channel_id=1, source_target_pairs={{0,11},{1,12},{2,13},{3,14},{4,15},{5,16},{6,17},{7,18},{8,19},{9,... | collective-permute-start | bytes 196616 | tf_op jit(solution)/shard_map/ppermute | solution.py:321
  92.8 32.0 %collective-permute-start.7 = (bf16[2,128,128]{2,1,0:T(8,128)(2,1)S(1)}, bf16[2,128,128]{2,1,0:T(8,128)(2,1)S(1)}, u32[]{:S(2)}, u32[]{:S(2)}) collective-permute-start(bf16[2,128,128]{2,1,0:T(8,128)(2,1)S(1)} %get-tuple-element.46), channel_id=1, source_target_pairs={{0,21},{1,22},{2,23},{3,24},{4,25},{5,26},{6,27},{7,28},{8,29},{9,... | collective-permute-start | bytes 196616 | tf_op jit(solution)/shard_map/ppermute | solution.py:321

commit v6 on v5

--- a/solution.py
+++ b/solution.py
@@ -10,7 +10,6 @@
 F32 = jnp.float32
 BF16 = jnp.bfloat16
 ROWS = 120
-FINAL_ROWS = 128
 TILE = 128
 UNROLL = 8
 BANK_COPIES = 8
@@ -154,22 +153,7 @@
     )(keep, right, left, ahead, astern)
 
 
-def with_total(chunk, total):
-    row = lax.broadcasted_iota(jnp.int32, (FINAL_ROWS - ROWS, TILE), 0)
-    tail = jnp.zeros((FINAL_ROWS - ROWS, TILE), F32)
-    for i in range(3):
-        piece = total.astype(BF16).astype(F32)
-        tail = jnp.where(row == i, piece, tail)
-        total = total - piece
-    return jnp.concatenate([chunk, tail], axis=0).astype(BF16)
-
-
-def total_in(chunk):
-    rows = chunk.astype(F32)
-    return rows[ROWS:ROWS + 1] + rows[ROWS + 1:ROWS + 2] + rows[ROWS + 2:ROWS + 3]
-
-
-def gather_kernel(own_ref, near_ref, back_ref, total_ref, rest_ref, plus_ref, minus_ref):
+def gather_kernel(own_ref, near_ref, back_ref, rest_ref, plus_ref, minus_ref):
     for o in range(2):
         for far in range(3):
             value = (own_ref[o, far] + near_ref[far + 3 * o].astype(F32)
@@ -177,24 +161,24 @@
             if far == 1:
                 rest_ref[o] = value
                 continue
-            sent = with_total(value, total_ref[...])
+            sent = value.astype(BF16)
             if (far == 2) == (o == 0):
                 plus_ref[o] = sent
             else:
                 minus_ref[o] = sent
 
 
-def gather(own, near, back, total):
-    vmem = pl.BlockSpec(memory_space=pltpu.VMEM)
-    pair = jax.ShapeDtypeStruct((2, FINAL_ROWS, TILE), BF16)
+def gather(own, near, back):
+    vmem = pl.BlockSpec(memory_space=pltpu.VMEM)
+    pair = jax.ShapeDtypeStruct((2, ROWS, TILE), BF16)
     return pl.pallas_call(
         gather_kernel,
         out_shape=(jax.ShapeDtypeStruct((2, ROWS, TILE), F32), pair, pair),
-        in_specs=[vmem] * 4,
+        in_specs=[vmem] * 3,
         out_specs=(vmem,) * 3,
         compiler_params=pltpu.CompilerParams(vmem_limit_bytes=16 << 20),
         name="gather",
-    )(own, near, back, total)
+    )(own, near, back)
 
 
 def mix_kernel(tracer_ref, diff_ref, depth_ref, solved_ref, unit_ref, state_ref, ahead, lower, upper):
@@ -271,22 +255,18 @@
     )(tracers, diffusivity, column_depth.reshape(1, columns))
 
 
-def finish_kernel(scale, ring, me_ref, state_ref, unit_ref, rest_ref, plus_ref, minus_ref,
+def finish_kernel(scale, state_ref, unit_ref, rest_ref, plus_ref, minus_ref,
                   total_ref, out_hbm,
                   surface, result, sems):
     fields, levels, columns = state_ref.shape
     eye = (lax.broadcasted_iota(jnp.int32, (ROWS, TILE), 0)
            == lax.broadcasted_iota(jnp.int32, (ROWS, TILE), 1))
-    me = me_ref[0]
-    half = ring // 2
-    crossed = ((me - FAR_STEP) & (ring - 1)) // half != me // half
-    total = (total_ref[...] + jnp.where(crossed, total_in(plus_ref[0]),
-                                        total_in(minus_ref[0]))) * scale
+    total = total_ref[...] * scale
     spread = jnp.where(eye, jnp.broadcast_to(total, (ROWS, TILE)), 0.0)
     fix = jnp.sum(spread, axis=1, keepdims=True)
     for o in range(2):
-        surface[:, pl.ds(o * TILE, TILE)] = (rest_ref[o] + plus_ref[o].astype(F32)[:ROWS]
-                                             + minus_ref[o].astype(F32)[:ROWS]) + fix
+        surface[:, pl.ds(o * TILE, TILE)] = (rest_ref[o] + plus_ref[o].astype(F32)
+                                             + minus_ref[o].astype(F32)) + fix
     once = unit_ref[0]
     twice = unit_ref[1]
     copies = []
@@ -302,19 +282,19 @@
         copy.wait()
 
 
-def finish(me, state, unit, rest, plus, minus, total, scale, ring):
+def finish(state, unit, rest, plus, minus, total, scale):
     vmem = pl.BlockSpec(memory_space=pltpu.VMEM)
     fields, levels, columns = state.shape
     return pl.pallas_call(
-        functools.partial(finish_kernel, scale, ring),
+        functools.partial(finish_kernel, scale),
         out_shape=jax.ShapeDtypeStruct(state.shape, F32),
-        in_specs=[pl.BlockSpec(memory_space=pltpu.SMEM)] + [vmem] * 6,
+        in_specs=[vmem] * 6,
         out_specs=pl.BlockSpec(memory_space=pltpu.HBM),
         scratch_shapes=[pltpu.VMEM((ROWS, columns), F32), pltpu.VMEM(state.shape, F32),
                         pltpu.SemaphoreType.DMA((fields // FIELD_CHUNK,))],
         compiler_params=pltpu.CompilerParams(vmem_limit_bytes=24 << 20),
         name="finish",
-    )(me, state, unit, rest, plus, minus, total)
+    )(state, unit, rest, plus, minus, total)
 
 
 def shift(x, by, ring):
@@ -348,18 +328,22 @@
     own, near, back = combine(keep, right, left, ahead, astern)
     near = shift(near, MID_STEP, ring)
     back = shift(back, -MID_STEP, ring)
-    gathered, column_depth, own = lax.optimization_barrier((gathered, column_depth, own))
-    state, unit = mix(tracers, diffusivity, column_depth)
+    gathered, own = lax.optimization_barrier((gathered, own))
     group = ring // 2
     total = jnp.broadcast_to(jnp.sum(gathered, axis=0, keepdims=True), (group, TILE))
     total = lax.all_to_all(total, "blk", 0, 0, tiled=True,
                            axis_index_groups=[list(range(group)), list(range(group, ring))])
-    total, near = lax.optimization_barrier((total, near))
+    rest, plus, minus = gather(own, near, back)
+    column_depth, rest = lax.optimization_barrier((column_depth, rest))
+    state, unit = mix(tracers, diffusivity, column_depth)
+    total, unit = lax.optimization_barrier((total, unit))
     total = jnp.sum(total, axis=0, keepdims=True)
-    rest, plus, minus = gather(own, near, back, total)
     plus = shift(plus, FAR_STEP, ring)
     minus = shift(minus, -FAR_STEP, ring)
-    result = finish(me, state, unit, rest, plus, minus, total, 1.0 / (columns * ring * plane), ring)
+    total = lax.all_to_all(jnp.concatenate([total, total], axis=0), "blk", 0, 0, tiled=True,
+                           axis_index_groups=[[i, ring - 1 - i] for i in range(group)])
+    total = jnp.sum(total, axis=0, keepdims=True)
+    result = finish(state, unit, rest, plus, minus, total, 1.0 / (columns * ring * plane))
     return jnp.transpose(result, (1, 0, 2))
 
 

time: 127 us -> 125 us (0.984)
  the two profiles are of different devices: /device:TPU:161 before, /device:TPU:224 now
where the time goes in v6:
time: 125 us; the launch traced here: 124 us
  starting transfers between devices  64.8 us (52%)
  blocking collectives  48 us (38%)
  Pallas kernels  7.84 us (6%)
  local copies, waits for them, and re-layouts  2.36 us (2%)
    ppermute x8, starting transfers between devices, shift(): return lax.ppermute(x, 'blk', [(i, (i + by) % ring) for i in range(ring)])  42.4 us
    all_to_all x1, blocking collectives, body(): lax.all_to_all(jnp.concatenate([total, total], axis=0), 'blk', 0, 0, tile...  32.4 us
    all_to_all x1, starting transfers between devices, body(): lax.all_to_all(total, 'blk', 0, 0, tiled=True, axis_index_groups=[list(ra...  22.5 us
    all_to_all x1, blocking collectives, body(): lax.all_to_all(jnp.broadcast_to(part[:1], (plane, TILE)), ('sec', 'grp'),...  15.5 us
    pallas_call x1, Pallas kernels, remap(): pl.pallas_call(remap_kernel, out_shape=(jax.ShapeDtypeStruct((PLUS + MINU...  4.04 us
  transfers between devices with their start and end apart: 9, of which 1 were waited for; matrix products, arithmetic and copies ran while one was open for 1% of the time, Pallas kernels for 2%

profile of v6, /device:TPU:224, one launch (start us, length us, event | category | flops | bytes accessed | tf_op | source)
XLA Modules:
  0.0 124.2 jit_solution(9271743495633553626)
XLA Ops:
  0.7 1.2 copy.12.flux_ref
  1.8 4.0 %remap.1 = (bf16[17,120,128]{2,1,0:T(8,128)(2,1)S(1)}, bf16[17,120,128]{2,1,0:T(8,128)(2,1)S(1)}, bf16[6,120,128]{2,1,0:T(8,128)(2,1)S(1)}, bf16[6,120,128]{2,1,...) custom-call(s32[1]{0:T(128)S(6)} %copy.15.count_ref, s32[1]{0:T(128)} %bitcast.me_ref, ...), custom_call_target="tpu_custom_call" | custom-call | flops 536870912 | bytes 8388608 | tf_op jit(solution)/shard_map/remap/pallas_call | solution.py:98
  5.9 0.0 copy-start.2
  5.9 5.4 %collective-permute-start = (bf16[17,120,128]{2,1,0:T(8,128)(2,1)S(1)}, bf16[17,120,128]{2,1,0:T(8,128)(2,1)S(1)}, u32[]{:S(2)}, u32[]{:S(2)}) collective-permute-start(bf16[17,120,128]{2,1,0:T(8,128)(2,1)S(1)} %get-tuple-element.28), channel_id=1, source_target_pairs={{0,1},{1,2},{2,3},{3,4},{4,5},{5,6},{6,7},{7,8},{8,9},{9,10},{10,1... | collective-permute-start | bytes 1566728 | tf_op jit(solution)/shard_map/ppermute | solution.py:301
  11.3 1.9 %collective-permute-start.1 = (bf16[17,120,128]{2,1,0:T(8,128)(2,1)S(1)}, bf16[17,120,128]{2,1,0:T(8,128)(2,1)S(1)}, u32[]{:S(2)}, u32[]{:S(2)}) collective-permute-start(bf16[17,120,128]{2,1,0:T(8,128)(2,1)S(1)} %get-tuple-element.32), channel_id=1, source_target_pairs={{0,31},{1,0},{2,1},{3,2},{4,3},{5,4},{6,5},{7,6},{8,7},{9,8},{10,9... | collective-permute-start | bytes 1566728 | tf_op jit(solution)/shard_map/ppermute | solution.py:301
  13.2 5.0 %collective-permute-start.2 = (bf16[6,120,128]{2,1,0:T(8,128)(2,1)S(1)}, bf16[6,120,128]{2,1,0:T(8,128)(2,1)S(1)}, u32[]{:S(2)}, u32[]{:S(2)}) collective-permute-start(bf16[6,120,128]{2,1,0:T(8,128)(2,1)S(1)} %get-tuple-element.33), channel_id=1, source_target_pairs={{0,2},{1,3},{2,4},{3,5},{4,6},{5,7},{6,8},{7,9},{8,10},{9,11},{10,... | collective-permute-start | bytes 552968 | tf_op jit(solution)/shard_map/ppermute | solution.py:301
  18.3 1.9 %collective-permute-start.3 = (bf16[6,120,128]{2,1,0:T(8,128)(2,1)S(1)}, bf16[6,120,128]{2,1,0:T(8,128)(2,1)S(1)}, u32[]{:S(2)}, u32[]{:S(2)}) collective-permute-start(bf16[6,120,128]{2,1,0:T(8,128)(2,1)S(1)} %get-tuple-element.34), channel_id=1, source_target_pairs={{0,30},{1,31},{2,0},{3,1},{4,2},{5,3},{6,4},{7,5},{8,6},{9,7},{10,... | collective-permute-start | bytes 552968 | tf_op jit(solution)/shard_map/ppermute | solution.py:301
  20.2 15.5 %all_to_all.27 = f32[32,1,128]{2,1,0:T(1,128)S(1)} all-to-all(f32[32,1,128]{2,1,0:T(1,128)S(1)} %broadcast_in_dim.8), channel_id=1, replica_groups=mesh['sec'=2,'grp'=16,'blk'=32] {'sec','grp'}, dimensions={0} | all-to-all | bytes 32768 | tf_op jit(solution)/shard_map/all_to_all | solution.py:325
  35.8 0.0 collective-permute-done.right_ref
  35.8 0.0 collective-permute-done.2.ahead_ref
  35.8 0.2 collective-permute-done.3.astern_ref
  36.0 0.0 collective-permute-done.1.left_ref
  36.0 0.0 copy-start
  36.0 0.0 copy-start.1
  36.0 0.2 combine.1
  36.3 8.9 %collective-permute-start.4 = (bf16[6,120,128]{2,1,0:T(8,128)(2,1)S(1)}, bf16[6,120,128]{2,1,0:T(8,128)(2,1)S(1)}, u32[]{:S(2)}, u32[]{:S(2)}) collective-permute-start(bf16[6,120,128]{2,1,0:T(8,128)(2,1)S(1)} %get-tuple-element.37), channel_id=1, source_target_pairs={{0,4},{1,5},{2,6},{3,7},{4,8},{5,9},{6,10},{7,11},{8,12},{9,13},{1... | collective-permute-start | bytes 552968 | tf_op jit(solution)/shard_map/ppermute | solution.py:301
  45.2 1.9 %collective-permute-start.5 = (bf16[6,120,128]{2,1,0:T(8,128)(2,1)S(1)}, bf16[6,120,128]{2,1,0:T(8,128)(2,1)S(1)}, u32[]{:S(2)}, u32[]{:S(2)}) collective-permute-start(bf16[6,120,128]{2,1,0:T(8,128)(2,1)S(1)} %get-tuple-element.38), channel_id=1, source_target_pairs={{0,28},{1,29},{2,30},{3,31},{4,0},{5,1},{6,2},{7,3},{8,4},{9,5},{1... | collective-permute-start | bytes 552968 | tf_op jit(solution)/shard_map/ppermute | solution.py:301
  47.1 0.6 broadcast_in_dim.18
  47.7 22.5 %all-to-all-start.1 = ((f32[16,1,128]{2,1,0:T(1,128)}), f32[16,1,128]{2,1,0:T(1,128)S(1)}, u32[]{:S(2)}, u32[]{:S(2)}) async-start(f32[16,1,128]{2,1,0:T(1,128)} %broadcast_in_dim.18), calls=%async_computation.1 | async-start | bytes 16384 | tf_op jit(solution)/shard_map/all_to_all | solution.py:334
  70.2 0.0 copy-done.2
  70.2 0.6 copy.13.tracer_ref
  70.8 0.0 collective-permute-done.4.near_ref
  70.8 0.0 collective-permute-done.5.back_ref
  70.8 0.1 gather.1
  70.9 7.7 %collective-permute-start.6 = (bf16[2,120,128]{2,1,0:T(8,128)(2,1)S(1)}, bf16[2,120,128]{2,1,0:T(8,128)(2,1)S(1)}, u32[]{:S(2)}, u32[]{:S(2)}) collective-permute-start(bf16[2,120,128]{2,1,0:T(8,128)(2,1)S(1)} %get-tuple-element.46), channel_id=1, source_target_pairs={{0,11},{1,12},{2,13},{3,14},{4,15},{5,16},{6,17},{7,18},{8,19},{9,... | collective-permute-start | bytes 184328 | tf_op jit(solution)/shard_map/ppermute | solution.py:301
  78.6 9.5 %collective-permute-start.7 = (bf16[2,120,128]{2,1,0:T(8,128)(2,1)S(1)}, bf16[2,120,128]{2,1,0:T(8,128)(2,1)S(1)}, u32[]{:S(2)}, u32[]{:S(2)}) collective-permute-start(bf16[2,120,128]{2,1,0:T(8,128)(2,1)S(1)} %get-tuple-element.47), channel_id=1, source_target_pairs={{0,21},{1,22},{2,23},{3,24},{4,25},{5,26},{6,27},{7,28},{8,29},{9,... | collective-permute-start | bytes 184328 | tf_op jit(solution)/shard_map/ppermute | solution.py:301
  88.1 0.0 copy-done
  88.1 0.0 copy-done.1
  88.1 2.0 %mix.1 = (f32[60,32,256]{2,1,0:T(8,128)S(1)}, f32[2,32,256]{2,1,0:T(8,128)S(1)}) custom-call(bf16[32,60,256]{2,1,0:T(8,128)(2,1)S(1)} %copy.13.tracer_ref, f32[31,256]{1,0:T(8,128)S(1)} %copy-done, s32[1,256]{1,0:T(1,128)S(1)} %bitcast.13), custom_call_target="tpu_custom_call" | custom-call | flops 5898240 | bytes 2949120 | tf_op jit(solution)/shard_map/mix/pallas_call | solution.py:244
  90.2 0.0 all-to-all-done.1
  90.2 32.4 %all_to_all.28 = f32[2,1,128]{2,1,0:T(1,128)S(1)} all-to-all(f32[2,1,128]{2,1,0:T(1,128)S(1)} %bitcast.16), channel_id=1, replica_groups={{0,31},{1,30},{2,29},{3,28},{4,27},{5,26},{6,25},{7,24},{8,23},{9,22},{..., dimensions={0} | all-to-all | bytes 2048 | tf_op jit(solution)/shard_map/all_to_all | solution.py:343
  122.7 0.0 collective-permute-done.6.plus_ref
  122.7 0.0 collective-permute-done.7.minus_ref
  122.7 1.5 %finish.1 = f32[60,32,256]{2,1,0:T(8,128)} custom-call(f32[60,32,256]{2,1,0:T(8,128)S(1)} %get-tuple-element.41.state_ref, f32[2,32,256]{2,1,0:T(8,128)S(1)} %get-tuple-element.44.unit_ref, f32[2,120,128]{2,1,0:T(8,128)S(1)} %get-tuple-element.45.rest_ref, bf16[2,120,128]{2,1,0:T(8,128)(2,1)S(1)} %collective-permute-done.6.plus_ref, ...), custom_call_target="tpu_custom_call" | custom-call | tf_op jit(solution)/shard_map/finish/pallas_call | solution.py:288
  (6 shorter events, 0.1 us)
Async XLA Ops:
  5.9 64.3 %copy-start.2 = (bf16[32,60,256]{2,0,1:T(8,128)(2,1)S(1)}, bf16[32,60,256]{2,0,1:T(8,128)(2,1)}, u32[]{:S(2)}) copy-start(bf16[32,60,256]{2,0,1:T(8,128)(2,1)} %param.15) | copy-start | bytes 2949124
  5.9 29.9 %collective-permute-start = (bf16[17,120,128]{2,1,0:T(8,128)(2,1)S(1)}, bf16[17,120,128]{2,1,0:T(8,128)(2,1)S(1)}, u32[]{:S(2)}, u32[]{:S(2)}) collective-permute-start(bf16[17,120,128]{2,1,0:T(8,128)(2,1)S(1)} %get-tuple-element.28), channel_id=1, source_target_pairs={{0,1},{1,2},{2,3},{3,4},{4,5},{5,6},{6,7},{7,8},{8,9},{9,10},{10,1... | collective-permute-start | bytes 1566728 | tf_op jit(solution)/shard_map/ppermute | solution.py:301
  11.3 24.7 %collective-permute-start.1 = (bf16[17,120,128]{2,1,0:T(8,128)(2,1)S(1)}, bf16[17,120,128]{2,1,0:T(8,128)(2,1)S(1)}, u32[]{:S(2)}, u32[]{:S(2)}) collective-permute-start(bf16[17,120,128]{2,1,0:T(8,128)(2,1)S(1)} %get-tuple-element.32), channel_id=1, source_target_pairs={{0,31},{1,0},{2,1},{3,2},{4,3},{5,4},{6,5},{7,6},{8,7},{9,8},{10,9... | collective-permute-start | bytes 1566728 | tf_op jit(solution)/shard_map/ppermute | solution.py:301
  13.2 22.5 %collective-permute-start.2 = (bf16[6,120,128]{2,1,0:T(8,128)(2,1)S(1)}, bf16[6,120,128]{2,1,0:T(8,128)(2,1)S(1)}, u32[]{:S(2)}, u32[]{:S(2)}) collective-permute-start(bf16[6,120,128]{2,1,0:T(8,128)(2,1)S(1)} %get-tuple-element.33), channel_id=1, source_target_pairs={{0,2},{1,3},{2,4},{3,5},{4,6},{5,7},{6,8},{7,9},{8,10},{9,11},{10,... | collective-permute-start | bytes 552968 | tf_op jit(solution)/shard_map/ppermute | solution.py:301
  18.3 17.7 %collective-permute-start.3 = (bf16[6,120,128]{2,1,0:T(8,128)(2,1)S(1)}, bf16[6,120,128]{2,1,0:T(8,128)(2,1)S(1)}, u32[]{:S(2)}, u32[]{:S(2)}) collective-permute-start(bf16[6,120,128]{2,1,0:T(8,128)(2,1)S(1)} %get-tuple-element.34), channel_id=1, source_target_pairs={{0,30},{1,31},{2,0},{3,1},{4,2},{5,3},{6,4},{7,5},{8,6},{9,7},{10,... | collective-permute-start | bytes 552968 | tf_op jit(solution)/shard_map/ppermute | solution.py:301
  36.0 52.1 %copy-start = (f32[31,256]{1,0:T(8,128)S(1)}, f32[31,256]{1,0:T(8,128)}, u32[]{:S(2)}) copy-start(f32[31,256]{1,0:T(8,128)} %diff_ref.1) | copy-start | bytes 95236
  36.0 52.1 %copy-start.1 = (s32[256]{0:T(256)S(1)}, s32[256]{0:T(256)}, u32[]{:S(2)}) copy-start(s32[256]{0:T(256)} %param.17) | copy-start | bytes 3076
  36.3 34.5 %collective-permute-start.4 = (bf16[6,120,128]{2,1,0:T(8,128)(2,1)S(1)}, bf16[6,120,128]{2,1,0:T(8,128)(2,1)S(1)}, u32[]{:S(2)}, u32[]{:S(2)}) collective-permute-start(bf16[6,120,128]{2,1,0:T(8,128)(2,1)S(1)} %get-tuple-element.37), channel_id=1, source_target_pairs={{0,4},{1,5},{2,6},{3,7},{4,8},{5,9},{6,10},{7,11},{8,12},{9,13},{1... | collective-permute-start | bytes 552968 | tf_op jit(solution)/shard_map/ppermute | solution.py:301
  45.2 25.6 %collective-permute-start.5 = (bf16[6,120,128]{2,1,0:T(8,128)(2,1)S(1)}, bf16[6,120,128]{2,1,0:T(8,128)(2,1)S(1)}, u32[]{:S(2)}, u32[]{:S(2)}) collective-permute-start(bf16[6,120,128]{2,1,0:T(8,128)(2,1)S(1)} %get-tuple-element.38), channel_id=1, source_target_pairs={{0,28},{1,29},{2,30},{3,31},{4,0},{5,1},{6,2},{7,3},{8,4},{9,5},{1... | collective-permute-start | bytes 552968 | tf_op jit(solution)/shard_map/ppermute | solution.py:301
  47.7 42.5 %all-to-all-start.1 = ((f32[16,1,128]{2,1,0:T(1,128)}), f32[16,1,128]{2,1,0:T(1,128)S(1)}, u32[]{:S(2)}, u32[]{:S(2)}) async-start(f32[16,1,128]{2,1,0:T(1,128)} %broadcast_in_dim.18), calls=%async_computation.1 | async-start | bytes 16384 | tf_op jit(solution)/shard_map/all_to_all | solution.py:334
  70.9 51.8 %collective-permute-start.6 = (bf16[2,120,128]{2,1,0:T(8,128)(2,1)S(1)}, bf16[2,120,128]{2,1,0:T(8,128)(2,1)S(1)}, u32[]{:S(2)}, u32[]{:S(2)}) collective-permute-start(bf16[2,120,128]{2,1,0:T(8,128)(2,1)S(1)} %get-tuple-element.46), channel_id=1, source_target_pairs={{0,11},{1,12},{2,13},{3,14},{4,15},{5,16},{6,17},{7,18},{8,19},{9,... | collective-permute-start | bytes 184328 | tf_op jit(solution)/shard_map/ppermute | solution.py:301
  78.6 44.1 %collective-permute-start.7 = (bf16[2,120,128]{2,1,0:T(8,128)(2,1)S(1)}, bf16[2,120,128]{2,1,0:T(8,128)(2,1)S(1)}, u32[]{:S(2)}, u32[]{:S(2)}) collective-permute-start(bf16[2,120,128]{2,1,0:T(8,128)(2,1)S(1)} %get-tuple-element.47), channel_id=1, source_target_pairs={{0,21},{1,22},{2,23},{3,24},{4,25},{5,26},{6,27},{7,28},{8,29},{9,... | collective-permute-start | bytes 184328 | tf_op jit(solution)/shard_map/ppermute | solution.py:301

commit v7 on v6

--- a/solution.py
+++ b/solution.py
@@ -329,10 +329,12 @@
     near = shift(near, MID_STEP, ring)
     back = shift(back, -MID_STEP, ring)
     gathered, own = lax.optimization_barrier((gathered, own))
-    group = ring // 2
+    group = ring // 4
     total = jnp.broadcast_to(jnp.sum(gathered, axis=0, keepdims=True), (group, TILE))
     total = lax.all_to_all(total, "blk", 0, 0, tiled=True,
-                           axis_index_groups=[list(range(group)), list(range(group, ring))])
+                           axis_index_groups=[[g * group + i for i in range(group)]
+                                              for g in range(4)])
+    total, near = lax.optimization_barrier((total, near))
     rest, plus, minus = gather(own, near, back)
     column_depth, rest = lax.optimization_barrier((column_depth, rest))
     state, unit = mix(tracers, diffusivity, column_depth)
@@ -340,8 +342,9 @@
     total = jnp.sum(total, axis=0, keepdims=True)
     plus = shift(plus, FAR_STEP, ring)
     minus = shift(minus, -FAR_STEP, ring)
-    total = lax.all_to_all(jnp.concatenate([total, total], axis=0), "blk", 0, 0, tiled=True,
-                           axis_index_groups=[[i, ring - 1 - i] for i in range(group)])
+    total = lax.all_to_all(jnp.concatenate([total] * 4, axis=0), "blk", 0, 0, tiled=True,
+                           axis_index_groups=[[i, 2 * group - 1 - i, 2 * group + i, ring - 1 - i]
+                                              for i in range(group)])
     total = jnp.sum(total, axis=0, keepdims=True)
     result = finish(state, unit, rest, plus, minus, total, 1.0 / (columns * ring * plane))
     return jnp.transpose(result, (1, 0, 2))

time: 125 us -> 137 us (1.096)
  the two profiles are of different devices: /device:TPU:224 before, /device:TPU:1 now
where the time goes in v7:
time: 137 us; the launch traced here: 136 us
  blocking collectives  69.6 us (51%)
  starting transfers between devices  55.5 us (41%)
  Pallas kernels  8.08 us (6%)
  local copies, waits for them, and re-layouts  1.78 us (1%)
    ppermute x8, starting transfers between devices, shift(): return lax.ppermute(x, 'blk', [(i, (i + by) % ring) for i in range(ring)])  55.5 us
    all_to_all x1, blocking collectives, body(): lax.all_to_all(jnp.concatenate([total] * 4, axis=0), 'blk', 0, 0, tiled=T...  37.5 us
    all_to_all x1, blocking collectives, body(): lax.all_to_all(total, 'blk', 0, 0, tiled=True, axis_index_groups=[[g * gr...  16.3 us
    all_to_all x1, blocking collectives, body(): lax.all_to_all(jnp.broadcast_to(part[:1], (plane, TILE)), ('sec', 'grp'),...  15.8 us
    pallas_call x1, Pallas kernels, remap(): pl.pallas_call(remap_kernel, out_shape=(jax.ShapeDtypeStruct((PLUS + MINU...  4.28 us
  transfers between devices with their start and end apart: 8, of which 0 were waited for; matrix products, arithmetic and copies ran while one was open for 0% of the time, Pallas kernels for 1%

profile of v7, /device:TPU:1, one launch (start us, length us, event | category | flops | bytes accessed | tf_op | source)
XLA Modules:
  0.0 135.9 jit_solution(17453395487635956063)
XLA Ops:
  0.7 1.2 copy.14.flux_ref
  1.8 4.3 %remap.1 = (bf16[17,120,128]{2,1,0:T(8,128)(2,1)S(1)}, bf16[17,120,128]{2,1,0:T(8,128)(2,1)S(1)}, bf16[6,120,128]{2,1,0:T(8,128)(2,1)S(1)}, bf16[6,120,128]{2,1,...) custom-call(s32[1]{0:T(128)S(6)} %copy.17.count_ref, s32[1]{0:T(128)} %bitcast.me_ref, ...), custom_call_target="tpu_custom_call" | custom-call | flops 536870912 | bytes 8388608 | tf_op jit(solution)/shard_map/remap/pallas_call | solution.py:98
  6.1 0.0 copy-start.2
  6.1 5.0 %collective-permute-start = (bf16[17,120,128]{2,1,0:T(8,128)(2,1)S(1)}, bf16[17,120,128]{2,1,0:T(8,128)(2,1)S(1)}, u32[]{:S(2)}, u32[]{:S(2)}) collective-permute-start(bf16[17,120,128]{2,1,0:T(8,128)(2,1)S(1)} %get-tuple-element.30), channel_id=1, source_target_pairs={{0,1},{1,2},{2,3},{3,4},{4,5},{5,6},{6,7},{7,8},{8,9},{9,10},{10,1... | collective-permute-start | bytes 1566728 | tf_op jit(solution)/shard_map/ppermute | solution.py:301
  11.1 16.1 %collective-permute-start.1 = (bf16[17,120,128]{2,1,0:T(8,128)(2,1)S(1)}, bf16[17,120,128]{2,1,0:T(8,128)(2,1)S(1)}, u32[]{:S(2)}, u32[]{:S(2)}) collective-permute-start(bf16[17,120,128]{2,1,0:T(8,128)(2,1)S(1)} %get-tuple-element.34), channel_id=1, source_target_pairs={{0,31},{1,0},{2,1},{3,2},{4,3},{5,4},{6,5},{7,6},{8,7},{9,8},{10,9... | collective-permute-start | bytes 1566728 | tf_op jit(solution)/shard_map/ppermute | solution.py:301
  27.2 1.9 %collective-permute-start.2 = (bf16[6,120,128]{2,1,0:T(8,128)(2,1)S(1)}, bf16[6,120,128]{2,1,0:T(8,128)(2,1)S(1)}, u32[]{:S(2)}, u32[]{:S(2)}) collective-permute-start(bf16[6,120,128]{2,1,0:T(8,128)(2,1)S(1)} %get-tuple-element.35), channel_id=1, source_target_pairs={{0,2},{1,3},{2,4},{3,5},{4,6},{5,7},{6,8},{7,9},{8,10},{9,11},{10,... | collective-permute-start | bytes 552968 | tf_op jit(solution)/shard_map/ppermute | solution.py:301
  29.1 5.5 %collective-permute-start.3 = (bf16[6,120,128]{2,1,0:T(8,128)(2,1)S(1)}, bf16[6,120,128]{2,1,0:T(8,128)(2,1)S(1)}, u32[]{:S(2)}, u32[]{:S(2)}) collective-permute-start(bf16[6,120,128]{2,1,0:T(8,128)(2,1)S(1)} %get-tuple-element.36), channel_id=1, source_target_pairs={{0,30},{1,31},{2,0},{3,1},{4,2},{5,3},{6,4},{7,5},{8,6},{9,7},{10,... | collective-permute-start | bytes 552968 | tf_op jit(solution)/shard_map/ppermute | solution.py:301
  34.6 15.8 %all_to_all.24 = f32[32,1,128]{2,1,0:T(1,128)S(1)} all-to-all(f32[32,1,128]{2,1,0:T(1,128)S(1)} %broadcast_in_dim.6), channel_id=1, replica_groups=mesh['sec'=2,'grp'=16,'blk'=32] {'sec','grp'}, dimensions={0} | all-to-all | bytes 32768 | tf_op jit(solution)/shard_map/all_to_all | solution.py:325
  50.4 0.0 collective-permute-done.right_ref
  50.4 0.0 collective-permute-done.2.ahead_ref
  50.4 0.0 collective-permute-done.3.astern_ref
  50.4 0.0 collective-permute-done.1.left_ref
  50.5 0.0 copy-start
  50.5 0.0 copy-start.1
  50.5 0.3 combine.1
  50.7 1.9 %collective-permute-start.4 = (bf16[6,120,128]{2,1,0:T(8,128)(2,1)S(1)}, bf16[6,120,128]{2,1,0:T(8,128)(2,1)S(1)}, u32[]{:S(2)}, u32[]{:S(2)}) collective-permute-start(bf16[6,120,128]{2,1,0:T(8,128)(2,1)S(1)} %get-tuple-element.40), channel_id=1, source_target_pairs={{0,4},{1,5},{2,6},{3,7},{4,8},{5,9},{6,10},{7,11},{8,12},{9,13},{1... | collective-permute-start | bytes 552968 | tf_op jit(solution)/shard_map/ppermute | solution.py:301
  52.7 7.3 %collective-permute-start.5 = (bf16[6,120,128]{2,1,0:T(8,128)(2,1)S(1)}, bf16[6,120,128]{2,1,0:T(8,128)(2,1)S(1)}, u32[]{:S(2)}, u32[]{:S(2)}) collective-permute-start(bf16[6,120,128]{2,1,0:T(8,128)(2,1)S(1)} %get-tuple-element.42), channel_id=1, source_target_pairs={{0,28},{1,29},{2,30},{3,31},{4,0},{5,1},{6,2},{7,3},{8,4},{9,5},{1... | collective-permute-start | bytes 552968 | tf_op jit(solution)/shard_map/ppermute | solution.py:301
  60.0 16.3 %all_to_all.25 = f32[8,1,128]{2,1,0:T(1,128)S(1)} all-to-all(f32[8,1,128]{2,1,0:T(1,128)S(1)} %broadcast_in_dim.7), channel_id=1, replica_groups={{0,1,2,3,4,5,6,7},{8,9,10,11,12,13,14,15},{16,17,18,19,20,21,22,23},{24..., dimensions={0} | all-to-all | bytes 8192 | tf_op jit(solution)/shard_map/all_to_all | solution.py:334
  76.2 0.0 collective-permute-done.4.near_ref
  76.2 0.0 collective-permute-done.5.back_ref
  76.2 0.1 gather.1
  76.3 10.9 %collective-permute-start.6 = (bf16[2,120,128]{2,1,0:T(8,128)(2,1)S(1)}, bf16[2,120,128]{2,1,0:T(8,128)(2,1)S(1)}, u32[]{:S(2)}, u32[]{:S(2)}) collective-permute-start(bf16[2,120,128]{2,1,0:T(8,128)(2,1)S(1)} %get-tuple-element.50), channel_id=1, source_target_pairs={{0,11},{1,12},{2,13},{3,14},{4,15},{5,16},{6,17},{7,18},{8,19},{9,... | collective-permute-start | bytes 184328 | tf_op jit(solution)/shard_map/ppermute | solution.py:301
  87.3 7.0 %collective-permute-start.7 = (bf16[2,120,128]{2,1,0:T(8,128)(2,1)S(1)}, bf16[2,120,128]{2,1,0:T(8,128)(2,1)S(1)}, u32[]{:S(2)}, u32[]{:S(2)}) collective-permute-start(bf16[2,120,128]{2,1,0:T(8,128)(2,1)S(1)} %get-tuple-element.51), channel_id=1, source_target_pairs={{0,21},{1,22},{2,23},{3,24},{4,25},{5,26},{6,27},{7,28},{8,29},{9,... | collective-permute-start | bytes 184328 | tf_op jit(solution)/shard_map/ppermute | solution.py:301
  94.2 0.0 copy-done.2
  94.2 0.6 copy.15.tracer_ref
  94.8 0.0 copy-done
  94.8 0.0 copy-done.1
  94.8 2.0 %mix.1 = (f32[60,32,256]{2,1,0:T(8,128)S(1)}, f32[2,32,256]{2,1,0:T(8,128)S(1)}) custom-call(bf16[32,60,256]{2,1,0:T(8,128)(2,1)S(1)} %copy.15.tracer_ref, f32[31,256]{1,0:T(8,128)S(1)} %copy-done, s32[1,256]{1,0:T(1,128)S(1)} %bitcast.10), custom_call_target="tpu_custom_call" | custom-call | flops 5898240 | bytes 2949120 | tf_op jit(solution)/shard_map/mix/pallas_call | solution.py:244
  96.9 37.5 %all_to_all.26 = f32[4,1,128]{2,1,0:T(1,128)S(1)} all-to-all(f32[4,1,128]{2,1,0:T(1,128)S(1)} %concatenate.3), channel_id=1, replica_groups={{0,15,16,31},{1,14,17,30},{2,13,18,29},{3,12,19,28},{4,11,20,27},{5,10,..., dimensions={0} | all-to-all | bytes 4096 | tf_op jit(solution)/shard_map/all_to_all | solution.py:345
  134.4 0.0 collective-permute-done.6.plus_ref
  134.4 0.0 collective-permute-done.7.minus_ref
  134.4 1.5 %finish.1 = f32[60,32,256]{2,1,0:T(8,128)} custom-call(f32[60,32,256]{2,1,0:T(8,128)S(1)} %get-tuple-element.45.state_ref, f32[2,32,256]{2,1,0:T(8,128)S(1)} %get-tuple-element.48.unit_ref, f32[2,120,128]{2,1,0:T(8,128)S(1)} %get-tuple-element.49.rest_ref, bf16[2,120,128]{2,1,0:T(8,128)(2,1)S(1)} %collective-permute-done.6.plus_ref, ...), custom_call_target="tpu_custom_call" | custom-call | tf_op jit(solution)/shard_map/finish/pallas_call | solution.py:288
  (7 shorter events, 0.1 us)
Async XLA Ops:
  6.1 88.1 %copy-start.2 = (bf16[32,60,256]{2,0,1:T(8,128)(2,1)S(1)}, bf16[32,60,256]{2,0,1:T(8,128)(2,1)}, u32[]{:S(2)}) copy-start(bf16[32,60,256]{2,0,1:T(8,128)(2,1)} %param.15) | copy-start | bytes 2949124
  6.1 44.3 %collective-permute-start = (bf16[17,120,128]{2,1,0:T(8,128)(2,1)S(1)}, bf16[17,120,128]{2,1,0:T(8,128)(2,1)S(1)}, u32[]{:S(2)}, u32[]{:S(2)}) collective-permute-start(bf16[17,120,128]{2,1,0:T(8,128)(2,1)S(1)} %get-tuple-element.30), channel_id=1, source_target_pairs={{0,1},{1,2},{2,3},{3,4},{4,5},{5,6},{6,7},{7,8},{8,9},{9,10},{10,1... | collective-permute-start | bytes 1566728 | tf_op jit(solution)/shard_map/ppermute | solution.py:301
  11.1 39.3 %collective-permute-start.1 = (bf16[17,120,128]{2,1,0:T(8,128)(2,1)S(1)}, bf16[17,120,128]{2,1,0:T(8,128)(2,1)S(1)}, u32[]{:S(2)}, u32[]{:S(2)}) collective-permute-start(bf16[17,120,128]{2,1,0:T(8,128)(2,1)S(1)} %get-tuple-element.34), channel_id=1, source_target_pairs={{0,31},{1,0},{2,1},{3,2},{4,3},{5,4},{6,5},{7,6},{8,7},{9,8},{10,9... | collective-permute-start | bytes 1566728 | tf_op jit(solution)/shard_map/ppermute | solution.py:301
  27.2 23.2 %collective-permute-start.2 = (bf16[6,120,128]{2,1,0:T(8,128)(2,1)S(1)}, bf16[6,120,128]{2,1,0:T(8,128)(2,1)S(1)}, u32[]{:S(2)}, u32[]{:S(2)}) collective-permute-start(bf16[6,120,128]{2,1,0:T(8,128)(2,1)S(1)} %get-tuple-element.35), channel_id=1, source_target_pairs={{0,2},{1,3},{2,4},{3,5},{4,6},{5,7},{6,8},{7,9},{8,10},{9,11},{10,... | collective-permute-start | bytes 552968 | tf_op jit(solution)/shard_map/ppermute | solution.py:301
  29.1 21.3 %collective-permute-start.3 = (bf16[6,120,128]{2,1,0:T(8,128)(2,1)S(1)}, bf16[6,120,128]{2,1,0:T(8,128)(2,1)S(1)}, u32[]{:S(2)}, u32[]{:S(2)}) collective-permute-start(bf16[6,120,128]{2,1,0:T(8,128)(2,1)S(1)} %get-tuple-element.36), channel_id=1, source_target_pairs={{0,30},{1,31},{2,0},{3,1},{4,2},{5,3},{6,4},{7,5},{8,6},{9,7},{10,... | collective-permute-start | bytes 552968 | tf_op jit(solution)/shard_map/ppermute | solution.py:301
  50.5 44.4 %copy-start = (f32[31,256]{1,0:T(8,128)S(1)}, f32[31,256]{1,0:T(8,128)}, u32[]{:S(2)}) copy-start(f32[31,256]{1,0:T(8,128)} %diff_ref.1) | copy-start | bytes 95236
  50.5 44.3 %copy-start.1 = (s32[256]{0:T(256)S(1)}, s32[256]{0:T(256)}, u32[]{:S(2)}) copy-start(s32[256]{0:T(256)} %param.17) | copy-start | bytes 3076
  50.7 25.5 %collective-permute-start.4 = (bf16[6,120,128]{2,1,0:T(8,128)(2,1)S(1)}, bf16[6,120,128]{2,1,0:T(8,128)(2,1)S(1)}, u32[]{:S(2)}, u32[]{:S(2)}) collective-permute-start(bf16[6,120,128]{2,1,0:T(8,128)(2,1)S(1)} %get-tuple-element.40), channel_id=1, source_target_pairs={{0,4},{1,5},{2,6},{3,7},{4,8},{5,9},{6,10},{7,11},{8,12},{9,13},{1... | collective-permute-start | bytes 552968 | tf_op jit(solution)/shard_map/ppermute | solution.py:301
  52.7 23.6 %collective-permute-start.5 = (bf16[6,120,128]{2,1,0:T(8,128)(2,1)S(1)}, bf16[6,120,128]{2,1,0:T(8,128)(2,1)S(1)}, u32[]{:S(2)}, u32[]{:S(2)}) collective-permute-start(bf16[6,120,128]{2,1,0:T(8,128)(2,1)S(1)} %get-tuple-element.42), channel_id=1, source_target_pairs={{0,28},{1,29},{2,30},{3,31},{4,0},{5,1},{6,2},{7,3},{8,4},{9,5},{1... | collective-permute-start | bytes 552968 | tf_op jit(solution)/shard_map/ppermute | solution.py:301
  76.3 58.1 %collective-permute-start.6 = (bf16[2,120,128]{2,1,0:T(8,128)(2,1)S(1)}, bf16[2,120,128]{2,1,0:T(8,128)(2,1)S(1)}, u32[]{:S(2)}, u32[]{:S(2)}) collective-permute-start(bf16[2,120,128]{2,1,0:T(8,128)(2,1)S(1)} %get-tuple-element.50), channel_id=1, source_target_pairs={{0,11},{1,12},{2,13},{3,14},{4,15},{5,16},{6,17},{7,18},{8,19},{9,... | collective-permute-start | bytes 184328 | tf_op jit(solution)/shard_map/ppermute | solution.py:301
  87.3 47.1 %collective-permute-start.7 = (bf16[2,120,128]{2,1,0:T(8,128)(2,1)S(1)}, bf16[2,120,128]{2,1,0:T(8,128)(2,1)S(1)}, u32[]{:S(2)}, u32[]{:S(2)}) collective-permute-start(bf16[2,120,128]{2,1,0:T(8,128)(2,1)S(1)} %get-tuple-element.51), channel_id=1, source_target_pairs={{0,21},{1,22},{2,23},{3,24},{4,25},{5,26},{6,27},{7,28},{8,29},{9,... | collective-permute-start | bytes 184328 | tf_op jit(solution)/shard_map/ppermute | solution.py:301
